TPU v7x, 32 devices: a whole 2x2x4 slice. The times are simulated.
32 devices in a mesh: group: 4 (over x, core), seq: 8 (over z, y).
Axes of the slice: x: 2, y: 2, z: 4, core: 2. Of those that a mesh axis runs over, the one named last changes fastest.
Arguments:
- tokens: bfloat16 [4, 1024, 2048], P('group', 'seq'), may hold values from -6 to 6
- norm_gain: bfloat16 [2048], replicated, may hold values from 0.25 to 1.75
- w_qkv: bfloat16 [2048, 1920], P(('group', 'seq')), may hold values from -1.767767 to 1.767767
- prefix_kv: bfloat16 [4, 512, 640], P('group', 'seq'), may hold values from -12 to 12
- segments: int32 [4, 1024], P('group', 'seq'), may hold values from 0 to 3, never falling along the last dimension, each value on 1 to 512 neighbouring positions
Outputs:
- context: bfloat16 [4, 1024, 1280], P('group', 'seq')
Inputs may be any that keep to these rules, and one draw needn't show every extreme that they name: `segments`: within each group's 1024 suffix tokens the request numbers never fall; every request holds 1 to 512 tokens and one holds exactly 512.
All inputs are finite; a program needn't handle non-finite values.
Results may differ from a plain program's by a relative error of at most 0.0096.
Values may be sent and summed in bfloat16 or wider, within the bound.
No kernel may reach another device: no remote copies, remote signals or barrier semaphores. Data moves between devices by JAX's collectives and lax.ppermute only.
A program may use at most 64 MiB of HBM per device.

v0:
```python
import math

import jax
import jax.numpy as jnp
from jax import lax
from jax.sharding import PartitionSpec as P

HD = 64
QW = 1280
KVW = 320


def body(tokens, norm_gain, w_qkv, prefix_kv, segments):
    inputs = tokens[0]
    seg_ids = segments[0]
    row_count = inputs.shape[0]
    key_heads = KVW // HD
    repeats = QW // KVW
    values_f = inputs.astype(jnp.float32)
    mean_square = jnp.mean(values_f * values_f, axis=-1, keepdims=True)
    normed = (values_f * lax.rsqrt(mean_square + 1e-05) * norm_gain.astype(jnp.float32)).astype(
        jnp.bfloat16
    )
    folded = jnp.dot(
        normed,
        lax.all_gather(w_qkv, ("group", "seq"), axis=0, tiled=True),
        preferred_element_type=jnp.float32,
    )
    projected = folded.astype(jnp.bfloat16)
    queries = projected[:, :QW].reshape(row_count, key_heads, repeats, HD)
    local_kv = projected[:, QW:]

    def absorb(softmax_state, keyvals, visible):
        running_max, denominator, numerator = softmax_state
        key_count = keyvals.shape[0]
        key_part = keyvals[:, :KVW].reshape(key_count, key_heads, HD)
        value_part = keyvals[:, KVW:].reshape(key_count, key_heads, HD)
        scores = (
            jnp.einsum("tgrd,ngd->tgrn", queries, key_part, preferred_element_type=jnp.float32)
            * 0.125
        )
        if visible is not None:
            scores = jnp.where(visible[:, None, None, :], scores, jnp.float32(-1e30))
        new_max = jnp.maximum(running_max, jnp.max(scores, axis=-1))
        probability = jnp.exp(scores - new_max[..., None])
        if visible is not None:
            probability = jnp.where(visible[:, None, None, :], probability, jnp.float32(0.0))
        factor = jnp.exp(running_max - new_max)
        denominator = denominator * factor + jnp.sum(probability, axis=-1)
        numerator = numerator * factor[..., None] + jnp.einsum(
            "tgrn,ngd->tgrd",
            probability.astype(jnp.bfloat16),
            value_part,
            preferred_element_type=jnp.float32,
        )
        return (new_max, denominator, numerator)

    def sweep_keys(softmax_state, keyvals, key_seg, first_row, build):
        key_count = keyvals.shape[0]
        block_len = math.gcd(key_count, 512)
        if block_len == key_count:
            return absorb(softmax_state, keyvals, build(key_seg, first_row))

        def block_step(block_index, running):
            key_start = block_index * block_len
            keys_block = lax.dynamic_slice_in_dim(keyvals, key_start, block_len, 0)
            if key_seg is None:
                seg_block = None
            else:
                seg_block = lax.dynamic_slice_in_dim(key_seg, key_start, block_len, 0)
            return absorb(running, keys_block, build(seg_block, key_start))

        return lax.fori_loop(0, key_count // block_len, block_step, softmax_state)

    start_state = (
        jnp.full((row_count, key_heads, repeats), -1e30, jnp.float32),
        jnp.zeros((row_count, key_heads, repeats), jnp.float32),
        jnp.zeros((row_count, key_heads, repeats, HD), jnp.float32),
    )

    def open_rows(seg_block, key_start):
        return None

    softmax_state = sweep_keys(
        start_state,
        lax.all_gather(prefix_kv[0], "seq", axis=0, tiled=True),
        None,
        jnp.int32(0),
        open_rows,
    )
    query_pos = lax.axis_index("seq") * row_count + jnp.arange(row_count, dtype=jnp.int32)

    def causal_rows(seg_block, key_start):
        key_pos = key_start + jnp.arange(seg_block.shape[0], dtype=jnp.int32)
        return (seg_block[None, :] == seg_ids[:, None]) & (key_pos[None, :] <= query_pos[:, None])

    keyvals = lax.all_gather(local_kv, "seq", axis=0, tiled=True)
    key_seg = lax.all_gather(seg_ids, "seq", axis=0, tiled=True)
    softmax_state = sweep_keys(softmax_state, keyvals, key_seg, jnp.int32(0), causal_rows)
    running_max, denominator, numerator = softmax_state
    context = (numerator / denominator[..., None]).reshape(row_count, QW).astype(jnp.bfloat16)
    return context[None]


def solution(mesh):
    return jax.shard_map(
        body,
        mesh=mesh,
        in_specs=(
            P("group", "seq", None),
            P(),
            P(("group", "seq"), None),
            P("group", "seq", None),
            P("group", "seq"),
        ),
        out_specs=P("group", "seq", None),
        check_vma=False,
    )
```

profile of v0, /device:TPU:0, one launch (start us, length us, event | category | flops | bytes accessed | tf_op | source)
XLA Modules:
  0.0 169.5 jit_solution(7326391197680316243)
XLA Ops:
  6.5 0.7 all-gather.5.cloned.1.call-update
  7.3 0.7 convert_element_type.40
  8.0 1.2 fusion.30
  9.2 79.2 %all-gather.5.cloned.1.call-done = bf16[2048,1920]{1,0:T(8,128)(2,1)} async-done(((bf16[64,1920]{1,0:T(8,128)(2,1)}), bf16[2048,1920]{1,0:T(8,128)(2,1)}) %all-gather.5.cloned.1.call-update) | async-done | bytes 7864336 | tf_op jit(solution)/shard_map/all_gather | solution.py:26
  88.4 4.7 %convolution_convert_fusion = bf16[128,1920]{1,0:T(8,128)(2,1)S(1)} fusion(bf16[2048,1920]{1,0:T(8,128)(2,1)} %all-gather.5.cloned.1.call-done, bf16[1,128,2048]{2,1,0:T(8,128)(2,1)} %param.7, f32[2048]{0:T(1024)S(1)} %convert_element_type.40, f32[128]{0:T(128)S(1)} %add_rsqrt_fusion), kind=kOutput, calls=%fused_computation.27 | convolution fusion | flops 1007927296 | bytes 8888832 | tf_op jit(solution)/shard_map/dot_general | solution.py:24
  93.2 0.7 slice.35
  93.9 32.5 %all-gather = bf16[1,512,640]{2,1,0:T(8,128)(2,1)S(1)} all-gather(bf16[1,64,640]{2,1,0:T(8,128)(2,1)S(1)} %copy-done), channel_id=2, replica_groups=mesh['group'=4,'seq'=8] {'seq'}, dimensions={1}, use_global_device_ids=true | all-gather | bytes 737280 | tf_op jit(solution)/shard_map/all_gather | solution.py:86
  127.0 19.3 %all-gather.1 = s32[1,1024]{1,0:T(1,128)S(1)} all-gather(s32[1,128]{1,0:T(1,128)S(1)} %copy-done.1), channel_id=3, replica_groups=mesh['group'=4,'seq'=8] {'seq'}, dimensions={1}, use_global_device_ids=true | all-gather | bytes 4608 | tf_op jit(solution)/shard_map/all_gather | solution.py:98
  146.3 0.2 copy.14
  146.5 1.0 bitcast_reduce_fusion
  147.5 1.3 fusion.19
  148.9 1.4 fusion.27
  150.3 11.3 %while.18 = (s32[]{:T(128)}, f32[128,5,4]{0,2,1:T(4,128)S(1)}, f32[128,5,4]{0,2,1:T(4,128)S(1)}, f32[128,5,4,64]{0,3,2,1:T(8,128)S(1)}, s32[1024]{0:T(1024)S(1)}...) while((s32[]{:T(128)}, f32[128,5,4]{0,2,1:T(4,128)S(1)}, ...), condition=%wide.region_6.7_spmd.clone, body=%wide.region_3.6_spmd.clone.sunk | while | flops 353113728 | bytes 21081812 | solution.py:73
  150.4 0.2 compare_and_fusion.2
  150.6 1.4 fusion.60
  152.4 0.9 fusion.61
  153.3 1.2 fusion.62
  154.6 1.4 fusion.63
  156.1 0.2 compare_and_fusion.2
  156.3 1.4 fusion.60
  158.0 0.9 fusion.61
  159.0 1.2 fusion.62
  160.2 1.4 fusion.63
  161.7 0.9 copy.18
  (32 shorter events, 1.7 us)
Async XLA Ops:
  6.5 81.9 %all-gather.5.cloned.1.call-start = ((), (), s32[]{:S(2)}) async-start(), calls=%async_computation | async-start | bytes 8110080 | tf_op jit(solution)/shard_map/all_gather | solution.py:26
  7.3 143.1 %all-gather.7.cloned.1.call-start = ((), (), s32[]{:S(2)}) async-start(), calls=%async_computation.1 | async-start | bytes 1474560 | tf_op jit(solution)/shard_map/all_gather | solution.py:97
  9.2 84.6 %copy-start = (bf16[1,64,640]{2,1,0:T(8,128)(2,1)S(1)}, bf16[1,64,640]{2,1,0:T(8,128)(2,1)}, u32[]{:S(2)}) copy-start(bf16[1,64,640]{2,1,0:T(8,128)(2,1)} %param.10) | copy-start | bytes 245764
  9.2 117.7 %copy-start.1 = (s32[1,128]{1,0:T(1,128)S(1)}, s32[1,128]{1,0:T(1,128)}, u32[]{:S(2)}) copy-start(s32[1,128]{1,0:T(1,128)} %param.11) | copy-start | bytes 1540
Sparse Core Ops, SparseCore 0:
  10.3 78.1 all-gather.4
  94.0 42.5 all-gather.6
where the time goes:
time: 170 us; the launch traced here: 169 us
  waiting for transfers between devices  79.9 us (47%)
  blocking collectives  51.8 us (30%)
  between operations  13.5 us (8%)
  matrix products  11.8 us (7%)
  other arithmetic  6.27 us (4%)
  local copies, waits for them, and re-layouts  5.95 us (4%)
    all_gather x1, waiting for transfers between devices, body(): lax.all_gather(w_qkv, ('group', 'seq'), axis=0, tiled=True)  79.2 us
    all_gather x1, blocking collectives, body(): lax.all_gather(prefix_kv[0], 'seq', axis=0, tiled=True)  32.5 us
    all_gather x1, blocking collectives, body(): key_seg = lax.all_gather(seg_ids, 'seq', axis=0, tiled=True)  19.3 us
    dot_general x1, matrix products, body(): jnp.dot(normed, lax.all_gather(w_qkv, ('group', 'seq'), axis=0, tiled=Tru...  4.72 us
    dot_general x3, matrix products, absorb(): jnp.einsum('tgrn,ngd->tgrd', probability.astype(jnp.bfloat16), value_part...  4.22 us
    reduce_sum x3, other arithmetic, absorb(): denominator = denominator * factor + jnp.sum(probability, axis=-1)  3.76 us
  transfers between devices with their start and end apart: 2, of which 1 were waited for; matrix products, arithmetic and copies ran while one was open for 4% of the time, Pallas kernels for 0%

commit v1 on v0

v1 whole, which is shorter than its diff:
```python
import functools

import jax
import jax.numpy as jnp
from jax import lax
from jax.experimental import pallas as pl
from jax.experimental.pallas import tpu as pltpu
from jax.sharding import Mesh, PartitionSpec as P

HD = 64
QW = 1280
KVW = 320
KEY_HEADS = KVW // HD
REPEATS = QW // KVW
QH = QW // 2
NEG = -1e30
SMALL = 4
F32 = jnp.float32
BF16 = jnp.bfloat16


def rms_norm(inputs, norm_gain):
    values = inputs.astype(F32)
    mean_square = jnp.mean(values * values, axis=-1, keepdims=True)
    return (values * lax.rsqrt(mean_square + 1e-05) * norm_gain.astype(F32)).astype(BF16)


def swap(x, axis):
    return lax.ppermute(x, axis, [(0, 1), (1, 0)])


def z_swap(x, distance):
    return lax.ppermute(x, "z", [(i, i ^ distance) for i in range(4)])


def plane(piece, ident):
    from_x, from_y = swap(piece, "gx"), swap(piece, "y")
    half = piece.shape[0] // 2
    low = swap(from_x[:half], "y")
    high = swap(from_y[half:], "gx")
    return from_x, from_y, low, high


def project_kernel(scale, n_pieces, places, pos, own, other, *refs):
    pieces, (mine, theirs), (weights, sems) = refs[:n_pieces], refs[n_pieces:n_pieces + 2], refs[n_pieces + 2:]
    copies = []
    for i, (piece, row, spot) in enumerate(places):
        start = pl.multiple_of(pos[spot], 64)
        copies.append(
            pltpu.make_async_copy(pieces[piece].at[pl.ds(row, 64), :], weights.at[pl.ds(start, 64), :], sems.at[i])
        )
    for copy in copies:
        copy.start()
    for copy in copies:
        copy.wait()
    for source, target in ((own, mine), (other, theirs)):
        result = jnp.dot(source[...], weights[...], preferred_element_type=F32).astype(BF16)
        target[...] = result if scale is None else result * jnp.asarray(scale, BF16)


def project(own, other, pieces, places, pos, scale):
    rows, depth = own.shape
    width = pieces[0].shape[1]
    vmem = pl.BlockSpec(memory_space=pltpu.VMEM)
    return pl.pallas_call(
        functools.partial(project_kernel, scale, len(pieces), places),
        out_shape=[jax.ShapeDtypeStruct((rows, width), BF16)] * 2,
        in_specs=[pl.BlockSpec(memory_space=pltpu.SMEM), vmem, vmem]
        + [pl.BlockSpec(memory_space=pl.ANY)] * len(pieces),
        out_specs=[vmem, vmem],
        scratch_shapes=[pltpu.VMEM((depth, width), BF16), pltpu.SemaphoreType.DMA((len(places),))],
        compiler_params=pltpu.CompilerParams(vmem_limit_bytes=24 << 20),
        cost_estimate=pl.CostEstimate(
            flops=4 * rows * depth * width, bytes_accessed=2 * depth * width + 8 * rows * depth, transcendentals=0
        ),
    )(pos, own, other, *pieces)


def gather_columns(first, second):
    n = first.shape[0]
    own = jnp.concatenate([first, second])
    far = jnp.concatenate([z_swap(own, d) for d in (1, 2, 3)])
    arrays, places = [], []

    def add(array, blocks):
        for i, (dz, half, dx, dy) in enumerate(blocks):
            places.append((len(arrays), n * i, ((dz * 2 + dx) * 2 + dy) * 2 + half))
        arrays.append(array)

    for piece, zs in ((own, (0,)), (far, (1, 2, 3))):
        blocks = [(dz, half) for dz in zs for half in (0, 1)]
        mid = len(blocks) // 2
        from_x, from_y, low, high = plane(piece, None)
        add(piece, [b + (0, 0) for b in blocks])
        add(from_x, [b + (1, 0) for b in blocks])
        add(from_y, [b + (0, 1) for b in blocks])
        add(low, [b + (1, 1) for b in blocks[:mid]])
        add(high, [b + (1, 1) for b in blocks[mid:]])
    return arrays, places


def attend_kernel(earlier, scalars, q_mine, q_theirs, prefix, seg_col, *refs):
    blocks, out, q_all = refs[:earlier + 1], refs[earlier + 1], refs[earlier + 2]
    core, index = scalars[0], scalars[1]
    rows = q_mine.shape[0]
    low = core == 0
    q_all[:, :QH] = jnp.where(low, q_mine[...], q_theirs[...])
    q_all[:, QH:] = jnp.where(low, q_theirs[...], q_mine[...])
    biases = []
    q_seg = seg_col[...]
    for distance in range(earlier, -1, -1):
        k_seg = blocks[distance][rows:rows + 1, :rows].astype(F32)
        seen = q_seg == k_seg
        if distance == 0:
            q_at = lax.broadcasted_iota(jnp.int32, (rows, rows), 0)
            k_at = lax.broadcasted_iota(jnp.int32, (rows, rows), 1)
            seen = seen & (k_at <= q_at)
            biases.append(jnp.where(seen, 0.0, NEG))
        else:
            biases.append(jnp.where(seen, jnp.where(index >= distance, 0.0, NEG), NEG))
    bias = jnp.concatenate(biases, axis=1)
    bias = jnp.concatenate([bias] * REPEATS, axis=0)
    for head in range(KEY_HEADS):
        cols, vcols = slice(head * HD, (head + 1) * HD), slice(KVW + head * HD, KVW + (head + 1) * HD)
        base = head * REPEATS * HD
        queries = jnp.concatenate([q_all[:, base + r * HD:base + (r + 1) * HD] for r in range(REPEATS)], axis=0)
        keys = jnp.concatenate([blocks[d][:rows, cols] for d in range(earlier, -1, -1)], axis=0)
        values = jnp.concatenate([blocks[d][:rows, vcols] for d in range(earlier, -1, -1)], axis=0)
        contract = (((1,), (1,)), ((), ()))
        s_pre = lax.dot_general(queries, prefix[:, cols], contract, preferred_element_type=F32)
        s_suf = lax.dot_general(queries, keys, contract, preferred_element_type=F32) + bias
        top = jnp.maximum(jnp.max(s_pre, axis=-1, keepdims=True), jnp.max(s_suf, axis=-1, keepdims=True))
        p_pre, p_suf = jnp.exp(s_pre - top), jnp.exp(s_suf - top)
        total = jnp.sum(p_pre, axis=-1, keepdims=True) + jnp.sum(p_suf, axis=-1, keepdims=True)
        numerator = jnp.dot(p_pre.astype(BF16), prefix[:, vcols], preferred_element_type=F32)
        numerator += jnp.dot(p_suf.astype(BF16), values, preferred_element_type=F32)
        context = (numerator / total).astype(BF16)
        for r in range(REPEATS):
            out[:, base + r * HD:base + (r + 1) * HD] = context[r * rows:(r + 1) * rows]


def attend(q_mine, q_theirs, prefix, seg_col, blocks, scalars):
    rows = q_mine.shape[0]
    earlier = len(blocks) - 1
    vmem = pl.BlockSpec(memory_space=pltpu.VMEM)
    keys = prefix.shape[0] + rows * (earlier + 1)
    return pl.pallas_call(
        functools.partial(attend_kernel, earlier),
        out_shape=jax.ShapeDtypeStruct((rows, QW), BF16),
        in_specs=[pl.BlockSpec(memory_space=pltpu.SMEM)] + [vmem] * (4 + len(blocks)),
        out_specs=vmem,
        scratch_shapes=[pltpu.VMEM((rows, QW), BF16)],
        compiler_params=pltpu.CompilerParams(vmem_limit_bytes=40 << 20),
        cost_estimate=pl.CostEstimate(
            flops=4 * rows * keys * QW, bytes_accessed=4 * keys * KVW, transcendentals=rows * keys * QW // HD
        ),
    )(scalars, q_mine, q_theirs, prefix, seg_col, *blocks)


def swap_body(tokens, norm_gain, w_qkv, prefix_kv, segments):
    inputs, seg_ids, own_prefix = tokens[0], segments[0], prefix_kv[0]
    rows = inputs.shape[0]
    gx, core, z, y = (lax.axis_index(a) for a in ("gx", "core", "z", "y"))
    z_count, y_count = lax.axis_size("z"), lax.axis_size("y")
    index = z * y_count + y
    depth = w_qkv.shape[0]

    kv_own = lax.dynamic_slice_in_dim(w_qkv, QW + core * KVW, KVW, 1)
    kv_send = lax.dynamic_slice_in_dim(w_qkv, QW + (1 - core) * KVW, KVW, 1)
    q_own = lax.dynamic_slice_in_dim(w_qkv, core * QH, QH, 1)
    q_send = lax.dynamic_slice_in_dim(w_qkv, (1 - core) * QH, QH, 1)
    kv_got, q_got = swap(kv_send, "core"), swap(q_send, "core")

    spots = []
    for dz in range(4):
        for dx in range(2):
            for dy in range(2):
                for half in range(2):
                    block = (((gx ^ dx) * 2 + (core ^ half)) * z_count + (z ^ dz)) * y_count + (y ^ dy)
                    spots.append(block * depth)
    pos = jnp.stack(spots).astype(jnp.int32)

    kv_pieces, kv_places = gather_columns(kv_own, kv_got)
    q_pieces, q_places = gather_columns(q_own, q_got)

    normed = rms_norm(inputs, norm_gain)
    normed_sibling = swap(normed, "core")

    kv_mine, kv_theirs = project(normed, normed_sibling, kv_pieces, kv_places, pos, None)
    kv_other = swap(kv_theirs, "core")
    low = core == 0
    seg_row = jnp.pad(seg_ids.astype(BF16)[None, :], ((0, 7), (0, 2 * KVW - rows)))
    block = jnp.concatenate(
        [
            jnp.concatenate([jnp.where(low, kv_mine, kv_other), jnp.where(low, kv_other, kv_mine)], axis=1),
            seg_row,
        ],
        axis=0,
    )
    seq_count = z_count * y_count
    earlier = -(-(seq_count // 2 * rows - 1) // rows)
    blocks = [block] + [
        lax.ppermute(block, ("z", "y"), [(s, s + d) for s in range(seq_count - d)]) for d in range(1, earlier + 1)
    ]

    q_mine, q_theirs = project(normed, normed_sibling, q_pieces, q_places, pos, 0.125)
    q_other = swap(q_theirs, "core")

    line = jnp.concatenate([own_prefix] + [z_swap(own_prefix, d) for d in (1, 2, 3)])
    prefix = jnp.concatenate([line, swap(line, "y")])

    scalars = jnp.stack([core, index]).astype(jnp.int32)
    context = attend(q_mine, q_other, prefix, seg_ids.astype(F32)[:, None], blocks, scalars)
    return context[None]


def gather_body(tokens, norm_gain, w_qkv, prefix_kv, segments):
    inputs, seg_ids = tokens[0], segments[0]
    rows = inputs.shape[0]
    normed = rms_norm(inputs, norm_gain)
    weights = lax.all_gather(w_qkv, ("gx", "core", "z", "y"), axis=0, tiled=True)
    projected = jnp.dot(normed, weights, preferred_element_type=F32).astype(BF16)
    queries = projected[:, :QW].reshape(rows, KEY_HEADS, REPEATS, HD)

    def absorb(state, keyvals, visible):
        running_max, denominator, numerator = state
        count = keyvals.shape[0]
        key_part = keyvals[:, :KVW].reshape(count, KEY_HEADS, HD)
        value_part = keyvals[:, KVW:].reshape(count, KEY_HEADS, HD)
        scores = jnp.einsum("tgrd,ngd->tgrn", queries, key_part, preferred_element_type=F32) * 0.125
        if visible is not None:
            scores = jnp.where(visible[:, None, None, :], scores, F32(NEG))
        new_max = jnp.maximum(running_max, jnp.max(scores, axis=-1))
        probability = jnp.exp(scores - new_max[..., None])
        if visible is not None:
            probability = jnp.where(visible[:, None, None, :], probability, F32(0.0))
        factor = jnp.exp(running_max - new_max)
        denominator = denominator * factor + jnp.sum(probability, axis=-1)
        numerator = numerator * factor[..., None] + jnp.einsum(
            "tgrn,ngd->tgrd", probability.astype(BF16), value_part, preferred_element_type=F32
        )
        return new_max, denominator, numerator

    def sweep(state, keyvals, key_seg):
        length = min(keyvals.shape[0], 512)

        def step(i, running):
            start = i * length
            part = lax.dynamic_slice_in_dim(keyvals, start, length, 0)
            if key_seg is None:
                return absorb(running, part, None)
            seg_part = lax.dynamic_slice_in_dim(key_seg, start, length, 0)
            key_pos = start + jnp.arange(length, dtype=jnp.int32)
            visible = (seg_part[None, :] == seg_ids[:, None]) & (key_pos[None, :] <= query_pos[:, None])
            return absorb(running, part, visible)

        return lax.fori_loop(0, keyvals.shape[0] // length, step, state)

    query_pos = lax.axis_index(("z", "y")) * rows + jnp.arange(rows, dtype=jnp.int32)
    state = (
        jnp.full((rows, KEY_HEADS, REPEATS), NEG, F32),
        jnp.zeros((rows, KEY_HEADS, REPEATS), F32),
        jnp.zeros((rows, KEY_HEADS, REPEATS, HD), F32),
    )
    along = functools.partial(lax.all_gather, axis_name=("z", "y"), axis=0, tiled=True)
    state = sweep(state, along(prefix_kv[0]), None)
    _, denominator, numerator = sweep(state, along(projected[:, QW:]), along(seg_ids))
    return (numerator / denominator[..., None]).reshape(rows, QW).astype(BF16)[None]


def solution(mesh):
    groups, seqs = mesh.shape["group"], mesh.shape["seq"]
    chips, z_count = groups // 2, seqs // 2
    fine = Mesh(mesh.devices.reshape(chips, 2, z_count, 2), ("gx", "core", "z", "y"))
    group, seq = ("gx", "core"), ("z", "y")
    short = chips == 2 and z_count == SMALL
    return jax.shard_map(
        swap_body if short else gather_body,
        mesh=fine,
        in_specs=(P(group, seq, None), P(), P(group + seq, None), P(group, seq, None), P(group, seq)),
        out_specs=P(group, seq, None),
        check_vma=False,
    )
```

time: 170 us -> 112 us (0.66)
  the two profiles are of different devices: /device:TPU:0 before, /device:TPU:30 now
where the time goes in v1:
time: 112 us
  waiting for transfers between devices  53.6 us (48%)
  starting transfers between devices  30.7 us (27%)
  Pallas kernels  16.4 us (15%)
  local copies, waits for them, and re-layouts  6.92 us (6%)
  other arithmetic  3.49 us (3%)
    ppermute x9, waiting for transfers between devices, z_swap(): return lax.ppermute(x, 'z', [(i, i ^ distance) for i in range(4)])  25.5 us
    ppermute x22, starting transfers between devices, swap(): return lax.ppermute(x, axis, [(0, 1), (1, 0)])  20.3 us
    ppermute x22, waiting for transfers between devices, swap(): return lax.ppermute(x, axis, [(0, 1), (1, 0)])  15.2 us
    ppermute x4, waiting for transfers between devices, swap_body(): lax.ppermute(block, ('z', 'y'), [(s, s + d) for s in range(seq_count - d)])  13 us
    pallas_call x2, Pallas kernels, project(): pl.pallas_call(functools.partial(project_kernel, scale, len(pieces), plac...  10 us
    pallas_call x1, Pallas kernels, attend(): pl.pallas_call(functools.partial(attend_kernel, earlier), out_shape=jax.S...  6.34 us
    ppermute x9, starting transfers between devices, z_swap(): return lax.ppermute(x, 'z', [(i, i ^ distance) for i in range(4)])  5.18 us
    ppermute x4, starting transfers between devices, swap_body(): lax.ppermute(block, ('z', 'y'), [(s, s + d) for s in range(seq_count - d)])  5.15 us
  transfers between devices with their start and end apart: 35, of which 11 were waited for; matrix products, arithmetic and copies ran while one was open for 5% of the time, Pallas kernels for 9%

profile of v1, /device:TPU:30, one launch (start us, length us, event | category | flops | bytes accessed | tf_op | source)
XLA Modules:
  0.0 111.5 jit_solution(9278731992669211997)
XLA Ops:
  6.2 5.2 %collective-permute-done.23 = bf16[128,320]{1,0:T(8,128)(2,1)S(1)} collective-permute-done((bf16[128,320]{1,0:T(8,128)(2,1)S(1)}, bf16[128,320]{1,0:T(8,128)(2,1)S(1)}, u32[]{:S(2)}, u32[]{:S(2)}) %collective-permute-start.23) | collective-permute-done | bytes 81952 | tf_op jit(solution)/shard_map/ppermute | solution.py:33
  11.4 4.1 %collective-permute-done.24 = bf16[128,320]{1,0:T(8,128)(2,1)S(1)} collective-permute-done((bf16[128,320]{1,0:T(8,128)(2,1)S(1)}, bf16[128,320]{1,0:T(8,128)(2,1)S(1)}, u32[]{:S(2)}, u32[]{:S(2)}) %collective-permute-start.24) | collective-permute-done | bytes 81952 | tf_op jit(solution)/shard_map/ppermute | solution.py:33
  15.5 2.3 %collective-permute-done.25 = bf16[128,320]{1,0:T(8,128)(2,1)S(1)} collective-permute-done((bf16[128,320]{1,0:T(8,128)(2,1)S(1)}, bf16[128,320]{1,0:T(8,128)(2,1)S(1)}, u32[]{:S(2)}, u32[]{:S(2)}) %collective-permute-start.25) | collective-permute-done | bytes 81952 | tf_op jit(solution)/shard_map/ppermute | solution.py:33
  18.3 1.8 %collective-permute-start.8 = (bf16[128,640]{1,0:T(8,128)(2,1)S(1)}, bf16[128,640]{1,0:T(8,128)(2,1)S(1)}, u32[]{:S(2)}, u32[]{:S(2)}) collective-permute-start(bf16[128,640]{1,0:T(8,128)(2,1)S(1)} %pad_maximum_fusion.1.refs_0_), channel_id=1, source_target_pairs={{0,6},{2,4},{4,2},{6,0},{1,7},{3,5},{5,3},{7,1},{8,14},{10,12},{12... | collective-permute-start | bytes 491528 | tf_op jit(solution)/shard_map/ppermute | solution.py:33
  20.7 1.5 %collective-permute-start.26 = (bf16[384,320]{1,0:T(8,128)(2,1)S(1)}, bf16[384,320]{1,0:T(8,128)(2,1)S(1)}, u32[]{:S(2)}, u32[]{:S(2)}) collective-permute-start(bf16[384,320]{1,0:T(8,128)(2,1)S(1)} %constant_dynamic-update-slice_fusion.8.refs_5_), channel_id=1, source_target_pairs={{0,16},{16,0},{1,17},{17,1},{2,18},{18,2},{3,19},{19,3},{4,20},{20... | collective-permute-start | bytes 737288 | tf_op jit(solution)/shard_map/ppermute | solution.py:29
  23.4 1.5 %collective-permute-start.27 = (bf16[384,320]{1,0:T(8,128)(2,1)S(1)}, bf16[384,320]{1,0:T(8,128)(2,1)S(1)}, u32[]{:S(2)}, u32[]{:S(2)}) collective-permute-start(bf16[384,320]{1,0:T(8,128)(2,1)S(1)} %constant_dynamic-update-slice_fusion.8.refs_5_), channel_id=1, source_target_pairs={{0,1},{1,0},{2,3},{3,2},{4,5},{5,4},{6,7},{7,6},{8,9},{9,8},{10,11... | collective-permute-start | bytes 737288 | tf_op jit(solution)/shard_map/ppermute | solution.py:29
  25.0 5.4 %collective-permute-done.7 = bf16[128,640]{1,0:T(8,128)(2,1)S(1)} collective-permute-done((bf16[128,640]{1,0:T(8,128)(2,1)S(1)}, bf16[128,640]{1,0:T(8,128)(2,1)S(1)}, u32[]{:S(2)}, u32[]{:S(2)}) %collective-permute-start.7) | collective-permute-done | bytes 163872 | tf_op jit(solution)/shard_map/ppermute | solution.py:33
  30.4 4.4 %collective-permute-done.14 = bf16[64,640]{1,0:T(8,128)(2,1)S(1)} collective-permute-done((bf16[64,640]{1,0:T(8,128)(2,1)S(1)}, bf16[64,640]{1,0:T(8,128)(2,1)S(1)}, u32[]{:S(2)}, u32[]{:S(2)}) %collective-permute-start.14) | collective-permute-done | bytes 81952 | tf_op jit(solution)/shard_map/ppermute | solution.py:33
  35.4 2.2 %collective-permute-start.16 = (bf16[64,640]{1,0:T(8,128)(2,1)S(1)}, bf16[64,640]{1,0:T(8,128)(2,1)S(1)}, u32[]{:S(2)}, u32[]{:S(2)}) collective-permute-start(bf16[64,640]{1,0:T(8,128)(2,1)S(1)} %bitcast.46), channel_id=1, source_target_pairs={{0,6},{2,4},{4,2},{6,0},{1,7},{3,5},{5,3},{7,1},{8,14},{10,12},{12... | collective-permute-start | bytes 245768 | tf_op jit(solution)/shard_map/ppermute | solution.py:33
  37.7 4.1 %collective-permute-done.15 = bf16[64,640]{1,0:T(8,128)(2,1)S(1)} collective-permute-done((bf16[64,640]{1,0:T(8,128)(2,1)S(1)}, bf16[64,640]{1,0:T(8,128)(2,1)S(1)}, u32[]{:S(2)}, u32[]{:S(2)}) %collective-permute-start.15) | collective-permute-done | bytes 81952 | tf_op jit(solution)/shard_map/ppermute | solution.py:33
  41.8 1.9 %collective-permute-start.21 = (bf16[64,320]{1,0:T(8,128)(2,1)}, bf16[64,320]{1,0:T(8,128)(2,1)S(1)}, u32[]{:S(2)}, u32[]{:S(2)}) collective-permute-start(bf16[64,320]{1,0:T(8,128)(2,1)} %slice.36), channel_id=1, source_target_pairs={{0,1},{1,0},{2,3},{3,2},{4,5},{5,4},{6,7},{7,6},{8,9},{9,8},{10,11... | collective-permute-start | bytes 122888 | tf_op jit(solution)/shard_map/ppermute | solution.py:29
  43.7 1.5 %collective-permute-start.22 = (bf16[64,320]{1,0:T(8,128)(2,1)}, bf16[64,320]{1,0:T(8,128)(2,1)}, u32[]{:S(2)}, u32[]{:S(2)}) collective-permute-start(bf16[64,320]{1,0:T(8,128)(2,1)} %slice.37), channel_id=1, source_target_pairs={{0,16},{16,0},{1,17},{17,1},{2,18},{18,2},{3,19},{19,3},{4,20},{20... | collective-permute-start | bytes 122888 | tf_op jit(solution)/shard_map/ppermute | solution.py:29
  48.0 1.9 %collective-permute-start.28 = (bf16[192,320]{1,0:T(8,128)(2,1)}, bf16[192,320]{1,0:T(8,128)(2,1)}, u32[]{:S(2)}, u32[]{:S(2)}) collective-permute-start(bf16[192,320]{1,0:T(8,128)(2,1)} %slice.38), channel_id=1, source_target_pairs={{0,1},{1,0},{2,3},{3,2},{4,5},{5,4},{6,7},{7,6},{8,9},{9,8},{10,11... | collective-permute-start | bytes 368648 | tf_op jit(solution)/shard_map/ppermute | solution.py:29
  49.9 1.5 %collective-permute-start.29 = (bf16[192,320]{1,0:T(8,128)(2,1)}, bf16[192,320]{1,0:T(8,128)(2,1)}, u32[]{:S(2)}, u32[]{:S(2)}) collective-permute-start(bf16[192,320]{1,0:T(8,128)(2,1)} %slice.39), channel_id=1, source_target_pairs={{0,16},{16,0},{1,17},{17,1},{2,18},{18,2},{3,19},{19,3},{4,20},{20... | collective-permute-start | bytes 368648 | tf_op jit(solution)/shard_map/ppermute | solution.py:29
  52.7 5.7 %collective-permute-done.28.refs_8_ = bf16[192,320]{1,0:T(8,128)(2,1)} collective-permute-done((bf16[192,320]{1,0:T(8,128)(2,1)}, bf16[192,320]{1,0:T(8,128)(2,1)}, u32[]{:S(2)}, u32[]{:S(2)}) %collective-permute-start.28) | collective-permute-done | bytes 122912 | tf_op jit(solution)/shard_map/ppermute | solution.py:29
  58.4 1.5 %collective-permute-start.2 = (bf16[128,640]{1,0:T(8,128)(2,1)S(1)}, bf16[128,640]{1,0:T(8,128)(2,1)S(1)}, u32[]{:S(2)}, u32[]{:S(2)}) collective-permute-start(bf16[128,640]{1,0:T(8,128)(2,1)S(1)} %pad_maximum_fusion.1.refs_0_), channel_id=1, source_target_pairs={{0,16},{16,0},{1,17},{17,1},{2,18},{18,2},{3,19},{19,3},{4,20},{20... | collective-permute-start | bytes 491528 | tf_op jit(solution)/shard_map/ppermute | solution.py:29
  61.6 4.3 %shard_map.56 = (bf16[128,320]{1,0:T(8,128)(2,1)S(1)}, bf16[128,320]{1,0:T(8,128)(2,1)S(1)}) custom-call(s32[32]{0:T(128)S(1)} %stack.143.pos, bf16[128,2048]{1,0:T(8,128)(2,1)S(1)} %fusion.2.own, bf16[128,2048]{1,0:T(8,128)(2,1)S(1)} %collective-permute-done.other, bf16[128,320]{1,0:T(8,128)(2,1)S(1)} %pad_maximum_fusion.2.refs_0_, ...), custom_call_target="tpu_custom_call" | custom-call | flops 335544320 | bytes 3407872 | tf_op jit(solution)/shard_map/pallas_call | solution.py:65
  70.0 1.6 %collective-permute-start.12 = (bf16[192,640]{1,0:T(8,128)(2,1)S(1)}, bf16[192,640]{1,0:T(8,128)(2,1)S(1)}, u32[]{:S(2)}, u32[]{:S(2)}) collective-permute-start(bf16[192,640]{1,0:T(8,128)(2,1)S(1)} %slice.35), channel_id=1, source_target_pairs={{0,16},{16,0},{1,17},{17,1},{2,18},{18,2},{3,19},{19,3},{4,20},{20... | collective-permute-start | bytes 737288 | tf_op jit(solution)/shard_map/ppermute | solution.py:29
  71.7 6.7 %collective-permute-done.4.refs_3_ = bf16[64,640]{1,0:T(8,128)(2,1)S(1)} collective-permute-done((bf16[64,640]{1,0:T(8,128)(2,1)S(1)}, bf16[64,640]{1,0:T(8,128)(2,1)S(1)}, u32[]{:S(2)}, u32[]{:S(2)}) %collective-permute-start.4) | collective-permute-done | bytes 81952 | tf_op jit(solution)/shard_map/ppermute | solution.py:29
  79.7 1.3 %collective-permute-start.32 = (bf16[136,640]{1,0:T(8,128)(2,1)S(1)}, bf16[136,640]{1,0:T(8,128)(2,1)S(1)}, u32[]{:S(2)}, u32[]{:S(2)}) collective-permute-start(bf16[136,640]{1,0:T(8,128)(2,1)S(1)} %fusion.4.refs_0_), channel_id=1, source_target_pairs={{0,2},{1,3},{2,4},{3,5},{4,6},{5,7},{8,10},{9,11},{10,12},{11,13},... | collective-permute-start | bytes 522248 | tf_op jit(solution)/shard_map/ppermute | solution.py:203
  81.0 2.7 %collective-permute-done.11.refs_8_ = bf16[192,640]{1,0:T(8,128)(2,1)S(1)} collective-permute-done((bf16[192,640]{1,0:T(8,128)(2,1)S(1)}, bf16[192,640]{1,0:T(8,128)(2,1)S(1)}, u32[]{:S(2)}, u32[]{:S(2)}) %collective-permute-start.11) | collective-permute-done | bytes 245792 | tf_op jit(solution)/shard_map/ppermute | solution.py:29
  86.3 5.7 %shard_map.55 = (bf16[128,640]{1,0:T(8,128)(2,1)S(1)}, bf16[128,640]{1,0:T(8,128)(2,1)S(1)}) custom-call(s32[32]{0:T(128)S(1)} %stack.143.pos, bf16[128,2048]{1,0:T(8,128)(2,1)S(1)} %fusion.2.own, bf16[128,2048]{1,0:T(8,128)(2,1)S(1)} %collective-permute-done.other, bf16[128,640]{1,0:T(8,128)(2,1)S(1)} %pad_maximum_fusion.1.refs_0_, ...), custom_call_target="tpu_custom_call" | custom-call | flops 671088640 | bytes 4718592 | tf_op jit(solution)/shard_map/pallas_call | solution.py:65
  93.5 11.7 %collective-permute-done.34.refs_4_ = bf16[136,640]{1,0:T(8,128)(2,1)S(1)} collective-permute-done((bf16[136,640]{1,0:T(8,128)(2,1)S(1)}, bf16[136,640]{1,0:T(8,128)(2,1)S(1)}, u32[]{:S(2)}, u32[]{:S(2)}) %collective-permute-start.34) | collective-permute-done | bytes 174112 | tf_op jit(solution)/shard_map/ppermute | solution.py:203
  105.2 6.3 %shard_map.57 = bf16[128,1280]{1,0:T(8,128)(2,1)} custom-call(s32[2]{0:T(128)S(1)} %pad_add_fusion.scalars, bf16[128,640]{1,0:T(8,128)(2,1)S(1)} %get-tuple-element.9.q_mine, bf16[128,640]{1,0:T(8,128)(2,1)S(1)} %collective-permute-done.13.q_theirs, bf16[512,640]{1,0:T(8,128)(2,1)S(1)} %constant_dynamic-update-slice_fusion.3.prefix, ...), custom_call_target="tpu_custom_call" | custom-call | flops 754974720 | bytes 1474560 | tf_op jit(solution)/shard_map/pallas_call | solution.py:147
  (117 shorter events, 24.3 us)
Async XLA Ops:
  2.2 59.4 %collective-permute-start = (bf16[128,2048]{1,0:T(8,128)(2,1)S(1)}, bf16[128,2048]{1,0:T(8,128)(2,1)S(1)}, u32[]{:S(2)}, u32[]{:S(2)}) collective-permute-start(bf16[128,2048]{1,0:T(8,128)(2,1)S(1)} %fusion.2.own), channel_id=1, source_target_pairs={{0,8},{8,0},{1,9},{9,1},{2,10},{10,2},{3,11},{11,3},{4,12},{12,4},... | collective-permute-start | bytes 1572872 | tf_op jit(solution)/shard_map/ppermute | solution.py:29
  4.6 13.7 %collective-permute-start.19 = (bf16[128,320]{1,0:T(8,128)(2,1)S(1)}, bf16[128,320]{1,0:T(8,128)(2,1)S(1)}, u32[]{:S(2)}, u32[]{:S(2)}) collective-permute-start(bf16[128,320]{1,0:T(8,128)(2,1)S(1)} %pad_maximum_fusion.2.refs_0_), channel_id=1, source_target_pairs={{0,16},{16,0},{1,17},{17,1},{2,18},{18,2},{3,19},{19,3},{4,20},{20... | collective-permute-start | bytes 245768 | tf_op jit(solution)/shard_map/ppermute | solution.py:29
  5.2 15.5 %collective-permute-start.20 = (bf16[128,320]{1,0:T(8,128)(2,1)S(1)}, bf16[128,320]{1,0:T(8,128)(2,1)S(1)}, u32[]{:S(2)}, u32[]{:S(2)}) collective-permute-start(bf16[128,320]{1,0:T(8,128)(2,1)S(1)} %pad_maximum_fusion.2.refs_0_), channel_id=1, source_target_pairs={{0,1},{1,0},{2,3},{3,2},{4,5},{5,4},{6,7},{7,6},{8,9},{9,8},{10,11... | collective-permute-start | bytes 245768 | tf_op jit(solution)/shard_map/ppermute | solution.py:29
  6.2 9.3 %collective-permute-start.24 = (bf16[128,320]{1,0:T(8,128)(2,1)S(1)}, bf16[128,320]{1,0:T(8,128)(2,1)S(1)}, u32[]{:S(2)}, u32[]{:S(2)}) collective-permute-start(bf16[128,320]{1,0:T(8,128)(2,1)S(1)} %pad_maximum_fusion.2.refs_0_), channel_id=1, source_target_pairs={{0,4},{2,6},{4,0},{6,2},{1,5},{3,7},{5,1},{7,3},{8,12},{10,14},{12... | collective-permute-start | bytes 245768 | tf_op jit(solution)/shard_map/ppermute | solution.py:33
  15.5 8.0 %collective-permute-start.6 = (bf16[128,640]{1,0:T(8,128)(2,1)S(1)}, bf16[128,640]{1,0:T(8,128)(2,1)S(1)}, u32[]{:S(2)}, u32[]{:S(2)}) collective-permute-start(bf16[128,640]{1,0:T(8,128)(2,1)S(1)} %pad_maximum_fusion.1.refs_0_), channel_id=1, source_target_pairs={{0,2},{2,0},{4,6},{6,4},{1,3},{3,1},{5,7},{7,5},{8,10},{10,8},{12,... | collective-permute-start | bytes 491528 | tf_op jit(solution)/shard_map/ppermute | solution.py:33
  17.8 12.5 %collective-permute-start.7 = (bf16[128,640]{1,0:T(8,128)(2,1)S(1)}, bf16[128,640]{1,0:T(8,128)(2,1)S(1)}, u32[]{:S(2)}, u32[]{:S(2)}) collective-permute-start(bf16[128,640]{1,0:T(8,128)(2,1)S(1)} %pad_maximum_fusion.1.refs_0_), channel_id=1, source_target_pairs={{0,4},{2,6},{4,0},{6,2},{1,5},{3,7},{5,1},{7,3},{8,12},{10,14},{12... | collective-permute-start | bytes 491528 | tf_op jit(solution)/shard_map/ppermute | solution.py:33
  18.3 17.2 %collective-permute-start.8 = (bf16[128,640]{1,0:T(8,128)(2,1)S(1)}, bf16[128,640]{1,0:T(8,128)(2,1)S(1)}, u32[]{:S(2)}, u32[]{:S(2)}) collective-permute-start(bf16[128,640]{1,0:T(8,128)(2,1)S(1)} %pad_maximum_fusion.1.refs_0_), channel_id=1, source_target_pairs={{0,6},{2,4},{4,2},{6,0},{1,7},{3,5},{5,3},{7,1},{8,14},{10,12},{12... | collective-permute-start | bytes 491528 | tf_op jit(solution)/shard_map/ppermute | solution.py:33
  20.7 24.5 %collective-permute-start.26 = (bf16[384,320]{1,0:T(8,128)(2,1)S(1)}, bf16[384,320]{1,0:T(8,128)(2,1)S(1)}, u32[]{:S(2)}, u32[]{:S(2)}) collective-permute-start(bf16[384,320]{1,0:T(8,128)(2,1)S(1)} %constant_dynamic-update-slice_fusion.8.refs_5_), channel_id=1, source_target_pairs={{0,16},{16,0},{1,17},{17,1},{2,18},{18,2},{3,19},{19,3},{4,20},{20... | collective-permute-start | bytes 737288 | tf_op jit(solution)/shard_map/ppermute | solution.py:29
  23.4 22.3 %collective-permute-start.27 = (bf16[384,320]{1,0:T(8,128)(2,1)S(1)}, bf16[384,320]{1,0:T(8,128)(2,1)S(1)}, u32[]{:S(2)}, u32[]{:S(2)}) collective-permute-start(bf16[384,320]{1,0:T(8,128)(2,1)S(1)} %constant_dynamic-update-slice_fusion.8.refs_5_), channel_id=1, source_target_pairs={{0,1},{1,0},{2,3},{3,2},{4,5},{5,4},{6,7},{7,6},{8,9},{9,8},{10,11... | collective-permute-start | bytes 737288 | tf_op jit(solution)/shard_map/ppermute | solution.py:29
  35.4 8.2 %collective-permute-start.16 = (bf16[64,640]{1,0:T(8,128)(2,1)S(1)}, bf16[64,640]{1,0:T(8,128)(2,1)S(1)}, u32[]{:S(2)}, u32[]{:S(2)}) collective-permute-start(bf16[64,640]{1,0:T(8,128)(2,1)S(1)} %bitcast.46), channel_id=1, source_target_pairs={{0,6},{2,4},{4,2},{6,0},{1,7},{3,5},{5,3},{7,1},{8,14},{10,12},{12... | collective-permute-start | bytes 245768 | tf_op jit(solution)/shard_map/ppermute | solution.py:33
  45.2 23.1 %collective-permute-start.9 = (bf16[384,640]{1,0:T(8,128)(2,1)S(1)}, bf16[384,640]{1,0:T(8,128)(2,1)S(1)}, u32[]{:S(2)}, u32[]{:S(2)}) collective-permute-start(bf16[384,640]{1,0:T(8,128)(2,1)S(1)} %constant_dynamic-update-slice_fusion.refs_5_), channel_id=1, source_target_pairs={{0,16},{16,0},{1,17},{17,1},{2,18},{18,2},{3,19},{19,3},{4,20},{20... | collective-permute-start | bytes 1474568 | tf_op jit(solution)/shard_map/ppermute | solution.py:29
  45.7 23.1 %collective-permute-start.10 = (bf16[384,640]{1,0:T(8,128)(2,1)S(1)}, bf16[384,640]{1,0:T(8,128)(2,1)S(1)}, u32[]{:S(2)}, u32[]{:S(2)}) collective-permute-start(bf16[384,640]{1,0:T(8,128)(2,1)S(1)} %constant_dynamic-update-slice_fusion.refs_5_), channel_id=1, source_target_pairs={{0,1},{1,0},{2,3},{3,2},{4,5},{5,4},{6,7},{7,6},{8,9},{9,8},{10,11... | collective-permute-start | bytes 1474568 | tf_op jit(solution)/shard_map/ppermute | solution.py:29
  48.0 10.4 %collective-permute-start.28 = (bf16[192,320]{1,0:T(8,128)(2,1)}, bf16[192,320]{1,0:T(8,128)(2,1)}, u32[]{:S(2)}, u32[]{:S(2)}) collective-permute-start(bf16[192,320]{1,0:T(8,128)(2,1)} %slice.38), channel_id=1, source_target_pairs={{0,1},{1,0},{2,3},{3,2},{4,5},{5,4},{6,7},{7,6},{8,9},{9,8},{10,11... | collective-permute-start | bytes 368648 | tf_op jit(solution)/shard_map/ppermute | solution.py:29
  49.9 10.0 %collective-permute-start.29 = (bf16[192,320]{1,0:T(8,128)(2,1)}, bf16[192,320]{1,0:T(8,128)(2,1)}, u32[]{:S(2)}, u32[]{:S(2)}) collective-permute-start(bf16[192,320]{1,0:T(8,128)(2,1)} %slice.39), channel_id=1, source_target_pairs={{0,16},{16,0},{1,17},{17,1},{2,18},{18,2},{3,19},{19,3},{4,20},{20... | collective-permute-start | bytes 368648 | tf_op jit(solution)/shard_map/ppermute | solution.py:29
  66.1 26.0 %collective-permute-start.17 = (bf16[256,640]{1,0:T(8,128)(2,1)S(1)}, bf16[256,640]{1,0:T(8,128)(2,1)S(1)}, u32[]{:S(2)}, u32[]{:S(2)}) collective-permute-start(bf16[256,640]{1,0:T(8,128)(2,1)S(1)} %pad_maximum_fusion), channel_id=1, source_target_pairs={{0,1},{1,0},{2,3},{3,2},{4,5},{5,4},{6,7},{7,6},{8,9},{9,8},{10,11... | collective-permute-start | bytes 983048 | tf_op jit(solution)/shard_map/ppermute | solution.py:29
  67.1 11.3 %collective-permute-start.4 = (bf16[64,640]{1,0:T(8,128)(2,1)S(1)}, bf16[64,640]{1,0:T(8,128)(2,1)S(1)}, u32[]{:S(2)}, u32[]{:S(2)}) collective-permute-start(bf16[64,640]{1,0:T(8,128)(2,1)S(1)} %slice.32), channel_id=1, source_target_pairs={{0,1},{1,0},{2,3},{3,2},{4,5},{5,4},{6,7},{7,6},{8,9},{9,8},{10,11... | collective-permute-start | bytes 245768 | tf_op jit(solution)/shard_map/ppermute | solution.py:29
  68.3 11.4 %collective-permute-start.5 = (bf16[64,640]{1,0:T(8,128)(2,1)S(1)}, bf16[64,640]{1,0:T(8,128)(2,1)S(1)}, u32[]{:S(2)}, u32[]{:S(2)}) collective-permute-start(bf16[64,640]{1,0:T(8,128)(2,1)S(1)} %slice.33), channel_id=1, source_target_pairs={{0,16},{16,0},{1,17},{17,1},{2,18},{18,2},{3,19},{19,3},{4,20},{20... | collective-permute-start | bytes 245768 | tf_op jit(solution)/shard_map/ppermute | solution.py:29
  68.8 14.9 %collective-permute-start.11 = (bf16[192,640]{1,0:T(8,128)(2,1)S(1)}, bf16[192,640]{1,0:T(8,128)(2,1)S(1)}, u32[]{:S(2)}, u32[]{:S(2)}) collective-permute-start(bf16[192,640]{1,0:T(8,128)(2,1)S(1)} %slice.34), channel_id=1, source_target_pairs={{0,1},{1,0},{2,3},{3,2},{4,5},{5,4},{6,7},{7,6},{8,9},{9,8},{10,11... | collective-permute-start | bytes 737288 | tf_op jit(solution)/shard_map/ppermute | solution.py:29
  70.0 15.0 %collective-permute-start.12 = (bf16[192,640]{1,0:T(8,128)(2,1)S(1)}, bf16[192,640]{1,0:T(8,128)(2,1)S(1)}, u32[]{:S(2)}, u32[]{:S(2)}) collective-permute-start(bf16[192,640]{1,0:T(8,128)(2,1)S(1)} %slice.35), channel_id=1, source_target_pairs={{0,16},{16,0},{1,17},{17,1},{2,18},{18,2},{3,19},{19,3},{4,20},{20... | collective-permute-start | bytes 737288 | tf_op jit(solution)/shard_map/ppermute | solution.py:29
  78.4 13.8 %collective-permute-start.31 = (bf16[136,640]{1,0:T(8,128)(2,1)S(1)}, bf16[136,640]{1,0:T(8,128)(2,1)S(1)}, u32[]{:S(2)}, u32[]{:S(2)}) collective-permute-start(bf16[136,640]{1,0:T(8,128)(2,1)S(1)} %fusion.4.refs_0_), channel_id=1, source_target_pairs={{0,1},{1,2},{2,3},{3,4},{4,5},{5,6},{6,7},{8,9},{9,10},{10,11},{11... | collective-permute-start | bytes 522248 | tf_op jit(solution)/shard_map/ppermute | solution.py:203
  79.7 12.5 %collective-permute-start.32 = (bf16[136,640]{1,0:T(8,128)(2,1)S(1)}, bf16[136,640]{1,0:T(8,128)(2,1)S(1)}, u32[]{:S(2)}, u32[]{:S(2)}) collective-permute-start(bf16[136,640]{1,0:T(8,128)(2,1)S(1)} %fusion.4.refs_0_), channel_id=1, source_target_pairs={{0,2},{1,3},{2,4},{3,5},{4,6},{5,7},{8,10},{9,11},{10,12},{11,13},... | collective-permute-start | bytes 522248 | tf_op jit(solution)/shard_map/ppermute | solution.py:203
  83.7 9.8 %collective-permute-start.33 = (bf16[136,640]{1,0:T(8,128)(2,1)S(1)}, bf16[136,640]{1,0:T(8,128)(2,1)S(1)}, u32[]{:S(2)}, u32[]{:S(2)}) collective-permute-start(bf16[136,640]{1,0:T(8,128)(2,1)S(1)} %fusion.4.refs_0_), channel_id=1, source_target_pairs={{0,3},{1,4},{2,5},{3,6},{4,7},{8,11},{9,12},{10,13},{11,14},{12,15... | collective-permute-start | bytes 522248 | tf_op jit(solution)/shard_map/ppermute | solution.py:203
  85.0 20.2 %collective-permute-start.34 = (bf16[136,640]{1,0:T(8,128)(2,1)S(1)}, bf16[136,640]{1,0:T(8,128)(2,1)S(1)}, u32[]{:S(2)}, u32[]{:S(2)}) collective-permute-start(bf16[136,640]{1,0:T(8,128)(2,1)S(1)} %fusion.4.refs_0_), channel_id=1, source_target_pairs={{0,4},{1,5},{2,6},{3,7},{8,12},{9,13},{10,14},{11,15},{16,20},{17,... | collective-permute-start | bytes 522248 | tf_op jit(solution)/shard_map/ppermute | solution.py:203
  92.0 13.1 %collective-permute-start.13 = (bf16[128,640]{1,0:T(8,128)(2,1)S(1)}, bf16[128,640]{1,0:T(8,128)(2,1)S(1)}, u32[]{:S(2)}, u32[]{:S(2)}) collective-permute-start(bf16[128,640]{1,0:T(8,128)(2,1)S(1)} %get-tuple-element.10), channel_id=1, source_target_pairs={{0,8},{8,0},{1,9},{9,1},{2,10},{10,2},{3,11},{11,3},{4,12},{12,4},... | collective-permute-start | bytes 491528 | tf_op jit(solution)/shard_map/ppermute | solution.py:29
  (28 other events, 150.6 us)

commit v2 on v1

v2 whole, which is shorter than its diff:
```python
import functools

import jax
import jax.numpy as jnp
from jax import lax
from jax.experimental import pallas as pl
from jax.experimental.pallas import tpu as pltpu
from jax.sharding import Mesh, PartitionSpec as P

HD = 64
QW = 1280
KVW = 320
KEY_HEADS = KVW // HD
REPEATS = QW // KVW
QH, QQ = QW // 2, QW // 4
NEG = -1e30
SMALL = 4
F32 = jnp.float32
BF16 = jnp.bfloat16


def rms_norm(inputs, norm_gain):
    values = inputs.astype(F32)
    mean_square = jnp.mean(values * values, axis=-1, keepdims=True)
    return (values * lax.rsqrt(mean_square + 1e-05) * norm_gain.astype(F32)).astype(BF16)


def swap(x, axis):
    return lax.ppermute(x, axis, [(0, 1), (1, 0)])


def z_swap(x, distance):
    return lax.ppermute(x, "z", [(i, i ^ distance) for i in range(4)])


def sides(piece):
    return swap(piece, "gx"), swap(piece, "y")


def corner(near_sides, far_sides):
    (near_x, near_y), (far_x, far_y) = near_sides, far_sides
    near, far = near_x.shape[0] // 2, far_x.shape[0] // 2
    low = swap(jnp.concatenate([near_x[:near], far_x[:far]]), "y")
    high = swap(jnp.concatenate([near_y[near:], far_y[far:]]), "gx")
    return low, high


def order_kernel(order, bits, *refs):
    sources, out = refs[:-1], refs[-1]
    at = 0
    for source in sources:
        rows, depth = source.shape
        x = source[...]
        for bit in range((depth // 64).bit_length() - 1):
            span = 64 << bit
            parts = [x[:, (i ^ 1) * span:((i ^ 1) + 1) * span] for i in range(depth // span)]
            x = jnp.where(bits[bit] == 1, jnp.concatenate(parts, axis=1), x)
        out[at:at + rows, :] = jnp.concatenate([x[:, b * 64:(b + 1) * 64] for b in order], axis=1)
        at += rows


def order_features(sources, order, bits):
    depth = sources[0].shape[1]
    rows = sum(x.shape[0] for x in sources)
    vmem = pl.BlockSpec(memory_space=pltpu.VMEM)
    return pl.pallas_call(
        functools.partial(order_kernel, order),
        out_shape=jax.ShapeDtypeStruct((rows, depth), BF16),
        in_specs=[pl.BlockSpec(memory_space=pltpu.SMEM)] + [vmem] * len(sources),
        out_specs=vmem,
        compiler_params=pltpu.CompilerParams(vmem_limit_bytes=24 << 20),
        cost_estimate=pl.CostEstimate(flops=0, bytes_accessed=4 * rows * depth, transcendentals=0),
    )(bits, *sources)


def add_products(total, features, at, pieces, side):
    for piece in pieces:
        rows, width = piece.shape[0], piece.shape[1] // side
        for i in range(side):
            term = jnp.dot(
                features[:, at:at + rows], piece[:, i * width:(i + 1) * width], preferred_element_type=F32
            )
            total = term if total is None else total + term
            at += rows
    return total


def first_kernel(side, features, *refs):
    pieces, out = refs[:-1], refs[-1]
    out[...] = add_products(None, features, 0, pieces, side)


def last_kernel(side, at, n_late, scale, features, so_far, *refs):
    late, outs = refs[:n_late], refs[n_late:]
    result = add_products(so_far[...], features, at, late, side).astype(BF16)
    if scale is not None:
        result = result * jnp.asarray(scale, BF16)
    rows = outs[0].shape[0]
    for i, out in enumerate(outs):
        out[...] = result[i * rows:(i + 1) * rows]


def project(features, pieces, side, parts, scale, late):
    rows, depth = features.shape
    width = pieces[0].shape[1] // side
    vmem = pl.BlockSpec(memory_space=pltpu.VMEM)
    early = len(pieces) - late
    params = pltpu.CompilerParams(vmem_limit_bytes=24 << 20)
    done = side * sum(p.shape[0] for p in pieces[:early])

    def cost(deep):
        return pl.CostEstimate(flops=2 * rows * deep * width, bytes_accessed=2 * deep * (width + rows), transcendentals=0)

    so_far = pl.pallas_call(
        functools.partial(first_kernel, side),
        out_shape=jax.ShapeDtypeStruct((rows, width), F32),
        in_specs=[vmem] * (1 + early),
        out_specs=vmem,
        compiler_params=params,
        cost_estimate=cost(done),
    )(features, *pieces[:early])
    return pl.pallas_call(
        functools.partial(last_kernel, side, done, late, scale),
        out_shape=[jax.ShapeDtypeStruct((rows // parts, width), BF16)] * parts,
        in_specs=[vmem] * (2 + late),
        out_specs=[vmem] * parts,
        compiler_params=params,
        cost_estimate=cost(depth - done),
    )(features, so_far, *pieces[early:])


def piece_order(near, far):
    pieces = [(dx, dy, some) for some in (near, far) for dx, dy in ((0, 0), (1, 0), (0, 1))]
    pieces += [(1, 1, near[:len(near) // 2] + far[:len(far) // 2]), (1, 1, near[len(near) // 2:] + far[len(far) // 2:])]
    return [[((dx * 2 + half) * 4 + dz) * 2 + dy for half, dz in some] for dx, dy, some in pieces]


def after(first, *then):
    return lax.optimization_barrier((first,) + then)[1:]


def attend_kernel(earlier, scalars, mine, pair, sibling, diagonal, prefix, seg_col, *refs):
    blocks, out, q_all = refs[:earlier + 1], refs[earlier + 1], refs[earlier + 2]
    quarter = scalars[0]
    rows = mine.shape[0]
    for i, part in enumerate((mine, pair, sibling, diagonal)):
        q_all[quarter ^ i] = part[...]
    biases = []
    q_seg = seg_col[...]
    for i, block in enumerate(blocks):
        k_seg = block[rows:rows + 1, :rows].astype(F32)
        seen = q_seg == k_seg
        if i == 0:
            q_at = lax.broadcasted_iota(jnp.int32, (rows, rows), 0)
            k_at = lax.broadcasted_iota(jnp.int32, (rows, rows), 1)
            seen = seen & (k_at <= q_at)
            biases.append(jnp.where(seen, 0.0, NEG))
        else:
            biases.append(jnp.where(seen, jnp.where(scalars[1 + i] == 0, 0.0, NEG), NEG))
    bias = jnp.concatenate(biases, axis=1)
    bias = jnp.concatenate([bias] * REPEATS, axis=0)
    for head in range(KEY_HEADS):
        cols, vcols = slice(head * HD, (head + 1) * HD), slice(KVW + head * HD, KVW + (head + 1) * HD)
        base = head * REPEATS * HD
        heads = [divmod(head * REPEATS + r, QQ // HD) for r in range(REPEATS)]
        queries = jnp.concatenate([q_all[part, :, h * HD:(h + 1) * HD] for part, h in heads], axis=0)
        keys = jnp.concatenate([block[:rows, cols] for block in blocks], axis=0)
        values = jnp.concatenate([block[:rows, vcols] for block in blocks], axis=0)
        contract = (((1,), (1,)), ((), ()))
        s_pre = lax.dot_general(queries, prefix[:, cols], contract, preferred_element_type=F32)
        s_suf = lax.dot_general(queries, keys, contract, preferred_element_type=F32) + bias
        top = jnp.maximum(jnp.max(s_pre, axis=-1, keepdims=True), jnp.max(s_suf, axis=-1, keepdims=True))
        p_pre, p_suf = jnp.exp(s_pre - top), jnp.exp(s_suf - top)
        total = jnp.sum(p_pre, axis=-1, keepdims=True) + jnp.sum(p_suf, axis=-1, keepdims=True)
        numerator = jnp.dot(p_pre.astype(BF16), prefix[:, vcols], preferred_element_type=F32)
        numerator += jnp.dot(p_suf.astype(BF16), values, preferred_element_type=F32)
        context = (numerator / total).astype(BF16)
        for r in range(REPEATS):
            out[:, base + r * HD:base + (r + 1) * HD] = context[r * rows:(r + 1) * rows]


def attend(quarters, prefix, seg_col, blocks, scalars):
    rows = quarters[0].shape[0]
    earlier = len(blocks) - 1
    vmem = pl.BlockSpec(memory_space=pltpu.VMEM)
    keys = prefix.shape[0] + rows * (earlier + 1)
    return pl.pallas_call(
        functools.partial(attend_kernel, earlier),
        out_shape=jax.ShapeDtypeStruct((rows, QW), BF16),
        in_specs=[pl.BlockSpec(memory_space=pltpu.SMEM)] + [vmem] * (6 + len(blocks)),
        out_specs=vmem,
        scratch_shapes=[pltpu.VMEM((4, rows, QQ), BF16)],
        compiler_params=pltpu.CompilerParams(vmem_limit_bytes=40 << 20),
        cost_estimate=pl.CostEstimate(
            flops=4 * rows * keys * QW, bytes_accessed=4 * keys * KVW, transcendentals=rows * keys * QW // HD
        ),
    )(scalars, *quarters, prefix, seg_col, *blocks)


def swap_body(tokens, norm_gain, w_qkv, prefix_kv, segments):
    inputs, seg_ids, own_prefix = tokens[0], segments[0], prefix_kv[0]
    rows = inputs.shape[0]
    gx, core, z, y = (lax.axis_index(a) for a in ("gx", "core", "z", "y"))
    z_count, y_count = lax.axis_size("z"), lax.axis_size("y")
    index = z * y_count + y
    depth = w_qkv.shape[0]

    def half(of):
        keys = lax.dynamic_slice_in_dim(w_qkv, QW + of * KVW, KVW, 1)
        return jnp.concatenate([lax.dynamic_slice_in_dim(w_qkv, of * QH, QH, 1), keys], axis=1)

    kept, got = half(core), swap(half(1 - core), "core")
    kv_near = jnp.concatenate([kept[:, QH:], got[:, QH:]])
    kv_zs = [z_swap(kv_near, d) for d in (1, 2, 3)]
    kv_near_sides = sides(kv_near)

    pair = z & 1
    kept, got, own_prefix = after(kv_near_sides, kept, got, own_prefix)
    q_rows = jnp.concatenate([kept[:, :QH], got[:, :QH]])
    q_send = lax.dynamic_slice_in_dim(q_rows, (1 - pair) * QQ, QQ, 1)
    q_send = jnp.concatenate([jnp.concatenate([q_send[:depth], q_send[depth:]], axis=1), own_prefix])
    q_got = z_swap(q_send, 1)
    q_keep = lax.dynamic_slice_in_dim(q_rows, pair * QQ, QQ, 1)
    q_got_rows = jnp.concatenate([q_got[:depth, :QQ], q_got[:depth, QQ:]])
    q_near = jnp.concatenate([q_keep, q_got_rows], axis=1)

    kv_far = jnp.concatenate(after(q_got, *kv_zs))
    kv_far_sides = sides(kv_far)

    (normed_in,) = after(kv_near, inputs)
    normed = rms_norm(normed_in, norm_gain)
    normed_sibling = swap(normed, "core")
    number = ((gx * 2 + core) * z_count + z) * y_count + y
    bits = jnp.stack([(number >> i) & 1 for i in range(5)]).astype(jnp.int32)
    kv_order = piece_order([(0, 0), (1, 0)], [(half, dz) for dz in (1, 2, 3) for half in (0, 1)])
    kv_features = order_features([normed, normed_sibling], [b for piece in kv_order for b in piece], bits)

    (q_load,) = after(kv_far, jnp.concatenate([q_near, own_prefix, q_got[depth:]]))
    q_across = z_swap(q_load, 2)
    (normed_out,) = after(kv_far_sides, normed)
    normed_pair = z_swap(normed_out, 1)

    kv_corner = corner(kv_near_sides, after(kv_features, *kv_far_sides))
    kv_pieces = [kv_near, *kv_near_sides, kv_far, *kv_far_sides, *kv_corner]
    kv_mine, kv_theirs = project(kv_features, kv_pieces, 1, 2, None, 2)
    kv_other = swap(kv_theirs, "core")
    q_line = jnp.concatenate([q_near, *after(kv_theirs, q_across[:2 * depth])])
    q_line_x, q_line_y = sides(q_line)
    low = core == 0
    seg_row = jnp.pad(seg_ids.astype(BF16)[None, :], ((0, 7), (0, 2 * KVW - rows)))
    block = jnp.concatenate(
        [
            jnp.concatenate([jnp.where(low, kv_mine, kv_other), jnp.where(low, kv_other, kv_mine)], axis=1),
            seg_row,
        ],
        axis=0,
    )
    upward = [(i, i + 1) for i in range(z_count - 1)]
    two_back = lax.ppermute(block, "z", upward)
    four_back = lax.ppermute(two_back, "z", upward)
    odd_a = swap(two_back, "y")
    odd_b = swap(jnp.where(y == 0, block, four_back), "y")
    blocks = [block, two_back, four_back, odd_a, odd_b]
    distances = [0, 2, 4, 1 + 2 * y, 3 - 2 * y]

    q_late_x, q_late_y = after(two_back, q_line_x[:2 * depth], q_line_y[2 * depth:])
    q_low, q_high = swap(q_late_x, "y"), swap(q_late_y, "gx")
    q_pieces = [q_line, q_line_x, q_line_y, q_low, q_high]
    q_order = []
    for dx, dy, spans in ((0, 0, (0, 2)), (1, 0, (0, 2)), (0, 1, (0, 2)), (1, 1, (0,)), (1, 1, (2,))):
        for pair_bit in (0, 1):
            q_order += [((dx * 2 + half) * 4 + (far ^ pair_bit)) * 2 + dy for far in spans for half in (0, 1)]
    (normed_pair,) = after(block, normed_pair)
    normed_diagonal = swap(normed_pair, "core")
    q_features = order_features([normed, normed_sibling, normed_pair, normed_diagonal], q_order, bits)
    q_mine, q_sibling, q_pair, q_diagonal = project(q_features, q_pieces, 2, 4, 0.125, 2)
    own_got, sibling_got = jnp.split(z_swap(jnp.concatenate([q_pair, q_diagonal]), 1), 2)
    from_sibling = swap(jnp.concatenate([q_sibling, sibling_got]), "core")
    quarters = [q_mine, own_got, *jnp.split(from_sibling, 2)]

    line = jnp.concatenate([own_prefix, q_got[depth:], q_across[2 * depth:]])
    prefix = jnp.concatenate([line, swap(line, "y")])

    scalars = jnp.stack([core * 2 + pair] + [jnp.where(index >= d, 0, 1) for d in distances]).astype(jnp.int32)
    context = attend(quarters, prefix, seg_ids.astype(F32)[:, None], blocks, scalars)
    return context[None]


def gather_body(tokens, norm_gain, w_qkv, prefix_kv, segments):
    inputs, seg_ids = tokens[0], segments[0]
    rows = inputs.shape[0]
    normed = rms_norm(inputs, norm_gain)
    weights = lax.all_gather(w_qkv, ("gx", "core", "z", "y"), axis=0, tiled=True)
    projected = jnp.dot(normed, weights, preferred_element_type=F32).astype(BF16)
    queries = projected[:, :QW].reshape(rows, KEY_HEADS, REPEATS, HD)

    def absorb(state, keyvals, visible):
        running_max, denominator, numerator = state
        count = keyvals.shape[0]
        key_part = keyvals[:, :KVW].reshape(count, KEY_HEADS, HD)
        value_part = keyvals[:, KVW:].reshape(count, KEY_HEADS, HD)
        scores = jnp.einsum("tgrd,ngd->tgrn", queries, key_part, preferred_element_type=F32) * 0.125
        if visible is not None:
            scores = jnp.where(visible[:, None, None, :], scores, F32(NEG))
        new_max = jnp.maximum(running_max, jnp.max(scores, axis=-1))
        probability = jnp.exp(scores - new_max[..., None])
        if visible is not None:
            probability = jnp.where(visible[:, None, None, :], probability, F32(0.0))
        factor = jnp.exp(running_max - new_max)
        denominator = denominator * factor + jnp.sum(probability, axis=-1)
        numerator = numerator * factor[..., None] + jnp.einsum(
            "tgrn,ngd->tgrd", probability.astype(BF16), value_part, preferred_element_type=F32
        )
        return new_max, denominator, numerator

    def sweep(state, keyvals, key_seg):
        length = min(keyvals.shape[0], 512)

        def step(i, running):
            start = i * length
            part = lax.dynamic_slice_in_dim(keyvals, start, length, 0)
            if key_seg is None:
                return absorb(running, part, None)
            seg_part = lax.dynamic_slice_in_dim(key_seg, start, length, 0)
            key_pos = start + jnp.arange(length, dtype=jnp.int32)
            visible = (seg_part[None, :] == seg_ids[:, None]) & (key_pos[None, :] <= query_pos[:, None])
            return absorb(running, part, visible)

        return lax.fori_loop(0, keyvals.shape[0] // length, step, state)

    query_pos = lax.axis_index(("z", "y")) * rows + jnp.arange(rows, dtype=jnp.int32)
    state = (
        jnp.full((rows, KEY_HEADS, REPEATS), NEG, F32),
        jnp.zeros((rows, KEY_HEADS, REPEATS), F32),
        jnp.zeros((rows, KEY_HEADS, REPEATS, HD), F32),
    )
    along = functools.partial(lax.all_gather, axis_name=("z", "y"), axis=0, tiled=True)
    state = sweep(state, along(prefix_kv[0]), None)
    _, denominator, numerator = sweep(state, along(projected[:, QW:]), along(seg_ids))
    return (numerator / denominator[..., None]).reshape(rows, QW).astype(BF16)[None]


def solution(mesh):
    groups, seqs = mesh.shape["group"], mesh.shape["seq"]
    chips, z_count = groups // 2, seqs // 2
    fine = Mesh(mesh.devices.reshape(chips, 2, z_count, 2), ("gx", "core", "z", "y"))
    group, seq = ("gx", "core"), ("z", "y")
    short = chips == 2 and z_count == SMALL
    return jax.shard_map(
        swap_body if short else gather_body,
        mesh=fine,
        in_specs=(P(group, seq, None), P(), P(group + seq, None), P(group, seq, None), P(group, seq)),
        out_specs=P(group, seq, None),
        check_vma=False,
    )
```

time: 112 us -> 86.1 us (0.77)
  the two profiles are of different devices: /device:TPU:30 before, /device:TPU:0 now
where the time goes in v2:
time: 86.1 us; the launch traced here: 85.5 us
  waiting for transfers between devices  34.8 us (40%)
  starting transfers between devices  33.3 us (39%)
  Pallas kernels  12.3 us (14%)
  local copies, waits for them, and re-layouts  2.61 us (3%)
  other arithmetic  2.03 us (2%)
    ppermute x18, starting transfers between devices, swap(): return lax.ppermute(x, axis, [(0, 1), (1, 0)])  15.9 us
    ppermute x7, waiting for transfers between devices, z_swap(): return lax.ppermute(x, 'z', [(i, i ^ distance) for i in range(4)])  15.8 us
    ppermute x18, waiting for transfers between devices, swap(): return lax.ppermute(x, axis, [(0, 1), (1, 0)])  15 us
    ppermute x7, starting transfers between devices, z_swap(): return lax.ppermute(x, 'z', [(i, i ^ distance) for i in range(4)])  11 us
    pallas_call x1, Pallas kernels, attend(): pl.pallas_call(functools.partial(attend_kernel, earlier), out_shape=jax.S...  6.3 us
    ppermute x1, starting transfers between devices, swap_body(): four_back = lax.ppermute(two_back, 'z', upward)  5.07 us
    pallas_call x2, Pallas kernels, order_features(): pl.pallas_call(functools.partial(order_kernel, order), out_shape=jax.Shap...  3.4 us
    ppermute x1, waiting for transfers between devices, swap_body(): two_back = lax.ppermute(block, 'z', upward)  2.18 us
  transfers between devices with their start and end apart: 27, of which 15 were waited for; matrix products, arithmetic and copies ran while one was open for 3% of the time, Pallas kernels for 7%

profile of v2, /device:TPU:0, one launch (start us, length us, event | category | flops | bytes accessed | tf_op | source)
XLA Modules:
  0.0 85.5 jit_solution(12533627385962103070)
XLA Ops:
  3.6 2.9 %collective-permute-start.2 = (bf16[128,320]{1,0:T(8,128)(2,1)S(1)}, bf16[128,320]{1,0:T(8,128)(2,1)S(1)}, u32[]{:S(2)}, u32[]{:S(2)}) collective-permute-start(bf16[128,320]{1,0:T(8,128)(2,1)S(1)} %pad_maximum_fusion.11.refs_0_), channel_id=1, source_target_pairs={{0,16},{16,0},{1,17},{17,1},{2,18},{18,2},{3,19},{19,3},{4,20},{20... | collective-permute-start | bytes 245768 | tf_op jit(solution)/shard_map/ppermute | solution.py:29
  6.5 1.5 %collective-permute-start.3 = (bf16[128,320]{1,0:T(8,128)(2,1)S(1)}, bf16[128,320]{1,0:T(8,128)(2,1)S(1)}, u32[]{:S(2)}, u32[]{:S(2)}) collective-permute-start(bf16[128,320]{1,0:T(8,128)(2,1)S(1)} %pad_maximum_fusion.11.refs_0_), channel_id=1, source_target_pairs={{0,1},{1,0},{2,3},{3,2},{4,5},{5,4},{6,7},{7,6},{8,9},{9,8},{10,11... | collective-permute-start | bytes 245768 | tf_op jit(solution)/shard_map/ppermute | solution.py:29
  8.0 1.6 %collective-permute-start.5 = (bf16[128,320]{1,0:T(8,128)(2,1)S(1)}, bf16[128,320]{1,0:T(8,128)(2,1)S(1)}, u32[]{:S(2)}, u32[]{:S(2)}) collective-permute-start(bf16[128,320]{1,0:T(8,128)(2,1)S(1)} %pad_maximum_fusion.11.refs_0_), channel_id=1, source_target_pairs={{0,2},{2,0},{4,6},{6,4},{1,3},{3,1},{5,7},{7,5},{8,10},{10,8},{12,... | collective-permute-start | bytes 245768 | tf_op jit(solution)/shard_map/ppermute | solution.py:33
  9.6 2.6 %collective-permute-start.6 = (bf16[128,320]{1,0:T(8,128)(2,1)S(1)}, bf16[128,320]{1,0:T(8,128)(2,1)S(1)}, u32[]{:S(2)}, u32[]{:S(2)}) collective-permute-start(bf16[128,320]{1,0:T(8,128)(2,1)S(1)} %pad_maximum_fusion.11.refs_0_), channel_id=1, source_target_pairs={{0,4},{2,6},{4,0},{6,2},{1,5},{3,7},{5,1},{7,3},{8,12},{10,14},{12... | collective-permute-start | bytes 245768 | tf_op jit(solution)/shard_map/ppermute | solution.py:33
  14.0 5.7 %collective-permute-done.6 = bf16[128,320]{1,0:T(8,128)(2,1)S(1)} collective-permute-done((bf16[128,320]{1,0:T(8,128)(2,1)S(1)}, bf16[128,320]{1,0:T(8,128)(2,1)S(1)}, u32[]{:S(2)}, u32[]{:S(2)}) %collective-permute-start.6) | collective-permute-done | bytes 81952 | tf_op jit(solution)/shard_map/ppermute | solution.py:33
  22.4 1.6 %collective-permute-start.15 = (bf16[256,640]{1,0:T(8,128)(2,1)S(1)}, bf16[256,640]{1,0:T(8,128)(2,1)S(1)}, u32[]{:S(2)}, u32[]{:S(2)}) collective-permute-start(bf16[256,640]{1,0:T(8,128)(2,1)S(1)} %pad_maximum_fusion.1), channel_id=1, source_target_pairs={{0,4},{2,6},{4,0},{6,2},{1,5},{3,7},{5,1},{7,3},{8,12},{10,14},{12... | collective-permute-start | bytes 983048 | tf_op jit(solution)/shard_map/ppermute | solution.py:33
  24.2 4.2 %collective-permute-done.8.refs_4_ = bf16[384,320]{1,0:T(8,128)(2,1)S(1)} collective-permute-done((bf16[384,320]{1,0:T(8,128)(2,1)S(1)}, bf16[384,320]{1,0:T(8,128)(2,1)S(1)}, u32[]{:S(2)}, u32[]{:S(2)}) %collective-permute-start.8) | collective-permute-done | bytes 245792 | tf_op jit(solution)/shard_map/ppermute | solution.py:29
  29.7 1.3 %shard_map.55.features = bf16[256,2048]{1,0:T(8,128)(2,1)S(1)} custom-call(s32[5]{0:T(128)S(1)} %stack.51.bits, bf16[128,2048]{1,0:T(8,128)(2,1)S(1)} %fusion.2.refs_0_, bf16[128,2048]{1,0:T(8,128)(2,1)S(1)} %collective-permute-done.1.refs_1_), custom_call_target="tpu_custom_call" | custom-call | bytes 2097152 | tf_op jit(solution)/shard_map/pallas_call | solution.py:66
  31.7 1.6 %collective-permute-start.11 = (bf16[256,320]{1,0:T(8,128)(2,1)S(1)}, bf16[256,320]{1,0:T(8,128)(2,1)S(1)}, u32[]{:S(2)}, u32[]{:S(2)}) collective-permute-start(bf16[256,320]{1,0:T(8,128)(2,1)S(1)} %pad_maximum_fusion.5), channel_id=1, source_target_pairs={{0,16},{16,0},{1,17},{17,1},{2,18},{18,2},{3,19},{19,3},{4,20},{20... | collective-permute-start | bytes 491528 | tf_op jit(solution)/shard_map/ppermute | solution.py:29
  34.0 4.3 %collective-permute-done.15 = bf16[256,640]{1,0:T(8,128)(2,1)S(1)} collective-permute-done((bf16[256,640]{1,0:T(8,128)(2,1)S(1)}, bf16[256,640]{1,0:T(8,128)(2,1)S(1)}, u32[]{:S(2)}, u32[]{:S(2)}) %collective-permute-start.15) | collective-permute-done | bytes 327712 | tf_op jit(solution)/shard_map/ppermute | solution.py:33
  39.9 1.5 %collective-permute-start.17 = (bf16[256,640]{1,0:T(8,128)(2,1)S(1)}, bf16[256,640]{1,0:T(8,128)(2,1)S(1)}, u32[]{:S(2)}, u32[]{:S(2)}) collective-permute-start(bf16[256,640]{1,0:T(8,128)(2,1)S(1)} %pad_maximum_fusion.2.refs_0_), channel_id=1, source_target_pairs={{0,1},{1,0},{2,3},{3,2},{4,5},{5,4},{6,7},{7,6},{8,9},{9,8},{10,11... | collective-permute-start | bytes 983048 | tf_op jit(solution)/shard_map/ppermute | solution.py:29
  41.5 4.5 %collective-permute-done.13.refs_2_ = bf16[128,2048]{1,0:T(8,128)(2,1)S(1)} collective-permute-done((bf16[128,2048]{1,0:T(8,128)(2,1)S(1)}, bf16[128,2048]{1,0:T(8,128)(2,1)S(1)}, u32[]{:S(2)}, u32[]{:S(2)}) %collective-permute-start.13) | collective-permute-done | bytes 524320 | tf_op jit(solution)/shard_map/ppermute | solution.py:33
  46.0 1.4 %collective-permute-start.18 = (bf16[136,640]{1,0:T(8,128)(2,1)S(1)}, bf16[136,640]{1,0:T(8,128)(2,1)S(1)}, u32[]{:S(2)}, u32[]{:S(2)}) collective-permute-start(bf16[136,640]{1,0:T(8,128)(2,1)S(1)} %fusion.4.refs_0_), channel_id=1, source_target_pairs={{0,2},{2,4},{4,6},{1,3},{3,5},{5,7},{8,10},{10,12},{12,14},{9,11},... | collective-permute-start | bytes 522248 | tf_op jit(solution)/shard_map/ppermute | solution.py:259
  47.5 1.5 %collective-permute-done.16.refs_1_ = bf16[256,640]{1,0:T(8,128)(2,1)S(1)} collective-permute-done((bf16[256,640]{1,0:T(8,128)(2,1)S(1)}, bf16[256,640]{1,0:T(8,128)(2,1)S(1)}, u32[]{:S(2)}, u32[]{:S(2)}) %collective-permute-start.16) | collective-permute-done | bytes 327712 | tf_op jit(solution)/shard_map/ppermute | solution.py:29
  49.7 2.2 %collective-permute-done.18.refs_1_ = bf16[136,640]{1,0:T(8,128)(2,1)S(1)} collective-permute-done((bf16[136,640]{1,0:T(8,128)(2,1)S(1)}, bf16[136,640]{1,0:T(8,128)(2,1)S(1)}, u32[]{:S(2)}, u32[]{:S(2)}) %collective-permute-start.18) | collective-permute-done | bytes 174112 | tf_op jit(solution)/shard_map/ppermute | solution.py:259
  53.5 1.6 %collective-permute-start.23 = (bf16[256,640]{1,0:T(8,128)(2,1)S(1)}, bf16[256,640]{1,0:T(8,128)(2,1)S(1)}, u32[]{:S(2)}, u32[]{:S(2)}) collective-permute-start(bf16[256,640]{1,0:T(8,128)(2,1)S(1)} %pad_maximum_fusion.3), channel_id=1, source_target_pairs={{0,1},{1,0},{2,3},{3,2},{4,5},{5,4},{6,7},{7,6},{8,9},{9,8},{10,11... | collective-permute-start | bytes 983048 | tf_op jit(solution)/shard_map/ppermute | solution.py:29
  55.1 2.1 %shard_map.58.features = bf16[512,2048]{1,0:T(8,128)(2,1)S(1)} custom-call(s32[5]{0:T(128)S(1)} %stack.51.bits, bf16[128,2048]{1,0:T(8,128)(2,1)S(1)} %fusion.2.refs_0_, bf16[128,2048]{1,0:T(8,128)(2,1)S(1)} %collective-permute-done.1.refs_1_, bf16[128,2048]{1,0:T(8,128)(2,1)S(1)} %collective-permute-done.13.refs_2_, ...), custom_call_target="tpu_custom_call" | custom-call | bytes 4194304 | tf_op jit(solution)/shard_map/pallas_call | solution.py:66
  59.7 3.1 %collective-permute-start.21 = (bf16[256,320]{1,0:T(8,128)(2,1)S(1)}, bf16[256,320]{1,0:T(8,128)(2,1)S(1)}, u32[]{:S(2)}, u32[]{:S(2)}) collective-permute-start(bf16[256,320]{1,0:T(8,128)(2,1)S(1)} %pad_maximum_fusion.6), channel_id=1, source_target_pairs={{0,2},{2,0},{4,6},{6,4},{1,3},{3,1},{5,7},{7,5},{8,10},{10,8},{12,... | collective-permute-start | bytes 491528 | tf_op jit(solution)/shard_map/ppermute | solution.py:33
  63.0 1.8 %collective-permute-done.23 = bf16[256,640]{1,0:T(8,128)(2,1)S(1)} collective-permute-done((bf16[256,640]{1,0:T(8,128)(2,1)S(1)}, bf16[256,640]{1,0:T(8,128)(2,1)S(1)}, u32[]{:S(2)}, u32[]{:S(2)}) %collective-permute-start.23) | collective-permute-done | bytes 327712 | tf_op jit(solution)/shard_map/ppermute | solution.py:29
  64.9 5.1 %collective-permute-start.24 = (bf16[136,640]{1,0:T(8,128)(2,1)S(1)}, bf16[136,640]{1,0:T(8,128)(2,1)S(1)}, u32[]{:S(2)}, u32[]{:S(2)}) collective-permute-start(bf16[136,640]{1,0:T(8,128)(2,1)S(1)} %collective-permute-done.18.refs_1_), channel_id=1, source_target_pairs={{0,2},{2,4},{4,6},{1,3},{3,5},{5,7},{8,10},{10,12},{12,14},{9,11},... | collective-permute-start | bytes 522248 | tf_op jit(solution)/shard_map/ppermute | solution.py:260
  70.9 1.7 %collective-permute-done.24.refs_2_ = bf16[136,640]{1,0:T(8,128)(2,1)S(1)} collective-permute-done((bf16[136,640]{1,0:T(8,128)(2,1)S(1)}, bf16[136,640]{1,0:T(8,128)(2,1)S(1)}, u32[]{:S(2)}, u32[]{:S(2)}) %collective-permute-start.24) | collective-permute-done | bytes 174112 | tf_op jit(solution)/shard_map/ppermute | solution.py:260
  73.7 3.1 %collective-permute-done.25.refs_3_ = bf16[136,640]{1,0:T(8,128)(2,1)S(1)} collective-permute-done((bf16[136,640]{1,0:T(8,128)(2,1)S(1)}, bf16[136,640]{1,0:T(8,128)(2,1)S(1)}, u32[]{:S(2)}, u32[]{:S(2)}) %collective-permute-start.25) | collective-permute-done | bytes 174112 | tf_op jit(solution)/shard_map/ppermute | solution.py:29
  76.7 2.4 %collective-permute-done.26.refs_4_ = bf16[136,640]{1,0:T(8,128)(2,1)S(1)} collective-permute-done((bf16[136,640]{1,0:T(8,128)(2,1)S(1)}, bf16[136,640]{1,0:T(8,128)(2,1)S(1)}, u32[]{:S(2)}, u32[]{:S(2)}) %collective-permute-start.26) | collective-permute-done | bytes 174112 | tf_op jit(solution)/shard_map/ppermute | solution.py:29
  79.2 6.3 %shard_map.61 = bf16[128,1280]{1,0:T(8,128)(2,1)} custom-call(s32[6]{0:T(128)S(1)} %stack.45.scalars, bf16[128,320]{1,0:T(8,128)(2,1)S(1)} %get-tuple-element.43.mine, bf16[128,320]{1,0:T(8,128)(2,1)S(1)} %get-tuple-element.56.pair, bf16[128,320]{1,0:T(8,128)(2,1)S(1)} %get-tuple-element.54.sibling, bf16[128,320]{1,0:T(8,128)(2,1)S(1)} %get-tuple-element.53.diagonal, ...), custom_call_target="tpu_custom_call" | custom-call | flops 754974720 | bytes 1474560 | tf_op jit(solution)/shard_map/pallas_call | solution.py:187
  (97 shorter events, 19.5 us)
Async XLA Ops:
  3.6 9.0 %collective-permute-start.2 = (bf16[128,320]{1,0:T(8,128)(2,1)S(1)}, bf16[128,320]{1,0:T(8,128)(2,1)S(1)}, u32[]{:S(2)}, u32[]{:S(2)}) collective-permute-start(bf16[128,320]{1,0:T(8,128)(2,1)S(1)} %pad_maximum_fusion.11.refs_0_), channel_id=1, source_target_pairs={{0,16},{16,0},{1,17},{17,1},{2,18},{18,2},{3,19},{19,3},{4,20},{20... | collective-permute-start | bytes 245768 | tf_op jit(solution)/shard_map/ppermute | solution.py:29
  6.5 6.1 %collective-permute-start.3 = (bf16[128,320]{1,0:T(8,128)(2,1)S(1)}, bf16[128,320]{1,0:T(8,128)(2,1)S(1)}, u32[]{:S(2)}, u32[]{:S(2)}) collective-permute-start(bf16[128,320]{1,0:T(8,128)(2,1)S(1)} %pad_maximum_fusion.11.refs_0_), channel_id=1, source_target_pairs={{0,1},{1,0},{2,3},{3,2},{4,5},{5,4},{6,7},{7,6},{8,9},{9,8},{10,11... | collective-permute-start | bytes 245768 | tf_op jit(solution)/shard_map/ppermute | solution.py:29
  8.0 6.0 %collective-permute-start.5 = (bf16[128,320]{1,0:T(8,128)(2,1)S(1)}, bf16[128,320]{1,0:T(8,128)(2,1)S(1)}, u32[]{:S(2)}, u32[]{:S(2)}) collective-permute-start(bf16[128,320]{1,0:T(8,128)(2,1)S(1)} %pad_maximum_fusion.11.refs_0_), channel_id=1, source_target_pairs={{0,2},{2,0},{4,6},{6,4},{1,3},{3,1},{5,7},{7,5},{8,10},{10,8},{12,... | collective-permute-start | bytes 245768 | tf_op jit(solution)/shard_map/ppermute | solution.py:33
  9.6 10.2 %collective-permute-start.6 = (bf16[128,320]{1,0:T(8,128)(2,1)S(1)}, bf16[128,320]{1,0:T(8,128)(2,1)S(1)}, u32[]{:S(2)}, u32[]{:S(2)}) collective-permute-start(bf16[128,320]{1,0:T(8,128)(2,1)S(1)} %pad_maximum_fusion.11.refs_0_), channel_id=1, source_target_pairs={{0,4},{2,6},{4,0},{6,2},{1,5},{3,7},{5,1},{7,3},{8,12},{10,14},{12... | collective-permute-start | bytes 245768 | tf_op jit(solution)/shard_map/ppermute | solution.py:33
  12.1 7.6 %collective-permute-start.7 = (bf16[128,320]{1,0:T(8,128)(2,1)S(1)}, bf16[128,320]{1,0:T(8,128)(2,1)S(1)}, u32[]{:S(2)}, u32[]{:S(2)}) collective-permute-start(bf16[128,320]{1,0:T(8,128)(2,1)S(1)} %pad_maximum_fusion.11.refs_0_), channel_id=1, source_target_pairs={{0,6},{2,4},{4,2},{6,0},{1,7},{3,5},{5,3},{7,1},{8,14},{10,12},{12... | collective-permute-start | bytes 245768 | tf_op jit(solution)/shard_map/ppermute | solution.py:33
  13.0 8.1 %collective-permute-start.4 = (bf16[128,640]{1,0:T(8,128)(2,1)S(1)}, bf16[128,640]{1,0:T(8,128)(2,1)S(1)}, u32[]{:S(2)}, u32[]{:S(2)}) collective-permute-start(bf16[128,640]{1,0:T(8,128)(2,1)S(1)} %pad_maximum_fusion.8), channel_id=1, source_target_pairs={{0,2},{2,0},{4,6},{6,4},{1,3},{3,1},{5,7},{7,5},{8,10},{10,8},{12,... | collective-permute-start | bytes 491528 | tf_op jit(solution)/shard_map/ppermute | solution.py:33
  13.9 15.8 %collective-permute-start.1 = (bf16[128,2048]{1,0:T(8,128)(2,1)S(1)}, bf16[128,2048]{1,0:T(8,128)(2,1)S(1)}, u32[]{:S(2)}, u32[]{:S(2)}) collective-permute-start(bf16[128,2048]{1,0:T(8,128)(2,1)S(1)} %fusion.2.refs_0_), channel_id=1, source_target_pairs={{0,8},{8,0},{1,9},{9,1},{2,10},{10,2},{3,11},{11,3},{4,12},{12,4},... | collective-permute-start | bytes 1572872 | tf_op jit(solution)/shard_map/ppermute | solution.py:29
  21.1 7.2 %collective-permute-start.8 = (bf16[384,320]{1,0:T(8,128)(2,1)S(1)}, bf16[384,320]{1,0:T(8,128)(2,1)S(1)}, u32[]{:S(2)}, u32[]{:S(2)}) collective-permute-start(bf16[384,320]{1,0:T(8,128)(2,1)S(1)} %constant_dynamic-update-slice_fusion.refs_3_), channel_id=1, source_target_pairs={{0,16},{16,0},{1,17},{17,1},{2,18},{18,2},{3,19},{19,3},{4,20},{20... | collective-permute-start | bytes 737288 | tf_op jit(solution)/shard_map/ppermute | solution.py:29
  21.7 6.9 %collective-permute-start.9 = (bf16[384,320]{1,0:T(8,128)(2,1)S(1)}, bf16[384,320]{1,0:T(8,128)(2,1)S(1)}, u32[]{:S(2)}, u32[]{:S(2)}) collective-permute-start(bf16[384,320]{1,0:T(8,128)(2,1)S(1)} %constant_dynamic-update-slice_fusion.refs_3_), channel_id=1, source_target_pairs={{0,1},{1,0},{2,3},{3,2},{4,5},{5,4},{6,7},{7,6},{8,9},{9,8},{10,11... | collective-permute-start | bytes 737288 | tf_op jit(solution)/shard_map/ppermute | solution.py:29
  22.4 15.8 %collective-permute-start.15 = (bf16[256,640]{1,0:T(8,128)(2,1)S(1)}, bf16[256,640]{1,0:T(8,128)(2,1)S(1)}, u32[]{:S(2)}, u32[]{:S(2)}) collective-permute-start(bf16[256,640]{1,0:T(8,128)(2,1)S(1)} %pad_maximum_fusion.1), channel_id=1, source_target_pairs={{0,4},{2,6},{4,0},{6,2},{1,5},{3,7},{5,1},{7,3},{8,12},{10,14},{12... | collective-permute-start | bytes 983048 | tf_op jit(solution)/shard_map/ppermute | solution.py:33
  28.6 17.4 %collective-permute-start.13 = (bf16[128,2048]{1,0:T(8,128)(2,1)S(1)}, bf16[128,2048]{1,0:T(8,128)(2,1)S(1)}, u32[]{:S(2)}, u32[]{:S(2)}) collective-permute-start(bf16[128,2048]{1,0:T(8,128)(2,1)S(1)} %fusion.2.refs_0_), channel_id=1, source_target_pairs={{0,2},{2,0},{4,6},{6,4},{1,3},{3,1},{5,7},{7,5},{8,10},{10,8},{12,... | collective-permute-start | bytes 1572872 | tf_op jit(solution)/shard_map/ppermute | solution.py:33
  31.1 7.2 %collective-permute-start.10 = (bf16[256,320]{1,0:T(8,128)(2,1)S(1)}, bf16[256,320]{1,0:T(8,128)(2,1)S(1)}, u32[]{:S(2)}, u32[]{:S(2)}) collective-permute-start(bf16[256,320]{1,0:T(8,128)(2,1)S(1)} %pad_maximum_fusion.4), channel_id=1, source_target_pairs={{0,1},{1,0},{2,3},{3,2},{4,5},{5,4},{6,7},{7,6},{8,9},{9,8},{10,11... | collective-permute-start | bytes 491528 | tf_op jit(solution)/shard_map/ppermute | solution.py:29
  31.7 6.5 %collective-permute-start.11 = (bf16[256,320]{1,0:T(8,128)(2,1)S(1)}, bf16[256,320]{1,0:T(8,128)(2,1)S(1)}, u32[]{:S(2)}, u32[]{:S(2)}) collective-permute-start(bf16[256,320]{1,0:T(8,128)(2,1)S(1)} %pad_maximum_fusion.5), channel_id=1, source_target_pairs={{0,16},{16,0},{1,17},{17,1},{2,18},{18,2},{3,19},{19,3},{4,20},{20... | collective-permute-start | bytes 491528 | tf_op jit(solution)/shard_map/ppermute | solution.py:29
  38.8 10.2 %collective-permute-start.16 = (bf16[256,640]{1,0:T(8,128)(2,1)S(1)}, bf16[256,640]{1,0:T(8,128)(2,1)S(1)}, u32[]{:S(2)}, u32[]{:S(2)}) collective-permute-start(bf16[256,640]{1,0:T(8,128)(2,1)S(1)} %pad_maximum_fusion.2.refs_0_), channel_id=1, source_target_pairs={{0,16},{16,0},{1,17},{17,1},{2,18},{18,2},{3,19},{19,3},{4,20},{20... | collective-permute-start | bytes 983048 | tf_op jit(solution)/shard_map/ppermute | solution.py:29
  39.9 9.8 %collective-permute-start.17 = (bf16[256,640]{1,0:T(8,128)(2,1)S(1)}, bf16[256,640]{1,0:T(8,128)(2,1)S(1)}, u32[]{:S(2)}, u32[]{:S(2)}) collective-permute-start(bf16[256,640]{1,0:T(8,128)(2,1)S(1)} %pad_maximum_fusion.2.refs_0_), channel_id=1, source_target_pairs={{0,1},{1,0},{2,3},{3,2},{4,5},{5,4},{6,7},{7,6},{8,9},{9,8},{10,11... | collective-permute-start | bytes 983048 | tf_op jit(solution)/shard_map/ppermute | solution.py:29
  46.0 9.1 %collective-permute-start.14 = (bf16[128,2048]{1,0:T(8,128)(2,1)S(1)}, bf16[128,2048]{1,0:T(8,128)(2,1)S(1)}, u32[]{:S(2)}, u32[]{:S(2)}) collective-permute-start(bf16[128,2048]{1,0:T(8,128)(2,1)S(1)} %collective-permute-done.13.refs_2_), channel_id=1, source_target_pairs={{0,8},{8,0},{1,9},{9,1},{2,10},{10,2},{3,11},{11,3},{4,12},{12,4},... | collective-permute-start | bytes 1572872 | tf_op jit(solution)/shard_map/ppermute | solution.py:29
  46.0 5.9 %collective-permute-start.18 = (bf16[136,640]{1,0:T(8,128)(2,1)S(1)}, bf16[136,640]{1,0:T(8,128)(2,1)S(1)}, u32[]{:S(2)}, u32[]{:S(2)}) collective-permute-start(bf16[136,640]{1,0:T(8,128)(2,1)S(1)} %fusion.4.refs_0_), channel_id=1, source_target_pairs={{0,2},{2,4},{4,6},{1,3},{3,5},{5,7},{8,10},{10,12},{12,14},{9,11},... | collective-permute-start | bytes 522248 | tf_op jit(solution)/shard_map/ppermute | solution.py:259
  51.9 7.1 %collective-permute-start.19 = (bf16[128,640]{1,0:T(8,128)(2,1)S(1)}, bf16[128,640]{1,0:T(8,128)(2,1)S(1)}, u32[]{:S(2)}, u32[]{:S(2)}) collective-permute-start(bf16[128,640]{1,0:T(8,128)(2,1)S(1)} %slice.74), channel_id=1, source_target_pairs={{0,1},{1,0},{2,3},{3,2},{4,5},{5,4},{6,7},{7,6},{8,9},{9,8},{10,11... | collective-permute-start | bytes 491528 | tf_op jit(solution)/shard_map/ppermute | solution.py:29
  52.8 6.2 %collective-permute-start.20 = (bf16[128,640]{1,0:T(8,128)(2,1)S(1)}, bf16[128,640]{1,0:T(8,128)(2,1)S(1)}, u32[]{:S(2)}, u32[]{:S(2)}) collective-permute-start(bf16[128,640]{1,0:T(8,128)(2,1)S(1)} %slice.75), channel_id=1, source_target_pairs={{0,16},{16,0},{1,17},{17,1},{2,18},{18,2},{3,19},{19,3},{4,20},{20... | collective-permute-start | bytes 491528 | tf_op jit(solution)/shard_map/ppermute | solution.py:29
  53.5 11.3 %collective-permute-start.23 = (bf16[256,640]{1,0:T(8,128)(2,1)S(1)}, bf16[256,640]{1,0:T(8,128)(2,1)S(1)}, u32[]{:S(2)}, u32[]{:S(2)}) collective-permute-start(bf16[256,640]{1,0:T(8,128)(2,1)S(1)} %pad_maximum_fusion.3), channel_id=1, source_target_pairs={{0,1},{1,0},{2,3},{3,2},{4,5},{5,4},{6,7},{7,6},{8,9},{9,8},{10,11... | collective-permute-start | bytes 983048 | tf_op jit(solution)/shard_map/ppermute | solution.py:29
  59.7 11.1 %collective-permute-start.21 = (bf16[256,320]{1,0:T(8,128)(2,1)S(1)}, bf16[256,320]{1,0:T(8,128)(2,1)S(1)}, u32[]{:S(2)}, u32[]{:S(2)}) collective-permute-start(bf16[256,320]{1,0:T(8,128)(2,1)S(1)} %pad_maximum_fusion.6), channel_id=1, source_target_pairs={{0,2},{2,0},{4,6},{6,4},{1,3},{3,1},{5,7},{7,5},{8,10},{10,8},{12,... | collective-permute-start | bytes 491528 | tf_op jit(solution)/shard_map/ppermute | solution.py:33
  64.9 7.8 %collective-permute-start.24 = (bf16[136,640]{1,0:T(8,128)(2,1)S(1)}, bf16[136,640]{1,0:T(8,128)(2,1)S(1)}, u32[]{:S(2)}, u32[]{:S(2)}) collective-permute-start(bf16[136,640]{1,0:T(8,128)(2,1)S(1)} %collective-permute-done.18.refs_1_), channel_id=1, source_target_pairs={{0,2},{2,4},{4,6},{1,3},{3,5},{5,7},{8,10},{10,12},{12,14},{9,11},... | collective-permute-start | bytes 522248 | tf_op jit(solution)/shard_map/ppermute | solution.py:260
  69.9 6.8 %collective-permute-start.25 = (bf16[136,640]{1,0:T(8,128)(2,1)S(1)}, bf16[136,640]{1,0:T(8,128)(2,1)S(1)}, u32[]{:S(2)}, u32[]{:S(2)}) collective-permute-start(bf16[136,640]{1,0:T(8,128)(2,1)S(1)} %collective-permute-done.18.refs_1_), channel_id=1, source_target_pairs={{0,1},{1,0},{2,3},{3,2},{4,5},{5,4},{6,7},{7,6},{8,9},{9,8},{10,11... | collective-permute-start | bytes 522248 | tf_op jit(solution)/shard_map/ppermute | solution.py:29
  72.8 6.4 %collective-permute-start.26 = (bf16[136,640]{1,0:T(8,128)(2,1)S(1)}, bf16[136,640]{1,0:T(8,128)(2,1)S(1)}, u32[]{:S(2)}, u32[]{:S(2)}) collective-permute-start(bf16[136,640]{1,0:T(8,128)(2,1)S(1)} %broadcast_select_fusion), channel_id=1, source_target_pairs={{0,1},{1,0},{2,3},{3,2},{4,5},{5,4},{6,7},{7,6},{8,9},{9,8},{10,11... | collective-permute-start | bytes 522248 | tf_op jit(solution)/shard_map/ppermute | solution.py:29
  (12 other events, 98.3 us)

commit v3 on v2

v3 whole, which is shorter than its diff:
```python
import functools

import jax
import jax.numpy as jnp
from jax import lax
from jax.experimental import pallas as pl
from jax.experimental.pallas import tpu as pltpu
from jax.sharding import Mesh, PartitionSpec as P

HD = 64
QW = 1280
KVW = 320
KEY_HEADS = KVW // HD
REPEATS = QW // KVW
QH = QW // 2
NEG = -1e30
SMALL = 4
PREFIX_WITH_Q = True
CORNER_BY_X = True
Z_ORDER = (1, 2, 3)
WEIGHT = (1, 1, 1, 1)
ORDER = {
    "kv_near_sides": ("kv_z0",),
    "kv_far": ("kv_near_sides", "kv_features", "q_got",),
    "norm": ("kv_near",),
    "q_across": ("kv_far",),
    "normed_pair": ("kv_near_sides",),
    "kv_corner": ("kv_features",),
    "q_line": ("kv_far_sides",),
    "q_res": ("four_back",),
    "prefix_z1": ("kv_far_sides",),
    "prefix_z2": ("q_across",),
    "q_corner": ("two_back",),
    "four_back": ("normed_pair", "prefix_z2",),
    "q_last": ("four_back", "prefix_y",),
    "odd_a": ("prefix_y",),
}
F32 = jnp.float32
BF16 = jnp.bfloat16


def rms_norm(inputs, norm_gain):
    values = inputs.astype(F32)
    mean_square = jnp.mean(values * values, axis=-1, keepdims=True)
    return (values * lax.rsqrt(mean_square + 1e-05) * norm_gain.astype(F32)).astype(BF16)


def swap(x, axis):
    return lax.ppermute(x, axis, [(0, 1), (1, 0)])


def z_swap(x, distance):
    return lax.ppermute(x, "z", [(i, i ^ distance) for i in range(4)])


def sides(piece):
    return swap(piece, "gx"), swap(piece, "y")


def order_kernel(order, bits, *refs):
    sources, out = refs[:-1], refs[-1]
    at = 0
    for source in sources:
        rows, depth = source.shape
        x = source[...]
        for bit in range((depth // 64).bit_length() - 1):
            span = 64 << bit
            parts = [x[:, (i ^ 1) * span:((i ^ 1) + 1) * span] for i in range(depth // span)]
            x = jnp.where(bits[bit] == 1, jnp.concatenate(parts, axis=1), x)
        out[at:at + rows, :] = jnp.concatenate([x[:, b * 64:(b + 1) * 64] for b in order], axis=1)
        at += rows


def order_features(sources, order, bits, weight):
    depth = sources[0].shape[1]
    rows = sum(x.shape[0] for x in sources)
    vmem = pl.BlockSpec(memory_space=pltpu.VMEM)
    return pl.pallas_call(
        functools.partial(order_kernel, order),
        out_shape=jax.ShapeDtypeStruct((rows, 64 * len(order)), BF16),
        in_specs=[pl.BlockSpec(memory_space=pltpu.SMEM)] + [vmem] * len(sources),
        out_specs=vmem,
        compiler_params=pltpu.CompilerParams(vmem_limit_bytes=24 << 20),
        cost_estimate=pl.CostEstimate(flops=0, bytes_accessed=weight * 4 * rows * depth, transcendentals=0),
    )(bits, *sources)


def add_products(total, features, at, pieces):
    for piece in pieces:
        rows = piece.shape[0]
        term = jnp.dot(features[:, at:at + rows], piece[...], preferred_element_type=F32)
        total = term if total is None else total + term
        at += rows
    return total


def first_kernel(features, *refs):
    pieces, out = refs[:-1], refs[-1]
    out[...] = add_products(None, features, 0, pieces)


def last_kernel(at, keep, features, so_far, *refs):
    pieces, (kept, sent) = refs[:-2], refs[-2:]
    total = add_products(so_far[...], features, at, pieces)
    rows = total.shape[0] // (2 * keep)
    for i in range(keep):
        kept[i * rows:(i + 1) * rows, :] = total[2 * i * rows:(2 * i + 1) * rows]
        sent[i * rows:(i + 1) * rows, :] = total[(2 * i + 1) * rows:(2 * i + 2) * rows]


def project(features, pieces, late, keep, weight):
    rows, depth = features.shape
    width = pieces[0].shape[1]
    vmem = pl.BlockSpec(memory_space=pltpu.VMEM)
    early = len(pieces) - late
    params = pltpu.CompilerParams(vmem_limit_bytes=24 << 20)
    done = sum(p.shape[0] for p in pieces[:early])

    def cost(deep):
        return pl.CostEstimate(flops=2 * rows * deep * width, bytes_accessed=2 * deep * (width + rows), transcendentals=0)

    so_far = pl.pallas_call(
        first_kernel,
        out_shape=jax.ShapeDtypeStruct((rows, width), F32),
        in_specs=[vmem] * (1 + early),
        out_specs=vmem,
        compiler_params=params,
        cost_estimate=cost(weight * done),
    )(features, *pieces[:early])
    return pl.pallas_call(
        functools.partial(last_kernel, done, keep),
        out_shape=[jax.ShapeDtypeStruct((rows // 2, width), F32)] * 2,
        in_specs=[vmem] * (2 + late),
        out_specs=[vmem, vmem],
        compiler_params=params,
        cost_estimate=cost(depth - done),
    )(features, so_far, *pieces[early:])


def after(first, *then):
    return lax.optimization_barrier((first,) + then)[1:]


def attend_kernel(earlier, scalars, mine, pair, prefix, seg_col, *refs):
    blocks, out, q_all = refs[:earlier + 1], refs[earlier + 1], refs[earlier + 2]
    half = scalars[0]
    rows = mine.shape[0]
    q_all[half] = mine[...]
    q_all[1 - half] = pair[...]
    biases = []
    q_seg = seg_col[...]
    for i, block in enumerate(blocks):
        k_seg = block[rows:rows + 1, :rows].astype(F32)
        seen = q_seg == k_seg
        if i == 0:
            q_at = lax.broadcasted_iota(jnp.int32, (rows, rows), 0)
            k_at = lax.broadcasted_iota(jnp.int32, (rows, rows), 1)
            seen = seen & (k_at <= q_at)
            biases.append(jnp.where(seen, 0.0, NEG))
        else:
            biases.append(jnp.where(seen, jnp.where(scalars[1 + i] == 0, 0.0, NEG), NEG))
    bias = jnp.concatenate(biases, axis=1)
    bias = jnp.concatenate([bias] * REPEATS, axis=0)
    for head in range(KEY_HEADS):
        cols, vcols = slice(head * HD, (head + 1) * HD), slice(KVW + head * HD, KVW + (head + 1) * HD)
        base = head * REPEATS * HD
        heads = [divmod(head * REPEATS + r, QH // HD) for r in range(REPEATS)]
        queries = jnp.concatenate([q_all[part, :, h * HD:(h + 1) * HD] for part, h in heads], axis=0)
        keys = jnp.concatenate([block[:rows, cols] for block in blocks], axis=0)
        values = jnp.concatenate([block[:rows, vcols] for block in blocks], axis=0)
        contract = (((1,), (1,)), ((), ()))
        s_pre = lax.dot_general(queries, prefix[:, cols], contract, preferred_element_type=F32)
        s_suf = lax.dot_general(queries, keys, contract, preferred_element_type=F32) + bias
        top = jnp.maximum(jnp.max(s_pre, axis=-1, keepdims=True), jnp.max(s_suf, axis=-1, keepdims=True))
        p_pre, p_suf = jnp.exp(s_pre - top), jnp.exp(s_suf - top)
        total = jnp.sum(p_pre, axis=-1, keepdims=True) + jnp.sum(p_suf, axis=-1, keepdims=True)
        numerator = jnp.dot(p_pre.astype(BF16), prefix[:, vcols], preferred_element_type=F32)
        numerator += jnp.dot(p_suf.astype(BF16), values, preferred_element_type=F32)
        context = (numerator / total).astype(BF16)
        for r in range(REPEATS):
            out[:, base + r * HD:base + (r + 1) * HD] = context[r * rows:(r + 1) * rows]


def attend(halves, prefix, seg_col, blocks, scalars):
    rows = halves[0].shape[0]
    earlier = len(blocks) - 1
    vmem = pl.BlockSpec(memory_space=pltpu.VMEM)
    keys = prefix.shape[0] + rows * (earlier + 1)
    return pl.pallas_call(
        functools.partial(attend_kernel, earlier),
        out_shape=jax.ShapeDtypeStruct((rows, QW), BF16),
        in_specs=[pl.BlockSpec(memory_space=pltpu.SMEM)] + [vmem] * (4 + len(blocks)),
        out_specs=vmem,
        scratch_shapes=[pltpu.VMEM((2, rows, QH), BF16)],
        compiler_params=pltpu.CompilerParams(vmem_limit_bytes=40 << 20),
        cost_estimate=pl.CostEstimate(
            flops=4 * rows * keys * QW, bytes_accessed=4 * keys * KVW, transcendentals=rows * keys * QW // HD
        ),
    )(scalars, *halves, prefix, seg_col, *blocks)


def swap_body(tokens, norm_gain, w_qkv, prefix_kv, segments):
    inputs, seg_ids, own_prefix = tokens[0], segments[0], prefix_kv[0]
    rows = inputs.shape[0]
    gx, core, z, y = (lax.axis_index(a) for a in ("gx", "core", "z", "y"))
    z_count, y_count = lax.axis_size("z"), lax.axis_size("y")
    index = z * y_count + y
    depth = w_qkv.shape[0]

    have = {}

    def gate(point, *values):
        names = [n for n in ORDER.get(point, ()) if n in have]
        return after(tuple(have[n] for n in names), *values) if names else values

    kv_near = w_qkv[:, QW:]
    kv_zs = []
    for d in Z_ORDER:
        kv_zs.append(z_swap(*gate(f"kv_z{len(kv_zs)}", kv_near), d))
        have[f"kv_z{len(kv_zs) - 1}"] = kv_zs[-1]
    kv_near_sides = sides(*gate("kv_near_sides", kv_near))
    have["kv_near_sides"] = kv_near_sides

    pair = z & 1
    (w_own,) = gate("q_rows", w_qkv)
    q_got = z_swap(
        jnp.concatenate(
            [lax.dynamic_slice_in_dim(w_own, (1 - pair) * QH, QH, 1)] + ([own_prefix] if PREFIX_WITH_Q else [])
        ),
        1,
    )
    have["q_got"] = q_got
    q_near = jnp.concatenate([lax.dynamic_slice_in_dim(w_own, pair * QH, QH, 1), q_got[:depth]])

    kv_far = jnp.concatenate(gate("kv_far", *kv_zs))
    have["kv_far"] = kv_far
    kv_far_sides = sides(kv_far)
    have["kv_far_sides"] = kv_far_sides

    (normed_in,) = gate("norm", inputs)
    normed = rms_norm(normed_in, norm_gain)
    normed_sibling = swap(normed, "core")
    have["normed_sibling"] = normed_sibling
    number = ((gx * 2 + core) * z_count + z) * y_count + y
    bits = jnp.stack([(number >> i) & 1 for i in range(5)]).astype(jnp.int32)
    zs = (0,) + tuple(Z_ORDER)

    def blocks_at(dx, dy, dzs):
        return [(dx * 8 + dz) * 2 + dy for dz in dzs]

    kv_order = []
    for dx, dy, dzs in (
        (0, 0, zs[:1]), (1, 0, zs[:1]), (0, 1, zs[:1]), (0, 0, zs[1:]), (1, 0, zs[1:]), (0, 1, zs[1:]), (1, 1, zs)
    ):
        kv_order += blocks_at(dx, dy, dzs)
    kv_features = order_features([normed, normed_sibling], kv_order, bits, WEIGHT[0])
    have["kv_features"] = kv_features

    (q_load,) = gate("q_across", q_near)
    if PREFIX_WITH_Q:
        q_load = jnp.concatenate([q_load, own_prefix, q_got[depth:]])
    q_across = z_swap(q_load, 2)
    have["q_across"] = q_across
    normed_pair = z_swap(*gate("normed_pair", normed), 1)
    have["normed_pair"] = normed_pair

    near_x, far_x, far_y = gate("kv_corner", kv_near_sides[0], *kv_far_sides)
    kv_low = swap(jnp.concatenate([near_x, far_x[:depth]]), "y")
    kv_high = swap(far_y[depth:], "gx")
    have["kv_corner"] = (kv_low, kv_high)
    if not PREFIX_WITH_Q:
        (line,) = gate("prefix_z1", own_prefix)
        line = jnp.concatenate([line, z_swap(line, 1)])
        have["prefix_z1"] = line
    kv_pieces = [kv_near, *kv_near_sides, kv_far, *kv_far_sides, *gate("kv_last", kv_low, kv_high)]
    kv_kept, kv_sent = project(kv_features, kv_pieces, 2, 1, WEIGHT[2])
    have["kv_theirs"] = kv_sent
    kv_other = swap(*gate("kv_other", kv_sent), "core")
    have["kv_other"] = kv_other
    q_line = jnp.concatenate([q_near, *gate("q_line", q_across[:2 * depth])])
    q_line_x, q_line_y = sides(q_line)
    have["q_sides"] = (q_line_x, q_line_y)
    seg_row = jnp.pad(seg_ids.astype(BF16)[None, :], ((0, 7), (0, 2 * KVW - rows)))
    block = jnp.concatenate([(kv_kept + kv_other).astype(BF16), seg_row], axis=0)
    have["block"] = block
    if PREFIX_WITH_Q:
        line = jnp.concatenate([own_prefix, q_got[depth:], q_across[2 * depth:]])
    else:
        (line,) = gate("prefix_z2", line)
        line = jnp.concatenate([line, z_swap(line, 2)])
    have["prefix_z2"] = line

    upward = [(i, i + 1) for i in range(z_count - 1)]
    two_back = lax.ppermute(*gate("two_back", block), "z", upward)
    have["two_back"] = two_back
    prefix = jnp.concatenate([line, swap(*gate("prefix_y", line), "y")])
    have["prefix_y"] = prefix
    four_back = lax.ppermute(*gate("four_back", two_back), "z", upward)
    have["four_back"] = four_back
    odd_a = swap(*gate("odd_a", two_back), "y")
    have["odd_a"] = odd_a

    q_late_x, q_late_y = gate("q_corner", q_line_x, q_line_y)
    if CORNER_BY_X:
        q_corners = [swap(q_late_y, "gx")]
    else:
        q_corners = [swap(q_late_x[:2 * depth], "y"), swap(q_late_y[2 * depth:], "gx")]
    have["q_corner"] = q_corners
    odd_b = swap(*gate("odd_b", jnp.where(y == 0, block, four_back)), "y")
    have["odd_b"] = odd_b
    blocks = [block, two_back, four_back, odd_a, odd_b]
    distances = [0, 2, 4, 1 + 2 * y, 3 - 2 * y]

    q_pieces = [q_line, q_line_x, q_line_y, *gate("q_last", *q_corners)]
    q_order = []
    for dx, dy in ((0, 0), (1, 0), (0, 1), (1, 1)):
        q_order += blocks_at(dx, dy, (0, 1, 2, 3))
    (normed_pair,) = gate("diagonal", normed_pair)
    normed_diagonal = swap(normed_pair, "core")
    q_features = order_features([normed, normed_sibling, normed_pair, normed_diagonal], q_order, bits, WEIGHT[1])
    q_kept, q_sent = project(q_features, q_pieces, len(q_corners), 2, WEIGHT[3])
    queries = (q_kept + swap(q_sent, "core")).astype(BF16) * jnp.asarray(0.125, BF16)
    halves = [queries[:rows], z_swap(*gate("q_res", queries[rows:]), 1)]

    scalars = jnp.stack([pair] + [jnp.where(index >= d, 0, 1) for d in distances]).astype(jnp.int32)
    context = attend(halves, prefix, seg_ids.astype(F32)[:, None], blocks, scalars)
    return context[None]


def gather_body(tokens, norm_gain, w_qkv, prefix_kv, segments):
    inputs, seg_ids = tokens[0], segments[0]
    rows = inputs.shape[0]
    normed = rms_norm(inputs, norm_gain)
    weights = lax.all_gather(w_qkv, ("gx", "core", "z", "y"), axis=0, tiled=True)
    projected = jnp.dot(normed, weights, preferred_element_type=F32).astype(BF16)
    queries = projected[:, :QW].reshape(rows, KEY_HEADS, REPEATS, HD)

    def absorb(state, keyvals, visible):
        running_max, denominator, numerator = state
        count = keyvals.shape[0]
        key_part = keyvals[:, :KVW].reshape(count, KEY_HEADS, HD)
        value_part = keyvals[:, KVW:].reshape(count, KEY_HEADS, HD)
        scores = jnp.einsum("tgrd,ngd->tgrn", queries, key_part, preferred_element_type=F32) * 0.125
        if visible is not None:
            scores = jnp.where(visible[:, None, None, :], scores, F32(NEG))
        new_max = jnp.maximum(running_max, jnp.max(scores, axis=-1))
        probability = jnp.exp(scores - new_max[..., None])
        if visible is not None:
            probability = jnp.where(visible[:, None, None, :], probability, F32(0.0))
        factor = jnp.exp(running_max - new_max)
        denominator = denominator * factor + jnp.sum(probability, axis=-1)
        numerator = numerator * factor[..., None] + jnp.einsum(
            "tgrn,ngd->tgrd", probability.astype(BF16), value_part, preferred_element_type=F32
        )
        return new_max, denominator, numerator

    def sweep(state, keyvals, key_seg):
        length = min(keyvals.shape[0], 512)

        def step(i, running):
            start = i * length
            part = lax.dynamic_slice_in_dim(keyvals, start, length, 0)
            if key_seg is None:
                return absorb(running, part, None)
            seg_part = lax.dynamic_slice_in_dim(key_seg, start, length, 0)
            key_pos = start + jnp.arange(length, dtype=jnp.int32)
            visible = (seg_part[None, :] == seg_ids[:, None]) & (key_pos[None, :] <= query_pos[:, None])
            return absorb(running, part, visible)

        return lax.fori_loop(0, keyvals.shape[0] // length, step, state)

    query_pos = lax.axis_index(("z", "y")) * rows + jnp.arange(rows, dtype=jnp.int32)
    state = (
        jnp.full((rows, KEY_HEADS, REPEATS), NEG, F32),
        jnp.zeros((rows, KEY_HEADS, REPEATS), F32),
        jnp.zeros((rows, KEY_HEADS, REPEATS, HD), F32),
    )
    along = functools.partial(lax.all_gather, axis_name=("z", "y"), axis=0, tiled=True)
    state = sweep(state, along(prefix_kv[0]), None)
    _, denominator, numerator = sweep(state, along(projected[:, QW:]), along(seg_ids))
    return (numerator / denominator[..., None]).reshape(rows, QW).astype(BF16)[None]


def solution(mesh):
    groups, seqs = mesh.shape["group"], mesh.shape["seq"]
    chips, z_count = groups // 2, seqs // 2
    fine = Mesh(mesh.devices.reshape(chips, 2, z_count, 2), ("gx", "core", "z", "y"))
    group, seq = ("gx", "core"), ("z", "y")
    short = chips == 2 and z_count == SMALL
    return jax.shard_map(
        swap_body if short else gather_body,
        mesh=fine,
        in_specs=(P(group, seq, None), P(), P(group + seq, None), P(group, seq, None), P(group, seq)),
        out_specs=P(group, seq, None),
        check_vma=False,
    )
```

time: 86.1 us -> 72.8 us (0.85)
  waiting for transfers between devices: 34.8 us -> 22.8 us
  other arithmetic: 2.03 us -> 3.37 us
  local copies, waits for them, and re-layouts: 2.61 us -> 1.49 us
  Pallas kernels: 12.3 us -> 11.3 us
    ppermute x7, waiting for transfers between devices: 15.8 us -> 6.88 us  [z_swap(): return lax.ppermute(x, 'z', [(i, i ^ distance) for i in range(4)])]
    ppermute x2, waiting for transfers between devices: 3.93 us -> 0.64 us  [the longest x1 0.64 us: swap_body(): four_back = lax.ppermute(*gate('four_back', two_back), 'z', upward)]
    ppermute x7, starting transfers between devices: 11 us -> 12.7 us  [z_swap(): return lax.ppermute(x, 'z', [(i, i ^ distance) for i in range(4)])]
    ppermute x18 -> x16, starting transfers between devices: 15.9 us -> 14.3 us  [swap(): return lax.ppermute(x, axis, [(0, 1), (1, 0)])]
    reduce_sum x1, other arithmetic: 0.19 us -> 1.23 us  [rms_norm(): mean_square = jnp.mean(values * values, axis=-1, keepdims=True)]
    dynamic_slice x2 -> x1, local copies, waits for them, and re-layouts: 1.97 us -> 1.06 us  [swap_body(): lax.dynamic_slice_in_dim(w_own, pair * QH, QH, 1)]
    ppermute x18 -> x16, waiting for transfers between devices: 15 us -> 15.3 us  [swap(): return lax.ppermute(x, axis, [(0, 1), (1, 0)])]
  transfers between devices with their start and end apart: 27 -> 25, of which waited for: 15 -> 14; matrix products, arithmetic and copies ran while one was open for 3% -> 5% of each run, Pallas kernels for 7% -> 7%
where the time goes in v3:
time: 72.8 us; the launch traced here: 72.5 us
  starting transfers between devices  33.2 us (46%)
  waiting for transfers between devices  22.8 us (31%)
  Pallas kernels  11.3 us (16%)
  other arithmetic  3.37 us (5%)
  local copies, waits for them, and re-layouts  1.49 us (2%)
    ppermute x16, waiting for transfers between devices, swap(): return lax.ppermute(x, axis, [(0, 1), (1, 0)])  15.3 us
    ppermute x16, starting transfers between devices, swap(): return lax.ppermute(x, axis, [(0, 1), (1, 0)])  14.3 us
    ppermute x7, starting transfers between devices, z_swap(): return lax.ppermute(x, 'z', [(i, i ^ distance) for i in range(4)])  12.7 us
    ppermute x7, waiting for transfers between devices, z_swap(): return lax.ppermute(x, 'z', [(i, i ^ distance) for i in range(4)])  6.88 us
    pallas_call x1, Pallas kernels, attend(): pl.pallas_call(functools.partial(attend_kernel, earlier), out_shape=jax.S...  6.2 us
    ppermute x1, starting transfers between devices, swap_body(): four_back = lax.ppermute(*gate('four_back', two_back), 'z', upward)  3.83 us
    pallas_call x2, Pallas kernels, order_features(): pl.pallas_call(functools.partial(order_kernel, order), out_shape=jax.Shap...  2.87 us
    ppermute x1, starting transfers between devices, swap_body(): two_back = lax.ppermute(*gate('two_back', block), 'z', upward)  2.38 us
  transfers between devices with their start and end apart: 25, of which 14 were waited for; matrix products, arithmetic and copies ran while one was open for 5% of the time, Pallas kernels for 7%

profile of v3, /device:TPU:0, one launch (start us, length us, event | category | flops | bytes accessed | tf_op | source)
XLA Modules:
  0.0 72.5 jit_solution(10789830724432216415)
XLA Ops:
  1.1 3.1 %collective-permute-start.1 = (bf16[64,640]{1,0:T(8,128)(2,1)S(1)}, bf16[64,640]{1,0:T(8,128)(2,1)S(1)}, u32[]{:S(2)}, u32[]{:S(2)}) collective-permute-start(bf16[64,640]{1,0:T(8,128)(2,1)S(1)} %get-tuple-element.24.refs_0_), channel_id=1, source_target_pairs={{0,2},{2,0},{4,6},{6,4},{1,3},{3,1},{5,7},{7,5},{8,10},{10,8},{12,... | collective-permute-start | bytes 245768 | tf_op jit(solution)/shard_map/ppermute | solution.py:53
  4.2 2.6 %collective-permute-start.7 = (bf16[64,640]{1,0:T(8,128)(2,1)S(1)}, bf16[64,640]{1,0:T(8,128)(2,1)S(1)}, u32[]{:S(2)}, u32[]{:S(2)}) collective-permute-start(bf16[64,640]{1,0:T(8,128)(2,1)S(1)} %get-tuple-element.24.refs_0_), channel_id=1, source_target_pairs={{0,4},{2,6},{4,0},{6,2},{1,5},{3,7},{5,1},{7,3},{8,12},{10,14},{12... | collective-permute-start | bytes 245768 | tf_op jit(solution)/shard_map/ppermute | solution.py:53
  8.6 1.2 %fusion = f32[128]{0:T(128)S(1)} fusion(bf16[1,128,2048]{2,1,0:T(8,128)(2,1)} %param.5), kind=kLoop, calls=%fused_computation.2 | loop fusion | flops 786304 | bytes 524800 | tf_op jit(solution)/shard_map/reduce_sum | solution.py:44
  9.9 1.6 %collective-permute-start.2 = (bf16[64,640]{1,0:T(8,128)(2,1)S(1)}, bf16[64,640]{1,0:T(8,128)(2,1)S(1)}, u32[]{:S(2)}, u32[]{:S(2)}) collective-permute-start(bf16[64,640]{1,0:T(8,128)(2,1)S(1)} %get-tuple-element.24.refs_0_), channel_id=1, source_target_pairs={{0,16},{16,0},{1,17},{17,1},{2,18},{18,2},{3,19},{19,3},{4,20},{20... | collective-permute-start | bytes 245768 | tf_op jit(solution)/shard_map/ppermute | solution.py:49
  11.5 1.5 %collective-permute-start.3 = (bf16[64,640]{1,0:T(8,128)(2,1)S(1)}, bf16[64,640]{1,0:T(8,128)(2,1)S(1)}, u32[]{:S(2)}, u32[]{:S(2)}) collective-permute-start(bf16[64,640]{1,0:T(8,128)(2,1)S(1)} %get-tuple-element.24.refs_0_), channel_id=1, source_target_pairs={{0,1},{1,0},{2,3},{3,2},{4,5},{5,4},{6,7},{7,6},{8,9},{9,8},{10,11... | collective-permute-start | bytes 245768 | tf_op jit(solution)/shard_map/ppermute | solution.py:49
  14.4 1.5 %collective-permute-done.3.refs_2_ = bf16[64,640]{1,0:T(8,128)(2,1)S(1)} collective-permute-done((bf16[64,640]{1,0:T(8,128)(2,1)S(1)}, bf16[64,640]{1,0:T(8,128)(2,1)S(1)}, u32[]{:S(2)}, u32[]{:S(2)}) %collective-permute-start.3) | collective-permute-done | bytes 81952 | tf_op jit(solution)/shard_map/ppermute | solution.py:49
  15.9 1.6 %collective-permute-start.10 = (bf16[192,640]{1,0:T(8,128)(2,1)S(1)}, bf16[192,640]{1,0:T(8,128)(2,1)S(1)}, u32[]{:S(2)}, u32[]{:S(2)}) collective-permute-start(bf16[192,640]{1,0:T(8,128)(2,1)S(1)} %constant_dynamic-update-slice_fusion.refs_3_), channel_id=1, source_target_pairs={{0,1},{1,0},{2,3},{3,2},{4,5},{5,4},{6,7},{7,6},{8,9},{9,8},{10,11... | collective-permute-start | bytes 737288 | tf_op jit(solution)/shard_map/ppermute | solution.py:49
  18.7 3.0 %collective-permute-start.11 = (bf16[256,640]{1,0:T(8,128)(2,1)S(1)}, bf16[256,640]{1,0:T(8,128)(2,1)S(1)}, u32[]{:S(2)}, u32[]{:S(2)}) collective-permute-start(bf16[256,640]{1,0:T(8,128)(2,1)S(1)} %pad_maximum_fusion.1), channel_id=1, source_target_pairs={{0,4},{2,6},{4,0},{6,2},{1,5},{3,7},{5,1},{7,3},{8,12},{10,14},{12... | collective-permute-start | bytes 983048 | tf_op jit(solution)/shard_map/ppermute | solution.py:53
  24.4 1.6 %collective-permute-start.15 = (bf16[128,640]{1,0:T(8,128)(2,1)S(1)}, bf16[128,640]{1,0:T(8,128)(2,1)S(1)}, u32[]{:S(2)}, u32[]{:S(2)}) collective-permute-start(bf16[128,640]{1,0:T(8,128)(2,1)S(1)} %slice.34), channel_id=1, source_target_pairs={{0,16},{16,0},{1,17},{17,1},{2,18},{18,2},{3,19},{19,3},{4,20},{20... | collective-permute-start | bytes 491528 | tf_op jit(solution)/shard_map/ppermute | solution.py:49
  26.7 2.5 %collective-permute-done.14.refs_0_ = bf16[128,640]{1,0:T(8,128)(2,1)S(1)} collective-permute-done((bf16[128,640]{1,0:T(8,128)(2,1)S(1)}, bf16[128,640]{1,0:T(8,128)(2,1)S(1)}, u32[]{:S(2)}, u32[]{:S(2)}) %collective-permute-start.14) | collective-permute-done | bytes 163872 | tf_op jit(solution)/shard_map/ppermute | solution.py:49
  30.1 4.7 %collective-permute-done.11 = bf16[256,640]{1,0:T(8,128)(2,1)S(1)} collective-permute-done((bf16[256,640]{1,0:T(8,128)(2,1)S(1)}, bf16[256,640]{1,0:T(8,128)(2,1)S(1)}, u32[]{:S(2)}, u32[]{:S(2)}) %collective-permute-start.11) | collective-permute-done | bytes 327712 | tf_op jit(solution)/shard_map/ppermute | solution.py:53
  36.3 1.4 %collective-permute-start.19 = (bf16[256,640]{1,0:T(8,128)(2,1)S(1)}, bf16[256,640]{1,0:T(8,128)(2,1)S(1)}, u32[]{:S(2)}, u32[]{:S(2)}) collective-permute-start(bf16[256,640]{1,0:T(8,128)(2,1)S(1)} %pad_maximum_fusion.3), channel_id=1, source_target_pairs={{0,1},{1,0},{2,3},{3,2},{4,5},{5,4},{6,7},{7,6},{8,9},{9,8},{10,11... | collective-permute-start | bytes 983048 | tf_op jit(solution)/shard_map/ppermute | solution.py:49
  37.7 1.5 %collective-permute-done.4.refs_2_ = bf16[128,2048]{1,0:T(8,128)(2,1)S(1)} collective-permute-done((bf16[128,2048]{1,0:T(8,128)(2,1)S(1)}, bf16[128,2048]{1,0:T(8,128)(2,1)S(1)}, u32[]{:S(2)}, u32[]{:S(2)}) %collective-permute-start.4) | collective-permute-done | bytes 524320 | tf_op jit(solution)/shard_map/ppermute | solution.py:53
  39.3 2.4 %collective-permute-start.17 = (bf16[136,640]{1,0:T(8,128)(2,1)S(1)}, bf16[136,640]{1,0:T(8,128)(2,1)S(1)}, u32[]{:S(2)}, u32[]{:S(2)}) collective-permute-start(bf16[136,640]{1,0:T(8,128)(2,1)S(1)} %fusion.5.refs_0_), channel_id=1, source_target_pairs={{0,2},{2,4},{4,6},{1,3},{3,5},{5,7},{8,10},{10,12},{12,14},{9,11},... | collective-permute-start | bytes 522248 | tf_op jit(solution)/shard_map/ppermute | solution.py:294
  41.6 2.5 %collective-permute-done.12.refs_1_ = bf16[256,640]{1,0:T(8,128)(2,1)S(1)} collective-permute-done((bf16[256,640]{1,0:T(8,128)(2,1)S(1)}, bf16[256,640]{1,0:T(8,128)(2,1)S(1)}, u32[]{:S(2)}, u32[]{:S(2)}) %collective-permute-start.12) | collective-permute-done | bytes 327712 | tf_op jit(solution)/shard_map/ppermute | solution.py:49
  44.1 2.1 %collective-permute-done.13.refs_2_ = bf16[256,640]{1,0:T(8,128)(2,1)S(1)} collective-permute-done((bf16[256,640]{1,0:T(8,128)(2,1)S(1)}, bf16[256,640]{1,0:T(8,128)(2,1)S(1)}, u32[]{:S(2)}, u32[]{:S(2)}) %collective-permute-start.13) | collective-permute-done | bytes 327712 | tf_op jit(solution)/shard_map/ppermute | solution.py:49
  46.2 1.5 %collective-permute-start.20 = (bf16[256,640]{1,0:T(8,128)(2,1)S(1)}, bf16[256,640]{1,0:T(8,128)(2,1)S(1)}, u32[]{:S(2)}, u32[]{:S(2)}) collective-permute-start(bf16[256,640]{1,0:T(8,128)(2,1)S(1)} %collective-permute-done.13.refs_2_), channel_id=1, source_target_pairs={{0,16},{16,0},{1,17},{17,1},{2,18},{18,2},{3,19},{19,3},{4,20},{20... | collective-permute-start | bytes 983048 | tf_op jit(solution)/shard_map/ppermute | solution.py:49
  47.7 3.8 %collective-permute-start.18 = (bf16[136,640]{1,0:T(8,128)(2,1)S(1)}, bf16[136,640]{1,0:T(8,128)(2,1)S(1)}, u32[]{:S(2)}, u32[]{:S(2)}) collective-permute-start(bf16[136,640]{1,0:T(8,128)(2,1)S(1)} %collective-permute-done.17.refs_1_), channel_id=1, source_target_pairs={{0,2},{2,4},{4,6},{1,3},{3,5},{5,7},{8,10},{10,12},{12,14},{9,11},... | collective-permute-start | bytes 522248 | tf_op jit(solution)/shard_map/ppermute | solution.py:298
  51.6 1.7 %shard_map.55.features = bf16[512,1024]{1,0:T(8,128)(2,1)S(1)} custom-call(s32[5]{0:T(128)S(1)} %stack.51.bits, bf16[128,2048]{1,0:T(8,128)(2,1)S(1)} %fusion.2.refs_0_, bf16[128,2048]{1,0:T(8,128)(2,1)S(1)} %collective-permute-done.refs_1_, bf16[128,2048]{1,0:T(8,128)(2,1)S(1)} %collective-permute-done.4.refs_2_, ...), custom_call_target="tpu_custom_call" | custom-call | bytes 4194304 | tf_op jit(solution)/shard_map/pallas_call | solution.py:78
  57.4 1.2 %collective-permute-start.24 = (bf16[136,640]{1,0:T(8,128)(2,1)}, bf16[136,640]{1,0:T(8,128)(2,1)S(1)}, u32[]{:S(2)}, u32[]{:S(2)}) collective-permute-start(bf16[136,640]{1,0:T(8,128)(2,1)} %broadcast_select_fusion), channel_id=1, source_target_pairs={{0,1},{1,0},{2,3},{3,2},{4,5},{5,4},{6,7},{7,6},{8,9},{9,8},{10,11... | collective-permute-start | bytes 522248 | tf_op jit(solution)/shard_map/ppermute | solution.py:49
  58.7 2.5 %collective-permute-start.22 = (bf16[128,640]{1,0:T(8,128)(2,1)S(1)}, bf16[128,640]{1,0:T(8,128)(2,1)S(1)}, u32[]{:S(2)}, u32[]{:S(2)}) collective-permute-start(bf16[128,640]{1,0:T(8,128)(2,1)S(1)} %get-tuple-element.41), channel_id=1, source_target_pairs={{0,2},{2,0},{4,6},{6,4},{1,3},{3,1},{5,7},{7,5},{8,10},{10,8},{12,... | collective-permute-start | bytes 491528 | tf_op jit(solution)/shard_map/ppermute | solution.py:53
  61.4 1.6 %collective-permute-done.23.refs_3_ = bf16[136,640]{1,0:T(8,128)(2,1)S(1)} collective-permute-done((bf16[136,640]{1,0:T(8,128)(2,1)S(1)}, bf16[136,640]{1,0:T(8,128)(2,1)S(1)}, u32[]{:S(2)}, u32[]{:S(2)}) %collective-permute-start.23) | collective-permute-done | bytes 174112 | tf_op jit(solution)/shard_map/ppermute | solution.py:49
  63.1 3.3 %collective-permute-done.24.refs_4_ = bf16[136,640]{1,0:T(8,128)(2,1)S(1)} collective-permute-done((bf16[136,640]{1,0:T(8,128)(2,1)}, bf16[136,640]{1,0:T(8,128)(2,1)S(1)}, u32[]{:S(2)}, u32[]{:S(2)}) %collective-permute-start.24) | collective-permute-done | bytes 174112 | tf_op jit(solution)/shard_map/ppermute | solution.py:49
  66.3 6.2 %shard_map.61 = bf16[128,1280]{1,0:T(8,128)(2,1)} custom-call(s32[6]{0:T(128)S(1)} %stack.45.scalars, bf16[128,640]{1,0:T(8,128)(2,1)S(1)} %get-tuple-element.44.mine, bf16[128,640]{1,0:T(8,128)(2,1)S(1)} %collective-permute-done.22.pair, bf16[512,640]{1,0:T(8,128)(2,1)S(1)} %pad_maximum_fusion.prefix, f32[128,1]{1,0:T(8,128)S(1)} %copy.6.seg_col, ...), custom_call_target="tpu_custom_call" | custom-call | flops 754974720 | bytes 1474560 | tf_op jit(solution)/shard_map/pallas_call | solution.py:189
  (69 shorter events, 15.7 us)
Async XLA Ops:
  1.1 8.8 %collective-permute-start.1 = (bf16[64,640]{1,0:T(8,128)(2,1)S(1)}, bf16[64,640]{1,0:T(8,128)(2,1)S(1)}, u32[]{:S(2)}, u32[]{:S(2)}) collective-permute-start(bf16[64,640]{1,0:T(8,128)(2,1)S(1)} %get-tuple-element.24.refs_0_), channel_id=1, source_target_pairs={{0,2},{2,0},{4,6},{6,4},{1,3},{3,1},{5,7},{7,5},{8,10},{10,8},{12,... | collective-permute-start | bytes 245768 | tf_op jit(solution)/shard_map/ppermute | solution.py:53
  4.2 9.1 %collective-permute-start.7 = (bf16[64,640]{1,0:T(8,128)(2,1)S(1)}, bf16[64,640]{1,0:T(8,128)(2,1)S(1)}, u32[]{:S(2)}, u32[]{:S(2)}) collective-permute-start(bf16[64,640]{1,0:T(8,128)(2,1)S(1)} %get-tuple-element.24.refs_0_), channel_id=1, source_target_pairs={{0,4},{2,6},{4,0},{6,2},{1,5},{3,7},{5,1},{7,3},{8,12},{10,14},{12... | collective-permute-start | bytes 245768 | tf_op jit(solution)/shard_map/ppermute | solution.py:53
  6.7 7.2 %collective-permute-start.8 = (bf16[64,640]{1,0:T(8,128)(2,1)S(1)}, bf16[64,640]{1,0:T(8,128)(2,1)S(1)}, u32[]{:S(2)}, u32[]{:S(2)}) collective-permute-start(bf16[64,640]{1,0:T(8,128)(2,1)S(1)} %get-tuple-element.24.refs_0_), channel_id=1, source_target_pairs={{0,6},{2,4},{4,2},{6,0},{1,7},{3,5},{5,3},{7,1},{8,14},{10,12},{12... | collective-permute-start | bytes 245768 | tf_op jit(solution)/shard_map/ppermute | solution.py:53
  7.7 8.2 %collective-permute-start.6 = (bf16[128,640]{1,0:T(8,128)(2,1)S(1)}, bf16[128,640]{1,0:T(8,128)(2,1)S(1)}, u32[]{:S(2)}, u32[]{:S(2)}) collective-permute-start(bf16[128,640]{1,0:T(8,128)(2,1)S(1)} %pad_maximum_fusion.4), channel_id=1, source_target_pairs={{0,2},{2,0},{4,6},{6,4},{1,3},{3,1},{5,7},{7,5},{8,10},{10,8},{12,... | collective-permute-start | bytes 491528 | tf_op jit(solution)/shard_map/ppermute | solution.py:53
  9.9 4.5 %collective-permute-start.2 = (bf16[64,640]{1,0:T(8,128)(2,1)S(1)}, bf16[64,640]{1,0:T(8,128)(2,1)S(1)}, u32[]{:S(2)}, u32[]{:S(2)}) collective-permute-start(bf16[64,640]{1,0:T(8,128)(2,1)S(1)} %get-tuple-element.24.refs_0_), channel_id=1, source_target_pairs={{0,16},{16,0},{1,17},{17,1},{2,18},{18,2},{3,19},{19,3},{4,20},{20... | collective-permute-start | bytes 245768 | tf_op jit(solution)/shard_map/ppermute | solution.py:49
  11.5 4.4 %collective-permute-start.3 = (bf16[64,640]{1,0:T(8,128)(2,1)S(1)}, bf16[64,640]{1,0:T(8,128)(2,1)S(1)}, u32[]{:S(2)}, u32[]{:S(2)}) collective-permute-start(bf16[64,640]{1,0:T(8,128)(2,1)S(1)} %get-tuple-element.24.refs_0_), channel_id=1, source_target_pairs={{0,1},{1,0},{2,3},{3,2},{4,5},{5,4},{6,7},{7,6},{8,9},{9,8},{10,11... | collective-permute-start | bytes 245768 | tf_op jit(solution)/shard_map/ppermute | solution.py:49
  13.3 9.0 %collective-permute-start = (bf16[128,2048]{1,0:T(8,128)(2,1)S(1)}, bf16[128,2048]{1,0:T(8,128)(2,1)S(1)}, u32[]{:S(2)}, u32[]{:S(2)}) collective-permute-start(bf16[128,2048]{1,0:T(8,128)(2,1)S(1)} %fusion.2.refs_0_), channel_id=1, source_target_pairs={{0,8},{8,0},{1,9},{9,1},{2,10},{10,2},{3,11},{11,3},{4,12},{12,4},... | collective-permute-start | bytes 1572872 | tf_op jit(solution)/shard_map/ppermute | solution.py:49
  15.9 7.4 %collective-permute-start.10 = (bf16[192,640]{1,0:T(8,128)(2,1)S(1)}, bf16[192,640]{1,0:T(8,128)(2,1)S(1)}, u32[]{:S(2)}, u32[]{:S(2)}) collective-permute-start(bf16[192,640]{1,0:T(8,128)(2,1)S(1)} %constant_dynamic-update-slice_fusion.refs_3_), channel_id=1, source_target_pairs={{0,1},{1,0},{2,3},{3,2},{4,5},{5,4},{6,7},{7,6},{8,9},{9,8},{10,11... | collective-permute-start | bytes 737288 | tf_op jit(solution)/shard_map/ppermute | solution.py:49
  17.5 6.2 %collective-permute-start.9 = (bf16[192,640]{1,0:T(8,128)(2,1)S(1)}, bf16[192,640]{1,0:T(8,128)(2,1)S(1)}, u32[]{:S(2)}, u32[]{:S(2)}) collective-permute-start(bf16[192,640]{1,0:T(8,128)(2,1)S(1)} %constant_dynamic-update-slice_fusion.refs_3_), channel_id=1, source_target_pairs={{0,16},{16,0},{1,17},{17,1},{2,18},{18,2},{3,19},{19,3},{4,20},{20... | collective-permute-start | bytes 737288 | tf_op jit(solution)/shard_map/ppermute | solution.py:49
  18.7 16.2 %collective-permute-start.11 = (bf16[256,640]{1,0:T(8,128)(2,1)S(1)}, bf16[256,640]{1,0:T(8,128)(2,1)S(1)}, u32[]{:S(2)}, u32[]{:S(2)}) collective-permute-start(bf16[256,640]{1,0:T(8,128)(2,1)S(1)} %pad_maximum_fusion.1), channel_id=1, source_target_pairs={{0,4},{2,6},{4,0},{6,2},{1,5},{3,7},{5,1},{7,3},{8,12},{10,14},{12... | collective-permute-start | bytes 983048 | tf_op jit(solution)/shard_map/ppermute | solution.py:53
  21.7 17.5 %collective-permute-start.4 = (bf16[128,2048]{1,0:T(8,128)(2,1)S(1)}, bf16[128,2048]{1,0:T(8,128)(2,1)S(1)}, u32[]{:S(2)}, u32[]{:S(2)}) collective-permute-start(bf16[128,2048]{1,0:T(8,128)(2,1)S(1)} %fusion.2.refs_0_), channel_id=1, source_target_pairs={{0,2},{2,0},{4,6},{6,4},{1,3},{3,1},{5,7},{7,5},{8,10},{10,8},{12,... | collective-permute-start | bytes 1572872 | tf_op jit(solution)/shard_map/ppermute | solution.py:53
  23.8 5.4 %collective-permute-start.14 = (bf16[128,640]{1,0:T(8,128)(2,1)S(1)}, bf16[128,640]{1,0:T(8,128)(2,1)S(1)}, u32[]{:S(2)}, u32[]{:S(2)}) collective-permute-start(bf16[128,640]{1,0:T(8,128)(2,1)S(1)} %pad_maximum_fusion.6), channel_id=1, source_target_pairs={{0,1},{1,0},{2,3},{3,2},{4,5},{5,4},{6,7},{7,6},{8,9},{9,8},{10,11... | collective-permute-start | bytes 491528 | tf_op jit(solution)/shard_map/ppermute | solution.py:49
  24.4 5.4 %collective-permute-start.15 = (bf16[128,640]{1,0:T(8,128)(2,1)S(1)}, bf16[128,640]{1,0:T(8,128)(2,1)S(1)}, u32[]{:S(2)}, u32[]{:S(2)}) collective-permute-start(bf16[128,640]{1,0:T(8,128)(2,1)S(1)} %slice.34), channel_id=1, source_target_pairs={{0,16},{16,0},{1,17},{17,1},{2,18},{18,2},{3,19},{19,3},{4,20},{20... | collective-permute-start | bytes 491528 | tf_op jit(solution)/shard_map/ppermute | solution.py:49
  30.1 9.1 %collective-permute-start.16 = (f32[128,640]{1,0:T(8,128)S(1)}, f32[128,640]{1,0:T(8,128)S(1)}, u32[]{:S(2)}, u32[]{:S(2)}) collective-permute-start(f32[128,640]{1,0:T(8,128)S(1)} %get-tuple-element.35), channel_id=1, source_target_pairs={{0,8},{8,0},{1,9},{9,1},{2,10},{10,2},{3,11},{11,3},{4,12},{12,4},... | collective-permute-start | bytes 983048 | tf_op jit(solution)/shard_map/ppermute | solution.py:49
  35.0 9.2 %collective-permute-start.12 = (bf16[256,640]{1,0:T(8,128)(2,1)S(1)}, bf16[256,640]{1,0:T(8,128)(2,1)S(1)}, u32[]{:S(2)}, u32[]{:S(2)}) collective-permute-start(bf16[256,640]{1,0:T(8,128)(2,1)S(1)} %pad_maximum_fusion.2.refs_0_), channel_id=1, source_target_pairs={{0,16},{16,0},{1,17},{17,1},{2,18},{18,2},{3,19},{19,3},{4,20},{20... | collective-permute-start | bytes 983048 | tf_op jit(solution)/shard_map/ppermute | solution.py:49
  35.6 10.7 %collective-permute-start.13 = (bf16[256,640]{1,0:T(8,128)(2,1)S(1)}, bf16[256,640]{1,0:T(8,128)(2,1)S(1)}, u32[]{:S(2)}, u32[]{:S(2)}) collective-permute-start(bf16[256,640]{1,0:T(8,128)(2,1)S(1)} %pad_maximum_fusion.2.refs_0_), channel_id=1, source_target_pairs={{0,1},{1,0},{2,3},{3,2},{4,5},{5,4},{6,7},{7,6},{8,9},{9,8},{10,11... | collective-permute-start | bytes 983048 | tf_op jit(solution)/shard_map/ppermute | solution.py:49
  36.3 15.3 %collective-permute-start.19 = (bf16[256,640]{1,0:T(8,128)(2,1)S(1)}, bf16[256,640]{1,0:T(8,128)(2,1)S(1)}, u32[]{:S(2)}, u32[]{:S(2)}) collective-permute-start(bf16[256,640]{1,0:T(8,128)(2,1)S(1)} %pad_maximum_fusion.3), channel_id=1, source_target_pairs={{0,1},{1,0},{2,3},{3,2},{4,5},{5,4},{6,7},{7,6},{8,9},{9,8},{10,11... | collective-permute-start | bytes 983048 | tf_op jit(solution)/shard_map/ppermute | solution.py:49
  39.2 12.5 %collective-permute-start.5 = (bf16[128,2048]{1,0:T(8,128)(2,1)S(1)}, bf16[128,2048]{1,0:T(8,128)(2,1)S(1)}, u32[]{:S(2)}, u32[]{:S(2)}) collective-permute-start(bf16[128,2048]{1,0:T(8,128)(2,1)S(1)} %collective-permute-done.4.refs_2_), channel_id=1, source_target_pairs={{0,8},{8,0},{1,9},{9,1},{2,10},{10,2},{3,11},{11,3},{4,12},{12,4},... | collective-permute-start | bytes 1572872 | tf_op jit(solution)/shard_map/ppermute | solution.py:49
  39.3 7.0 %collective-permute-start.17 = (bf16[136,640]{1,0:T(8,128)(2,1)S(1)}, bf16[136,640]{1,0:T(8,128)(2,1)S(1)}, u32[]{:S(2)}, u32[]{:S(2)}) collective-permute-start(bf16[136,640]{1,0:T(8,128)(2,1)S(1)} %fusion.5.refs_0_), channel_id=1, source_target_pairs={{0,2},{2,4},{4,6},{1,3},{3,5},{5,7},{8,10},{10,12},{12,14},{9,11},... | collective-permute-start | bytes 522248 | tf_op jit(solution)/shard_map/ppermute | solution.py:294
  46.2 9.1 %collective-permute-start.20 = (bf16[256,640]{1,0:T(8,128)(2,1)S(1)}, bf16[256,640]{1,0:T(8,128)(2,1)S(1)}, u32[]{:S(2)}, u32[]{:S(2)}) collective-permute-start(bf16[256,640]{1,0:T(8,128)(2,1)S(1)} %collective-permute-done.13.refs_2_), channel_id=1, source_target_pairs={{0,16},{16,0},{1,17},{17,1},{2,18},{18,2},{3,19},{19,3},{4,20},{20... | collective-permute-start | bytes 983048 | tf_op jit(solution)/shard_map/ppermute | solution.py:49
  47.7 7.1 %collective-permute-start.18 = (bf16[136,640]{1,0:T(8,128)(2,1)S(1)}, bf16[136,640]{1,0:T(8,128)(2,1)S(1)}, u32[]{:S(2)}, u32[]{:S(2)}) collective-permute-start(bf16[136,640]{1,0:T(8,128)(2,1)S(1)} %collective-permute-done.17.refs_1_), channel_id=1, source_target_pairs={{0,2},{2,4},{4,6},{1,3},{3,5},{5,7},{8,10},{10,12},{12,14},{9,11},... | collective-permute-start | bytes 522248 | tf_op jit(solution)/shard_map/ppermute | solution.py:298
  55.8 7.3 %collective-permute-start.23 = (bf16[136,640]{1,0:T(8,128)(2,1)S(1)}, bf16[136,640]{1,0:T(8,128)(2,1)S(1)}, u32[]{:S(2)}, u32[]{:S(2)}) collective-permute-start(bf16[136,640]{1,0:T(8,128)(2,1)S(1)} %collective-permute-done.17.refs_1_), channel_id=1, source_target_pairs={{0,1},{1,0},{2,3},{3,2},{4,5},{5,4},{6,7},{7,6},{8,9},{9,8},{10,11... | collective-permute-start | bytes 522248 | tf_op jit(solution)/shard_map/ppermute | solution.py:49
  57.4 8.9 %collective-permute-start.24 = (bf16[136,640]{1,0:T(8,128)(2,1)}, bf16[136,640]{1,0:T(8,128)(2,1)S(1)}, u32[]{:S(2)}, u32[]{:S(2)}) collective-permute-start(bf16[136,640]{1,0:T(8,128)(2,1)} %broadcast_select_fusion), channel_id=1, source_target_pairs={{0,1},{1,0},{2,3},{3,2},{4,5},{5,4},{6,7},{7,6},{8,9},{9,8},{10,11... | collective-permute-start | bytes 522248 | tf_op jit(solution)/shard_map/ppermute | solution.py:49
  58.7 7.6 %collective-permute-start.22 = (bf16[128,640]{1,0:T(8,128)(2,1)S(1)}, bf16[128,640]{1,0:T(8,128)(2,1)S(1)}, u32[]{:S(2)}, u32[]{:S(2)}) collective-permute-start(bf16[128,640]{1,0:T(8,128)(2,1)S(1)} %get-tuple-element.41), channel_id=1, source_target_pairs={{0,2},{2,0},{4,6},{6,4},{1,3},{3,1},{5,7},{7,5},{8,10},{10,8},{12,... | collective-permute-start | bytes 491528 | tf_op jit(solution)/shard_map/ppermute | solution.py:53
  (5 other events, 43.9 us)

commit v4 on v3

--- a/solution.py
+++ b/solution.py
@@ -15,7 +15,7 @@
 QH = QW // 2
 NEG = -1e30
 SMALL = 4
-PREFIX_WITH_Q = True
+PREFIX_WITH_Q = 2
 CORNER_BY_X = True
 Z_ORDER = (1, 2, 3)
 WEIGHT = (1, 1, 1, 1)
@@ -31,9 +31,8 @@
     "prefix_z1": ("kv_far_sides",),
     "prefix_z2": ("q_across",),
     "q_corner": ("two_back",),
-    "four_back": ("normed_pair", "prefix_z2",),
-    "q_last": ("four_back", "prefix_y",),
-    "odd_a": ("prefix_y",),
+    "four_back": ("normed_pair", "prefix_z2", "q_features",),
+    "q_last": ("four_back", "prefix_y", "odd_a",),
 }
 F32 = jnp.float32
 BF16 = jnp.bfloat16
@@ -257,7 +256,7 @@
     have["kv_features"] = kv_features
 
     (q_load,) = gate("q_across", q_near)
-    if PREFIX_WITH_Q:
+    if PREFIX_WITH_Q == 1:
         q_load = jnp.concatenate([q_load, own_prefix, q_got[depth:]])
     q_across = z_swap(q_load, 2)
     have["q_across"] = q_across
@@ -283,12 +282,22 @@
     seg_row = jnp.pad(seg_ids.astype(BF16)[None, :], ((0, 7), (0, 2 * KVW - rows)))
     block = jnp.concatenate([(kv_kept + kv_other).astype(BF16), seg_row], axis=0)
     have["block"] = block
-    if PREFIX_WITH_Q:
+    if PREFIX_WITH_Q == 1:
         line = jnp.concatenate([own_prefix, q_got[depth:], q_across[2 * depth:]])
     else:
+        if PREFIX_WITH_Q:
+            line = jnp.concatenate([own_prefix, q_got[depth:]])
         (line,) = gate("prefix_z2", line)
         line = jnp.concatenate([line, z_swap(line, 2)])
     have["prefix_z2"] = line
+
+    q_order = []
+    for dx, dy in ((0, 0), (1, 0), (0, 1), (1, 1)):
+        q_order += blocks_at(dx, dy, (0, 1, 2, 3))
+    (normed_pair,) = gate("diagonal", normed_pair)
+    normed_diagonal = swap(normed_pair, "core")
+    q_features = order_features([normed, normed_sibling, normed_pair, normed_diagonal], q_order, bits, WEIGHT[1])
+    have["q_features"] = q_features
 
     upward = [(i, i + 1) for i in range(z_count - 1)]
     two_back = lax.ppermute(*gate("two_back", block), "z", upward)
@@ -312,12 +321,6 @@
     distances = [0, 2, 4, 1 + 2 * y, 3 - 2 * y]
 
     q_pieces = [q_line, q_line_x, q_line_y, *gate("q_last", *q_corners)]
-    q_order = []
-    for dx, dy in ((0, 0), (1, 0), (0, 1), (1, 1)):
-        q_order += blocks_at(dx, dy, (0, 1, 2, 3))
-    (normed_pair,) = gate("diagonal", normed_pair)
-    normed_diagonal = swap(normed_pair, "core")
-    q_features = order_features([normed, normed_sibling, normed_pair, normed_diagonal], q_order, bits, WEIGHT[1])
     q_kept, q_sent = project(q_features, q_pieces, len(q_corners), 2, WEIGHT[3])
     queries = (q_kept + swap(q_sent, "core")).astype(BF16) * jnp.asarray(0.125, BF16)
     halves = [queries[:rows], z_swap(*gate("q_res", queries[rows:]), 1)]

time: 72.8 us -> 71.6 us (0.984)
  waiting for transfers between devices: 22.8 us -> 17.1 us
  starting transfers between devices: 33.2 us -> 37.8 us
    ppermute x16, starting transfers between devices: 14.3 us -> 17.5 us  [swap(): return lax.ppermute(x, axis, [(0, 1), (1, 0)])]
    ppermute x16, waiting for transfers between devices: 15.3 us -> 12.1 us  [swap(): return lax.ppermute(x, axis, [(0, 1), (1, 0)])]
    ppermute x7 -> x8, starting transfers between devices: 12.7 us -> 15.1 us  [z_swap(): return lax.ppermute(x, 'z', [(i, i ^ distance) for i in range(4)])]
    ppermute x7 -> x8, waiting for transfers between devices: 6.88 us -> 4.97 us  [z_swap(): return lax.ppermute(x, 'z', [(i, i ^ distance) for i in range(4)])]
    ppermute x1, starting transfers between devices: 3.83 us -> 2.65 us  [swap_body(): four_back = lax.ppermute(*gate('four_back', two_back), 'z', upward)]
  transfers between devices with their start and end apart: 25 -> 26, of which waited for: 14 -> 12; matrix products, arithmetic and copies ran while one was open for 5% -> 5% of each run, Pallas kernels for 7% -> 7%
where the time goes in v4:
time: 71.6 us; the launch traced here: 71.4 us
  starting transfers between devices  37.8 us (53%)
  waiting for transfers between devices  17.1 us (24%)
  Pallas kernels  11.4 us (16%)
  other arithmetic  3.27 us (5%)
  local copies, waits for them, and re-layouts  1.57 us (2%)
    ppermute x16, starting transfers between devices, swap(): return lax.ppermute(x, axis, [(0, 1), (1, 0)])  17.5 us
    ppermute x8, starting transfers between devices, z_swap(): return lax.ppermute(x, 'z', [(i, i ^ distance) for i in range(4)])  15.1 us
    ppermute x16, waiting for transfers between devices, swap(): return lax.ppermute(x, axis, [(0, 1), (1, 0)])  12.1 us
    pallas_call x1, Pallas kernels, attend(): pl.pallas_call(functools.partial(attend_kernel, earlier), out_shape=jax.S...  6.28 us
    ppermute x8, waiting for transfers between devices, z_swap(): return lax.ppermute(x, 'z', [(i, i ^ distance) for i in range(4)])  4.97 us
    pallas_call x2, Pallas kernels, order_features(): pl.pallas_call(functools.partial(order_kernel, order), out_shape=jax.Shap...  2.87 us
    ppermute x1, starting transfers between devices, swap_body(): four_back = lax.ppermute(*gate('four_back', two_back), 'z', upward)  2.65 us
    ppermute x1, starting transfers between devices, swap_body(): two_back = lax.ppermute(*gate('two_back', block), 'z', upward)  2.55 us
  transfers between devices with their start and end apart: 26, of which 12 were waited for; matrix products, arithmetic and copies ran while one was open for 5% of the time, Pallas kernels for 7%

profile of v4, /device:TPU:0, one launch (start us, length us, event | category | flops | bytes accessed | tf_op | source)
XLA Modules:
  0.0 71.4 jit_solution(15442041125531732674)
XLA Ops:
  1.1 3.1 %collective-permute-start.1 = (bf16[64,640]{1,0:T(8,128)(2,1)S(1)}, bf16[64,640]{1,0:T(8,128)(2,1)S(1)}, u32[]{:S(2)}, u32[]{:S(2)}) collective-permute-start(bf16[64,640]{1,0:T(8,128)(2,1)S(1)} %get-tuple-element.24.refs_0_), channel_id=1, source_target_pairs={{0,2},{2,0},{4,6},{6,4},{1,3},{3,1},{5,7},{7,5},{8,10},{10,8},{12,... | collective-permute-start | bytes 245768 | tf_op jit(solution)/shard_map/ppermute | solution.py:52
  4.2 2.6 %collective-permute-start.7 = (bf16[64,640]{1,0:T(8,128)(2,1)S(1)}, bf16[64,640]{1,0:T(8,128)(2,1)S(1)}, u32[]{:S(2)}, u32[]{:S(2)}) collective-permute-start(bf16[64,640]{1,0:T(8,128)(2,1)S(1)} %get-tuple-element.24.refs_0_), channel_id=1, source_target_pairs={{0,4},{2,6},{4,0},{6,2},{1,5},{3,7},{5,1},{7,3},{8,12},{10,14},{12... | collective-permute-start | bytes 245768 | tf_op jit(solution)/shard_map/ppermute | solution.py:52
  8.6 1.2 %fusion = f32[128]{0:T(128)S(1)} fusion(bf16[1,128,2048]{2,1,0:T(8,128)(2,1)} %param.5), kind=kLoop, calls=%fused_computation.2 | loop fusion | flops 786304 | bytes 524800 | tf_op jit(solution)/shard_map/reduce_sum | solution.py:43
  9.9 1.6 %collective-permute-start.2 = (bf16[64,640]{1,0:T(8,128)(2,1)S(1)}, bf16[64,640]{1,0:T(8,128)(2,1)S(1)}, u32[]{:S(2)}, u32[]{:S(2)}) collective-permute-start(bf16[64,640]{1,0:T(8,128)(2,1)S(1)} %get-tuple-element.24.refs_0_), channel_id=1, source_target_pairs={{0,16},{16,0},{1,17},{17,1},{2,18},{18,2},{3,19},{19,3},{4,20},{20... | collective-permute-start | bytes 245768 | tf_op jit(solution)/shard_map/ppermute | solution.py:48
  11.4 1.5 %collective-permute-start.3 = (bf16[64,640]{1,0:T(8,128)(2,1)S(1)}, bf16[64,640]{1,0:T(8,128)(2,1)S(1)}, u32[]{:S(2)}, u32[]{:S(2)}) collective-permute-start(bf16[64,640]{1,0:T(8,128)(2,1)S(1)} %get-tuple-element.24.refs_0_), channel_id=1, source_target_pairs={{0,1},{1,0},{2,3},{3,2},{4,5},{5,4},{6,7},{7,6},{8,9},{9,8},{10,11... | collective-permute-start | bytes 245768 | tf_op jit(solution)/shard_map/ppermute | solution.py:48
  14.4 1.5 %collective-permute-done.3.refs_2_ = bf16[64,640]{1,0:T(8,128)(2,1)S(1)} collective-permute-done((bf16[64,640]{1,0:T(8,128)(2,1)S(1)}, bf16[64,640]{1,0:T(8,128)(2,1)S(1)}, u32[]{:S(2)}, u32[]{:S(2)}) %collective-permute-start.3) | collective-permute-done | bytes 81952 | tf_op jit(solution)/shard_map/ppermute | solution.py:48
  15.9 1.6 %collective-permute-start.10 = (bf16[192,640]{1,0:T(8,128)(2,1)S(1)}, bf16[192,640]{1,0:T(8,128)(2,1)S(1)}, u32[]{:S(2)}, u32[]{:S(2)}) collective-permute-start(bf16[192,640]{1,0:T(8,128)(2,1)S(1)} %constant_dynamic-update-slice_fusion.refs_3_), channel_id=1, source_target_pairs={{0,1},{1,0},{2,3},{3,2},{4,5},{5,4},{6,7},{7,6},{8,9},{9,8},{10,11... | collective-permute-start | bytes 737288 | tf_op jit(solution)/shard_map/ppermute | solution.py:48
  18.7 3.0 %collective-permute-start.11 = (bf16[128,640]{1,0:T(8,128)(2,1)S(1)}, bf16[128,640]{1,0:T(8,128)(2,1)S(1)}, u32[]{:S(2)}, u32[]{:S(2)}) collective-permute-start(bf16[128,640]{1,0:T(8,128)(2,1)S(1)} %pad_maximum_fusion.2), channel_id=1, source_target_pairs={{0,4},{2,6},{4,0},{6,2},{1,5},{3,7},{5,1},{7,3},{8,12},{10,14},{12... | collective-permute-start | bytes 491528 | tf_op jit(solution)/shard_map/ppermute | solution.py:52
  24.3 1.6 %collective-permute-start.16 = (bf16[128,640]{1,0:T(8,128)(2,1)S(1)}, bf16[128,640]{1,0:T(8,128)(2,1)S(1)}, u32[]{:S(2)}, u32[]{:S(2)}) collective-permute-start(bf16[128,640]{1,0:T(8,128)(2,1)S(1)} %slice.25), channel_id=1, source_target_pairs={{0,16},{16,0},{1,17},{17,1},{2,18},{18,2},{3,19},{19,3},{4,20},{20... | collective-permute-start | bytes 491528 | tf_op jit(solution)/shard_map/ppermute | solution.py:48
  26.7 2.4 %collective-permute-done.15.refs_0_ = bf16[128,640]{1,0:T(8,128)(2,1)S(1)} collective-permute-done((bf16[128,640]{1,0:T(8,128)(2,1)S(1)}, bf16[128,640]{1,0:T(8,128)(2,1)S(1)}, u32[]{:S(2)}, u32[]{:S(2)}) %collective-permute-start.15) | collective-permute-done | bytes 163872 | tf_op jit(solution)/shard_map/ppermute | solution.py:48
  30.2 3.6 %collective-permute-start.14 = (bf16[128,640]{1,0:T(8,128)(2,1)S(1)}, bf16[128,640]{1,0:T(8,128)(2,1)S(1)}, u32[]{:S(2)}, u32[]{:S(2)}) collective-permute-start(bf16[128,640]{1,0:T(8,128)(2,1)S(1)} %pad_maximum_fusion.3), channel_id=1, source_target_pairs={{0,4},{2,6},{4,0},{6,2},{1,5},{3,7},{5,1},{7,3},{8,12},{10,14},{12... | collective-permute-start | bytes 491528 | tf_op jit(solution)/shard_map/ppermute | solution.py:52
  34.4 2.0 %collective-permute-start.13 = (bf16[256,640]{1,0:T(8,128)(2,1)S(1)}, bf16[256,640]{1,0:T(8,128)(2,1)S(1)}, u32[]{:S(2)}, u32[]{:S(2)}) collective-permute-start(bf16[256,640]{1,0:T(8,128)(2,1)S(1)} %pad_maximum_fusion.refs_0_), channel_id=1, source_target_pairs={{0,1},{1,0},{2,3},{3,2},{4,5},{5,4},{6,7},{7,6},{8,9},{9,8},{10,11... | collective-permute-start | bytes 983048 | tf_op jit(solution)/shard_map/ppermute | solution.py:48
  36.4 2.5 %collective-permute-start.18 = (bf16[136,640]{1,0:T(8,128)(2,1)S(1)}, bf16[136,640]{1,0:T(8,128)(2,1)S(1)}, u32[]{:S(2)}, u32[]{:S(2)}) collective-permute-start(bf16[136,640]{1,0:T(8,128)(2,1)S(1)} %fusion.5.refs_0_), channel_id=1, source_target_pairs={{0,2},{2,4},{4,6},{1,3},{3,5},{5,7},{8,10},{10,12},{12,14},{9,11},... | collective-permute-start | bytes 522248 | tf_op jit(solution)/shard_map/ppermute | solution.py:303
  39.0 3.1 %collective-permute-done.14 = bf16[128,640]{1,0:T(8,128)(2,1)S(1)} collective-permute-done((bf16[128,640]{1,0:T(8,128)(2,1)S(1)}, bf16[128,640]{1,0:T(8,128)(2,1)S(1)}, u32[]{:S(2)}, u32[]{:S(2)}) %collective-permute-start.14) | collective-permute-done | bytes 163872 | tf_op jit(solution)/shard_map/ppermute | solution.py:52
  42.1 1.8 %collective-permute-start.20 = (bf16[256,640]{1,0:T(8,128)(2,1)S(1)}, bf16[256,640]{1,0:T(8,128)(2,1)S(1)}, u32[]{:S(2)}, u32[]{:S(2)}) collective-permute-start(bf16[256,640]{1,0:T(8,128)(2,1)S(1)} %get-tuple-element.49), channel_id=1, source_target_pairs={{0,1},{1,0},{2,3},{3,2},{4,5},{5,4},{6,7},{7,6},{8,9},{9,8},{10,11... | collective-permute-start | bytes 983048 | tf_op jit(solution)/shard_map/ppermute | solution.py:48
  44.2 1.6 %collective-permute-start.22 = (bf16[256,640]{1,0:T(8,128)(2,1)S(1)}, bf16[256,640]{1,0:T(8,128)(2,1)S(1)}, u32[]{:S(2)}, u32[]{:S(2)}) collective-permute-start(bf16[256,640]{1,0:T(8,128)(2,1)S(1)} %collective-permute-done.13.refs_2_), channel_id=1, source_target_pairs={{0,16},{16,0},{1,17},{17,1},{2,18},{18,2},{3,19},{19,3},{4,20},{20... | collective-permute-start | bytes 983048 | tf_op jit(solution)/shard_map/ppermute | solution.py:48
  45.8 1.7 %collective-permute-start.21 = (bf16[136,640]{1,0:T(8,128)(2,1)S(1)}, bf16[136,640]{1,0:T(8,128)(2,1)S(1)}, u32[]{:S(2)}, u32[]{:S(2)}) collective-permute-start(bf16[136,640]{1,0:T(8,128)(2,1)S(1)} %collective-permute-done.18.refs_1_), channel_id=1, source_target_pairs={{0,1},{1,0},{2,3},{3,2},{4,5},{5,4},{6,7},{7,6},{8,9},{9,8},{10,11... | collective-permute-start | bytes 522248 | tf_op jit(solution)/shard_map/ppermute | solution.py:48
  47.5 1.7 %shard_map.55.features = bf16[512,1024]{1,0:T(8,128)(2,1)S(1)} custom-call(s32[5]{0:T(128)S(1)} %stack.51.bits, bf16[128,2048]{1,0:T(8,128)(2,1)S(1)} %fusion.2.refs_0_, bf16[128,2048]{1,0:T(8,128)(2,1)S(1)} %collective-permute-done.refs_1_, bf16[128,2048]{1,0:T(8,128)(2,1)S(1)} %collective-permute-done.4.refs_2_, ...), custom_call_target="tpu_custom_call" | custom-call | bytes 4194304 | tf_op jit(solution)/shard_map/pallas_call | solution.py:77
  49.3 2.7 %collective-permute-start.19 = (bf16[136,640]{1,0:T(8,128)(2,1)S(1)}, bf16[136,640]{1,0:T(8,128)(2,1)S(1)}, u32[]{:S(2)}, u32[]{:S(2)}) collective-permute-start(bf16[136,640]{1,0:T(8,128)(2,1)S(1)} %collective-permute-done.18.refs_1_), channel_id=1, source_target_pairs={{0,2},{2,4},{4,6},{1,3},{3,5},{5,7},{8,10},{10,12},{12,14},{9,11},... | collective-permute-start | bytes 522248 | tf_op jit(solution)/shard_map/ppermute | solution.py:307
  53.6 2.1 %collective-permute-done.21.refs_3_ = bf16[136,640]{1,0:T(8,128)(2,1)S(1)} collective-permute-done((bf16[136,640]{1,0:T(8,128)(2,1)S(1)}, bf16[136,640]{1,0:T(8,128)(2,1)S(1)}, u32[]{:S(2)}, u32[]{:S(2)}) %collective-permute-start.21) | collective-permute-done | bytes 174112 | tf_op jit(solution)/shard_map/ppermute | solution.py:48
  56.9 1.7 %collective-permute-start.25 = (bf16[136,640]{1,0:T(8,128)(2,1)}, bf16[136,640]{1,0:T(8,128)(2,1)S(1)}, u32[]{:S(2)}, u32[]{:S(2)}) collective-permute-start(bf16[136,640]{1,0:T(8,128)(2,1)} %broadcast_select_fusion), channel_id=1, source_target_pairs={{0,1},{1,0},{2,3},{3,2},{4,5},{5,4},{6,7},{7,6},{8,9},{9,8},{10,11... | collective-permute-start | bytes 522248 | tf_op jit(solution)/shard_map/ppermute | solution.py:48
  58.7 1.4 %collective-permute-start.24 = (bf16[128,640]{1,0:T(8,128)(2,1)S(1)}, bf16[128,640]{1,0:T(8,128)(2,1)S(1)}, u32[]{:S(2)}, u32[]{:S(2)}) collective-permute-start(bf16[128,640]{1,0:T(8,128)(2,1)S(1)} %get-tuple-element.42), channel_id=1, source_target_pairs={{0,2},{2,0},{4,6},{6,4},{1,3},{3,1},{5,7},{7,5},{8,10},{10,8},{12,... | collective-permute-start | bytes 491528 | tf_op jit(solution)/shard_map/ppermute | solution.py:52
  60.3 3.6 %collective-permute-done.25.refs_4_ = bf16[136,640]{1,0:T(8,128)(2,1)S(1)} collective-permute-done((bf16[136,640]{1,0:T(8,128)(2,1)}, bf16[136,640]{1,0:T(8,128)(2,1)S(1)}, u32[]{:S(2)}, u32[]{:S(2)}) %collective-permute-start.25) | collective-permute-done | bytes 174112 | tf_op jit(solution)/shard_map/ppermute | solution.py:48
  65.1 6.3 %shard_map.61 = bf16[128,1280]{1,0:T(8,128)(2,1)} custom-call(s32[6]{0:T(128)S(1)} %stack.45.scalars, bf16[128,640]{1,0:T(8,128)(2,1)S(1)} %get-tuple-element.44.mine, bf16[128,640]{1,0:T(8,128)(2,1)S(1)} %collective-permute-done.24.pair, bf16[512,640]{1,0:T(8,128)(2,1)S(1)} %constant_dynamic-update-slice_fusion.5.prefix, f32[128,1]{1,0:T(8,128)S(1)} %copy.6.seg_col, ...), custom_call_target="tpu_custom_call" | custom-call | flops 754974720 | bytes 1474560 | tf_op jit(solution)/shard_map/pallas_call | solution.py:188
  (71 shorter events, 15.2 us)
Async XLA Ops:
  1.1 8.8 %collective-permute-start.1 = (bf16[64,640]{1,0:T(8,128)(2,1)S(1)}, bf16[64,640]{1,0:T(8,128)(2,1)S(1)}, u32[]{:S(2)}, u32[]{:S(2)}) collective-permute-start(bf16[64,640]{1,0:T(8,128)(2,1)S(1)} %get-tuple-element.24.refs_0_), channel_id=1, source_target_pairs={{0,2},{2,0},{4,6},{6,4},{1,3},{3,1},{5,7},{7,5},{8,10},{10,8},{12,... | collective-permute-start | bytes 245768 | tf_op jit(solution)/shard_map/ppermute | solution.py:52
  4.2 9.1 %collective-permute-start.7 = (bf16[64,640]{1,0:T(8,128)(2,1)S(1)}, bf16[64,640]{1,0:T(8,128)(2,1)S(1)}, u32[]{:S(2)}, u32[]{:S(2)}) collective-permute-start(bf16[64,640]{1,0:T(8,128)(2,1)S(1)} %get-tuple-element.24.refs_0_), channel_id=1, source_target_pairs={{0,4},{2,6},{4,0},{6,2},{1,5},{3,7},{5,1},{7,3},{8,12},{10,14},{12... | collective-permute-start | bytes 245768 | tf_op jit(solution)/shard_map/ppermute | solution.py:52
  6.7 7.2 %collective-permute-start.8 = (bf16[64,640]{1,0:T(8,128)(2,1)S(1)}, bf16[64,640]{1,0:T(8,128)(2,1)S(1)}, u32[]{:S(2)}, u32[]{:S(2)}) collective-permute-start(bf16[64,640]{1,0:T(8,128)(2,1)S(1)} %get-tuple-element.24.refs_0_), channel_id=1, source_target_pairs={{0,6},{2,4},{4,2},{6,0},{1,7},{3,5},{5,3},{7,1},{8,14},{10,12},{12... | collective-permute-start | bytes 245768 | tf_op jit(solution)/shard_map/ppermute | solution.py:52
  7.7 8.2 %collective-permute-start.6 = (bf16[128,640]{1,0:T(8,128)(2,1)S(1)}, bf16[128,640]{1,0:T(8,128)(2,1)S(1)}, u32[]{:S(2)}, u32[]{:S(2)}) collective-permute-start(bf16[128,640]{1,0:T(8,128)(2,1)S(1)} %pad_maximum_fusion.1), channel_id=1, source_target_pairs={{0,2},{2,0},{4,6},{6,4},{1,3},{3,1},{5,7},{7,5},{8,10},{10,8},{12,... | collective-permute-start | bytes 491528 | tf_op jit(solution)/shard_map/ppermute | solution.py:52
  9.9 4.5 %collective-permute-start.2 = (bf16[64,640]{1,0:T(8,128)(2,1)S(1)}, bf16[64,640]{1,0:T(8,128)(2,1)S(1)}, u32[]{:S(2)}, u32[]{:S(2)}) collective-permute-start(bf16[64,640]{1,0:T(8,128)(2,1)S(1)} %get-tuple-element.24.refs_0_), channel_id=1, source_target_pairs={{0,16},{16,0},{1,17},{17,1},{2,18},{18,2},{3,19},{19,3},{4,20},{20... | collective-permute-start | bytes 245768 | tf_op jit(solution)/shard_map/ppermute | solution.py:48
  13.3 8.9 %collective-permute-start = (bf16[128,2048]{1,0:T(8,128)(2,1)S(1)}, bf16[128,2048]{1,0:T(8,128)(2,1)S(1)}, u32[]{:S(2)}, u32[]{:S(2)}) collective-permute-start(bf16[128,2048]{1,0:T(8,128)(2,1)S(1)} %fusion.2.refs_0_), channel_id=1, source_target_pairs={{0,8},{8,0},{1,9},{9,1},{2,10},{10,2},{3,11},{11,3},{4,12},{12,4},... | collective-permute-start | bytes 1572872 | tf_op jit(solution)/shard_map/ppermute | solution.py:48
  15.9 7.4 %collective-permute-start.10 = (bf16[192,640]{1,0:T(8,128)(2,1)S(1)}, bf16[192,640]{1,0:T(8,128)(2,1)S(1)}, u32[]{:S(2)}, u32[]{:S(2)}) collective-permute-start(bf16[192,640]{1,0:T(8,128)(2,1)S(1)} %constant_dynamic-update-slice_fusion.refs_3_), channel_id=1, source_target_pairs={{0,1},{1,0},{2,3},{3,2},{4,5},{5,4},{6,7},{7,6},{8,9},{9,8},{10,11... | collective-permute-start | bytes 737288 | tf_op jit(solution)/shard_map/ppermute | solution.py:48
  17.5 6.2 %collective-permute-start.9 = (bf16[192,640]{1,0:T(8,128)(2,1)S(1)}, bf16[192,640]{1,0:T(8,128)(2,1)S(1)}, u32[]{:S(2)}, u32[]{:S(2)}) collective-permute-start(bf16[192,640]{1,0:T(8,128)(2,1)S(1)} %constant_dynamic-update-slice_fusion.refs_3_), channel_id=1, source_target_pairs={{0,16},{16,0},{1,17},{17,1},{2,18},{18,2},{3,19},{19,3},{4,20},{20... | collective-permute-start | bytes 737288 | tf_op jit(solution)/shard_map/ppermute | solution.py:48
  18.7 11.5 %collective-permute-start.11 = (bf16[128,640]{1,0:T(8,128)(2,1)S(1)}, bf16[128,640]{1,0:T(8,128)(2,1)S(1)}, u32[]{:S(2)}, u32[]{:S(2)}) collective-permute-start(bf16[128,640]{1,0:T(8,128)(2,1)S(1)} %pad_maximum_fusion.2), channel_id=1, source_target_pairs={{0,4},{2,6},{4,0},{6,2},{1,5},{3,7},{5,1},{7,3},{8,12},{10,14},{12... | collective-permute-start | bytes 491528 | tf_op jit(solution)/shard_map/ppermute | solution.py:52
  21.7 14.7 %collective-permute-start.4 = (bf16[128,2048]{1,0:T(8,128)(2,1)S(1)}, bf16[128,2048]{1,0:T(8,128)(2,1)S(1)}, u32[]{:S(2)}, u32[]{:S(2)}) collective-permute-start(bf16[128,2048]{1,0:T(8,128)(2,1)S(1)} %fusion.2.refs_0_), channel_id=1, source_target_pairs={{0,2},{2,0},{4,6},{6,4},{1,3},{3,1},{5,7},{7,5},{8,10},{10,8},{12,... | collective-permute-start | bytes 1572872 | tf_op jit(solution)/shard_map/ppermute | solution.py:52
  23.8 5.4 %collective-permute-start.15 = (bf16[128,640]{1,0:T(8,128)(2,1)S(1)}, bf16[128,640]{1,0:T(8,128)(2,1)S(1)}, u32[]{:S(2)}, u32[]{:S(2)}) collective-permute-start(bf16[128,640]{1,0:T(8,128)(2,1)S(1)} %pad_maximum_fusion.4), channel_id=1, source_target_pairs={{0,1},{1,0},{2,3},{3,2},{4,5},{5,4},{6,7},{7,6},{8,9},{9,8},{10,11... | collective-permute-start | bytes 491528 | tf_op jit(solution)/shard_map/ppermute | solution.py:48
  24.3 5.4 %collective-permute-start.16 = (bf16[128,640]{1,0:T(8,128)(2,1)S(1)}, bf16[128,640]{1,0:T(8,128)(2,1)S(1)}, u32[]{:S(2)}, u32[]{:S(2)}) collective-permute-start(bf16[128,640]{1,0:T(8,128)(2,1)S(1)} %slice.25), channel_id=1, source_target_pairs={{0,16},{16,0},{1,17},{17,1},{2,18},{18,2},{3,19},{19,3},{4,20},{20... | collective-permute-start | bytes 491528 | tf_op jit(solution)/shard_map/ppermute | solution.py:48
  30.1 6.3 %collective-permute-start.17 = (f32[128,640]{1,0:T(8,128)S(1)}, f32[128,640]{1,0:T(8,128)S(1)}, u32[]{:S(2)}, u32[]{:S(2)}) collective-permute-start(f32[128,640]{1,0:T(8,128)S(1)} %get-tuple-element.36), channel_id=1, source_target_pairs={{0,8},{8,0},{1,9},{9,1},{2,10},{10,2},{3,11},{11,3},{4,12},{12,4},... | collective-permute-start | bytes 983048 | tf_op jit(solution)/shard_map/ppermute | solution.py:48
  30.2 11.9 %collective-permute-start.14 = (bf16[128,640]{1,0:T(8,128)(2,1)S(1)}, bf16[128,640]{1,0:T(8,128)(2,1)S(1)}, u32[]{:S(2)}, u32[]{:S(2)}) collective-permute-start(bf16[128,640]{1,0:T(8,128)(2,1)S(1)} %pad_maximum_fusion.3), channel_id=1, source_target_pairs={{0,4},{2,6},{4,0},{6,2},{1,5},{3,7},{5,1},{7,3},{8,12},{10,14},{12... | collective-permute-start | bytes 491528 | tf_op jit(solution)/shard_map/ppermute | solution.py:52
  33.8 10.2 %collective-permute-start.12 = (bf16[256,640]{1,0:T(8,128)(2,1)S(1)}, bf16[256,640]{1,0:T(8,128)(2,1)S(1)}, u32[]{:S(2)}, u32[]{:S(2)}) collective-permute-start(bf16[256,640]{1,0:T(8,128)(2,1)S(1)} %pad_maximum_fusion.refs_0_), channel_id=1, source_target_pairs={{0,16},{16,0},{1,17},{17,1},{2,18},{18,2},{3,19},{19,3},{4,20},{20... | collective-permute-start | bytes 983048 | tf_op jit(solution)/shard_map/ppermute | solution.py:48
  34.4 9.8 %collective-permute-start.13 = (bf16[256,640]{1,0:T(8,128)(2,1)S(1)}, bf16[256,640]{1,0:T(8,128)(2,1)S(1)}, u32[]{:S(2)}, u32[]{:S(2)}) collective-permute-start(bf16[256,640]{1,0:T(8,128)(2,1)S(1)} %pad_maximum_fusion.refs_0_), channel_id=1, source_target_pairs={{0,1},{1,0},{2,3},{3,2},{4,5},{5,4},{6,7},{7,6},{8,9},{9,8},{10,11... | collective-permute-start | bytes 983048 | tf_op jit(solution)/shard_map/ppermute | solution.py:48
  36.4 11.2 %collective-permute-start.5 = (bf16[128,2048]{1,0:T(8,128)(2,1)S(1)}, bf16[128,2048]{1,0:T(8,128)(2,1)S(1)}, u32[]{:S(2)}, u32[]{:S(2)}) collective-permute-start(bf16[128,2048]{1,0:T(8,128)(2,1)S(1)} %collective-permute-done.4.refs_2_), channel_id=1, source_target_pairs={{0,8},{8,0},{1,9},{9,1},{2,10},{10,2},{3,11},{11,3},{4,12},{12,4},... | collective-permute-start | bytes 1572872 | tf_op jit(solution)/shard_map/ppermute | solution.py:48
  36.4 7.7 %collective-permute-start.18 = (bf16[136,640]{1,0:T(8,128)(2,1)S(1)}, bf16[136,640]{1,0:T(8,128)(2,1)S(1)}, u32[]{:S(2)}, u32[]{:S(2)}) collective-permute-start(bf16[136,640]{1,0:T(8,128)(2,1)S(1)} %fusion.5.refs_0_), channel_id=1, source_target_pairs={{0,2},{2,4},{4,6},{1,3},{3,5},{5,7},{8,10},{10,12},{12,14},{9,11},... | collective-permute-start | bytes 522248 | tf_op jit(solution)/shard_map/ppermute | solution.py:303
  42.1 10.6 %collective-permute-start.20 = (bf16[256,640]{1,0:T(8,128)(2,1)S(1)}, bf16[256,640]{1,0:T(8,128)(2,1)S(1)}, u32[]{:S(2)}, u32[]{:S(2)}) collective-permute-start(bf16[256,640]{1,0:T(8,128)(2,1)S(1)} %get-tuple-element.49), channel_id=1, source_target_pairs={{0,1},{1,0},{2,3},{3,2},{4,5},{5,4},{6,7},{7,6},{8,9},{9,8},{10,11... | collective-permute-start | bytes 983048 | tf_op jit(solution)/shard_map/ppermute | solution.py:48
  44.2 11.5 %collective-permute-start.22 = (bf16[256,640]{1,0:T(8,128)(2,1)S(1)}, bf16[256,640]{1,0:T(8,128)(2,1)S(1)}, u32[]{:S(2)}, u32[]{:S(2)}) collective-permute-start(bf16[256,640]{1,0:T(8,128)(2,1)S(1)} %collective-permute-done.13.refs_2_), channel_id=1, source_target_pairs={{0,16},{16,0},{1,17},{17,1},{2,18},{18,2},{3,19},{19,3},{4,20},{20... | collective-permute-start | bytes 983048 | tf_op jit(solution)/shard_map/ppermute | solution.py:48
  45.8 9.9 %collective-permute-start.21 = (bf16[136,640]{1,0:T(8,128)(2,1)S(1)}, bf16[136,640]{1,0:T(8,128)(2,1)S(1)}, u32[]{:S(2)}, u32[]{:S(2)}) collective-permute-start(bf16[136,640]{1,0:T(8,128)(2,1)S(1)} %collective-permute-done.18.refs_1_), channel_id=1, source_target_pairs={{0,1},{1,0},{2,3},{3,2},{4,5},{5,4},{6,7},{7,6},{8,9},{9,8},{10,11... | collective-permute-start | bytes 522248 | tf_op jit(solution)/shard_map/ppermute | solution.py:48
  49.3 6.4 %collective-permute-start.19 = (bf16[136,640]{1,0:T(8,128)(2,1)S(1)}, bf16[136,640]{1,0:T(8,128)(2,1)S(1)}, u32[]{:S(2)}, u32[]{:S(2)}) collective-permute-start(bf16[136,640]{1,0:T(8,128)(2,1)S(1)} %collective-permute-done.18.refs_1_), channel_id=1, source_target_pairs={{0,2},{2,4},{4,6},{1,3},{3,5},{5,7},{8,10},{10,12},{12,14},{9,11},... | collective-permute-start | bytes 522248 | tf_op jit(solution)/shard_map/ppermute | solution.py:307
  56.9 7.0 %collective-permute-start.25 = (bf16[136,640]{1,0:T(8,128)(2,1)}, bf16[136,640]{1,0:T(8,128)(2,1)S(1)}, u32[]{:S(2)}, u32[]{:S(2)}) collective-permute-start(bf16[136,640]{1,0:T(8,128)(2,1)} %broadcast_select_fusion), channel_id=1, source_target_pairs={{0,1},{1,0},{2,3},{3,2},{4,5},{5,4},{6,7},{7,6},{8,9},{9,8},{10,11... | collective-permute-start | bytes 522248 | tf_op jit(solution)/shard_map/ppermute | solution.py:48
  58.7 6.4 %collective-permute-start.24 = (bf16[128,640]{1,0:T(8,128)(2,1)S(1)}, bf16[128,640]{1,0:T(8,128)(2,1)S(1)}, u32[]{:S(2)}, u32[]{:S(2)}) collective-permute-start(bf16[128,640]{1,0:T(8,128)(2,1)S(1)} %get-tuple-element.42), channel_id=1, source_target_pairs={{0,2},{2,0},{4,6},{6,4},{1,3},{3,1},{5,7},{7,5},{8,10},{10,8},{12,... | collective-permute-start | bytes 491528 | tf_op jit(solution)/shard_map/ppermute | solution.py:52
  (6 other events, 41.3 us)

commit v5 on v4

--- a/solution.py
+++ b/solution.py
@@ -22,12 +22,11 @@
 ORDER = {
     "kv_near_sides": ("kv_z0",),
     "kv_far": ("kv_near_sides", "kv_features", "q_got",),
-    "norm": ("kv_near",),
     "q_across": ("kv_far",),
     "normed_pair": ("kv_near_sides",),
     "kv_corner": ("kv_features",),
     "q_line": ("kv_far_sides",),
-    "q_res": ("four_back",),
+    "q_res": ("four_back", "odd_a",),
     "prefix_z1": ("kv_far_sides",),
     "prefix_z2": ("q_across",),
     "q_corner": ("two_back",),

time: 71.6 us -> 71.6 us (level)
  no operation moved by 1% of the time
where the time goes in v5:
time: 71.6 us; the launch traced here: 71.4 us
  starting transfers between devices  37.8 us (53%)
  waiting for transfers between devices  17.1 us (24%)
  Pallas kernels  11.4 us (16%)
  other arithmetic  3.27 us (5%)
  local copies, waits for them, and re-layouts  1.57 us (2%)
    ppermute x16, starting transfers between devices, swap(): return lax.ppermute(x, axis, [(0, 1), (1, 0)])  17.5 us
    ppermute x8, starting transfers between devices, z_swap(): return lax.ppermute(x, 'z', [(i, i ^ distance) for i in range(4)])  15.1 us
    ppermute x16, waiting for transfers between devices, swap(): return lax.ppermute(x, axis, [(0, 1), (1, 0)])  12.1 us
    pallas_call x1, Pallas kernels, attend(): pl.pallas_call(functools.partial(attend_kernel, earlier), out_shape=jax.S...  6.28 us
    ppermute x8, waiting for transfers between devices, z_swap(): return lax.ppermute(x, 'z', [(i, i ^ distance) for i in range(4)])  4.97 us
    pallas_call x2, Pallas kernels, order_features(): pl.pallas_call(functools.partial(order_kernel, order), out_shape=jax.Shap...  2.87 us
    ppermute x1, starting transfers between devices, swap_body(): four_back = lax.ppermute(*gate('four_back', two_back), 'z', upward)  2.65 us
    ppermute x1, starting transfers between devices, swap_body(): two_back = lax.ppermute(*gate('two_back', block), 'z', upward)  2.55 us
  transfers between devices with their start and end apart: 26, of which 12 were waited for; matrix products, arithmetic and copies ran while one was open for 5% of the time, Pallas kernels for 7%

profile of v5, /device:TPU:0, one launch (start us, length us, event | category | flops | bytes accessed | tf_op | source)
XLA Modules:
  0.0 71.4 jit_solution(15442041125531732674)
XLA Ops:
  1.1 3.1 %collective-permute-start.1 = (bf16[64,640]{1,0:T(8,128)(2,1)S(1)}, bf16[64,640]{1,0:T(8,128)(2,1)S(1)}, u32[]{:S(2)}, u32[]{:S(2)}) collective-permute-start(bf16[64,640]{1,0:T(8,128)(2,1)S(1)} %get-tuple-element.24.refs_0_), channel_id=1, source_target_pairs={{0,2},{2,0},{4,6},{6,4},{1,3},{3,1},{5,7},{7,5},{8,10},{10,8},{12,... | collective-permute-start | bytes 245768 | tf_op jit(solution)/shard_map/ppermute | solution.py:51
  4.2 2.6 %collective-permute-start.7 = (bf16[64,640]{1,0:T(8,128)(2,1)S(1)}, bf16[64,640]{1,0:T(8,128)(2,1)S(1)}, u32[]{:S(2)}, u32[]{:S(2)}) collective-permute-start(bf16[64,640]{1,0:T(8,128)(2,1)S(1)} %get-tuple-element.24.refs_0_), channel_id=1, source_target_pairs={{0,4},{2,6},{4,0},{6,2},{1,5},{3,7},{5,1},{7,3},{8,12},{10,14},{12... | collective-permute-start | bytes 245768 | tf_op jit(solution)/shard_map/ppermute | solution.py:51
  8.6 1.2 %fusion = f32[128]{0:T(128)S(1)} fusion(bf16[1,128,2048]{2,1,0:T(8,128)(2,1)} %param.5), kind=kLoop, calls=%fused_computation.2 | loop fusion | flops 786304 | bytes 524800 | tf_op jit(solution)/shard_map/reduce_sum | solution.py:42
  9.9 1.6 %collective-permute-start.2 = (bf16[64,640]{1,0:T(8,128)(2,1)S(1)}, bf16[64,640]{1,0:T(8,128)(2,1)S(1)}, u32[]{:S(2)}, u32[]{:S(2)}) collective-permute-start(bf16[64,640]{1,0:T(8,128)(2,1)S(1)} %get-tuple-element.24.refs_0_), channel_id=1, source_target_pairs={{0,16},{16,0},{1,17},{17,1},{2,18},{18,2},{3,19},{19,3},{4,20},{20... | collective-permute-start | bytes 245768 | tf_op jit(solution)/shard_map/ppermute | solution.py:47
  11.4 1.5 %collective-permute-start.3 = (bf16[64,640]{1,0:T(8,128)(2,1)S(1)}, bf16[64,640]{1,0:T(8,128)(2,1)S(1)}, u32[]{:S(2)}, u32[]{:S(2)}) collective-permute-start(bf16[64,640]{1,0:T(8,128)(2,1)S(1)} %get-tuple-element.24.refs_0_), channel_id=1, source_target_pairs={{0,1},{1,0},{2,3},{3,2},{4,5},{5,4},{6,7},{7,6},{8,9},{9,8},{10,11... | collective-permute-start | bytes 245768 | tf_op jit(solution)/shard_map/ppermute | solution.py:47
  14.4 1.5 %collective-permute-done.3.refs_2_ = bf16[64,640]{1,0:T(8,128)(2,1)S(1)} collective-permute-done((bf16[64,640]{1,0:T(8,128)(2,1)S(1)}, bf16[64,640]{1,0:T(8,128)(2,1)S(1)}, u32[]{:S(2)}, u32[]{:S(2)}) %collective-permute-start.3) | collective-permute-done | bytes 81952 | tf_op jit(solution)/shard_map/ppermute | solution.py:47
  15.9 1.6 %collective-permute-start.10 = (bf16[192,640]{1,0:T(8,128)(2,1)S(1)}, bf16[192,640]{1,0:T(8,128)(2,1)S(1)}, u32[]{:S(2)}, u32[]{:S(2)}) collective-permute-start(bf16[192,640]{1,0:T(8,128)(2,1)S(1)} %constant_dynamic-update-slice_fusion.refs_3_), channel_id=1, source_target_pairs={{0,1},{1,0},{2,3},{3,2},{4,5},{5,4},{6,7},{7,6},{8,9},{9,8},{10,11... | collective-permute-start | bytes 737288 | tf_op jit(solution)/shard_map/ppermute | solution.py:47
  18.7 3.0 %collective-permute-start.11 = (bf16[128,640]{1,0:T(8,128)(2,1)S(1)}, bf16[128,640]{1,0:T(8,128)(2,1)S(1)}, u32[]{:S(2)}, u32[]{:S(2)}) collective-permute-start(bf16[128,640]{1,0:T(8,128)(2,1)S(1)} %pad_maximum_fusion.2), channel_id=1, source_target_pairs={{0,4},{2,6},{4,0},{6,2},{1,5},{3,7},{5,1},{7,3},{8,12},{10,14},{12... | collective-permute-start | bytes 491528 | tf_op jit(solution)/shard_map/ppermute | solution.py:51
  24.3 1.6 %collective-permute-start.16 = (bf16[128,640]{1,0:T(8,128)(2,1)S(1)}, bf16[128,640]{1,0:T(8,128)(2,1)S(1)}, u32[]{:S(2)}, u32[]{:S(2)}) collective-permute-start(bf16[128,640]{1,0:T(8,128)(2,1)S(1)} %slice.25), channel_id=1, source_target_pairs={{0,16},{16,0},{1,17},{17,1},{2,18},{18,2},{3,19},{19,3},{4,20},{20... | collective-permute-start | bytes 491528 | tf_op jit(solution)/shard_map/ppermute | solution.py:47
  26.7 2.4 %collective-permute-done.15.refs_0_ = bf16[128,640]{1,0:T(8,128)(2,1)S(1)} collective-permute-done((bf16[128,640]{1,0:T(8,128)(2,1)S(1)}, bf16[128,640]{1,0:T(8,128)(2,1)S(1)}, u32[]{:S(2)}, u32[]{:S(2)}) %collective-permute-start.15) | collective-permute-done | bytes 163872 | tf_op jit(solution)/shard_map/ppermute | solution.py:47
  30.2 3.6 %collective-permute-start.14 = (bf16[128,640]{1,0:T(8,128)(2,1)S(1)}, bf16[128,640]{1,0:T(8,128)(2,1)S(1)}, u32[]{:S(2)}, u32[]{:S(2)}) collective-permute-start(bf16[128,640]{1,0:T(8,128)(2,1)S(1)} %pad_maximum_fusion.3), channel_id=1, source_target_pairs={{0,4},{2,6},{4,0},{6,2},{1,5},{3,7},{5,1},{7,3},{8,12},{10,14},{12... | collective-permute-start | bytes 491528 | tf_op jit(solution)/shard_map/ppermute | solution.py:51
  34.4 2.0 %collective-permute-start.13 = (bf16[256,640]{1,0:T(8,128)(2,1)S(1)}, bf16[256,640]{1,0:T(8,128)(2,1)S(1)}, u32[]{:S(2)}, u32[]{:S(2)}) collective-permute-start(bf16[256,640]{1,0:T(8,128)(2,1)S(1)} %pad_maximum_fusion.refs_0_), channel_id=1, source_target_pairs={{0,1},{1,0},{2,3},{3,2},{4,5},{5,4},{6,7},{7,6},{8,9},{9,8},{10,11... | collective-permute-start | bytes 983048 | tf_op jit(solution)/shard_map/ppermute | solution.py:47
  36.4 2.5 %collective-permute-start.18 = (bf16[136,640]{1,0:T(8,128)(2,1)S(1)}, bf16[136,640]{1,0:T(8,128)(2,1)S(1)}, u32[]{:S(2)}, u32[]{:S(2)}) collective-permute-start(bf16[136,640]{1,0:T(8,128)(2,1)S(1)} %fusion.5.refs_0_), channel_id=1, source_target_pairs={{0,2},{2,4},{4,6},{1,3},{3,5},{5,7},{8,10},{10,12},{12,14},{9,11},... | collective-permute-start | bytes 522248 | tf_op jit(solution)/shard_map/ppermute | solution.py:302
  39.0 3.1 %collective-permute-done.14 = bf16[128,640]{1,0:T(8,128)(2,1)S(1)} collective-permute-done((bf16[128,640]{1,0:T(8,128)(2,1)S(1)}, bf16[128,640]{1,0:T(8,128)(2,1)S(1)}, u32[]{:S(2)}, u32[]{:S(2)}) %collective-permute-start.14) | collective-permute-done | bytes 163872 | tf_op jit(solution)/shard_map/ppermute | solution.py:51
  42.1 1.8 %collective-permute-start.20 = (bf16[256,640]{1,0:T(8,128)(2,1)S(1)}, bf16[256,640]{1,0:T(8,128)(2,1)S(1)}, u32[]{:S(2)}, u32[]{:S(2)}) collective-permute-start(bf16[256,640]{1,0:T(8,128)(2,1)S(1)} %get-tuple-element.49), channel_id=1, source_target_pairs={{0,1},{1,0},{2,3},{3,2},{4,5},{5,4},{6,7},{7,6},{8,9},{9,8},{10,11... | collective-permute-start | bytes 983048 | tf_op jit(solution)/shard_map/ppermute | solution.py:47
  44.2 1.6 %collective-permute-start.22 = (bf16[256,640]{1,0:T(8,128)(2,1)S(1)}, bf16[256,640]{1,0:T(8,128)(2,1)S(1)}, u32[]{:S(2)}, u32[]{:S(2)}) collective-permute-start(bf16[256,640]{1,0:T(8,128)(2,1)S(1)} %collective-permute-done.13.refs_2_), channel_id=1, source_target_pairs={{0,16},{16,0},{1,17},{17,1},{2,18},{18,2},{3,19},{19,3},{4,20},{20... | collective-permute-start | bytes 983048 | tf_op jit(solution)/shard_map/ppermute | solution.py:47
  45.8 1.7 %collective-permute-start.21 = (bf16[136,640]{1,0:T(8,128)(2,1)S(1)}, bf16[136,640]{1,0:T(8,128)(2,1)S(1)}, u32[]{:S(2)}, u32[]{:S(2)}) collective-permute-start(bf16[136,640]{1,0:T(8,128)(2,1)S(1)} %collective-permute-done.18.refs_1_), channel_id=1, source_target_pairs={{0,1},{1,0},{2,3},{3,2},{4,5},{5,4},{6,7},{7,6},{8,9},{9,8},{10,11... | collective-permute-start | bytes 522248 | tf_op jit(solution)/shard_map/ppermute | solution.py:47
  47.5 1.7 %shard_map.55.features = bf16[512,1024]{1,0:T(8,128)(2,1)S(1)} custom-call(s32[5]{0:T(128)S(1)} %stack.51.bits, bf16[128,2048]{1,0:T(8,128)(2,1)S(1)} %fusion.2.refs_0_, bf16[128,2048]{1,0:T(8,128)(2,1)S(1)} %collective-permute-done.refs_1_, bf16[128,2048]{1,0:T(8,128)(2,1)S(1)} %collective-permute-done.4.refs_2_, ...), custom_call_target="tpu_custom_call" | custom-call | bytes 4194304 | tf_op jit(solution)/shard_map/pallas_call | solution.py:76
  49.3 2.7 %collective-permute-start.19 = (bf16[136,640]{1,0:T(8,128)(2,1)S(1)}, bf16[136,640]{1,0:T(8,128)(2,1)S(1)}, u32[]{:S(2)}, u32[]{:S(2)}) collective-permute-start(bf16[136,640]{1,0:T(8,128)(2,1)S(1)} %collective-permute-done.18.refs_1_), channel_id=1, source_target_pairs={{0,2},{2,4},{4,6},{1,3},{3,5},{5,7},{8,10},{10,12},{12,14},{9,11},... | collective-permute-start | bytes 522248 | tf_op jit(solution)/shard_map/ppermute | solution.py:306
  53.6 2.1 %collective-permute-done.21.refs_3_ = bf16[136,640]{1,0:T(8,128)(2,1)S(1)} collective-permute-done((bf16[136,640]{1,0:T(8,128)(2,1)S(1)}, bf16[136,640]{1,0:T(8,128)(2,1)S(1)}, u32[]{:S(2)}, u32[]{:S(2)}) %collective-permute-start.21) | collective-permute-done | bytes 174112 | tf_op jit(solution)/shard_map/ppermute | solution.py:47
  56.9 1.7 %collective-permute-start.25 = (bf16[136,640]{1,0:T(8,128)(2,1)}, bf16[136,640]{1,0:T(8,128)(2,1)S(1)}, u32[]{:S(2)}, u32[]{:S(2)}) collective-permute-start(bf16[136,640]{1,0:T(8,128)(2,1)} %broadcast_select_fusion), channel_id=1, source_target_pairs={{0,1},{1,0},{2,3},{3,2},{4,5},{5,4},{6,7},{7,6},{8,9},{9,8},{10,11... | collective-permute-start | bytes 522248 | tf_op jit(solution)/shard_map/ppermute | solution.py:47
  58.7 1.4 %collective-permute-start.24 = (bf16[128,640]{1,0:T(8,128)(2,1)S(1)}, bf16[128,640]{1,0:T(8,128)(2,1)S(1)}, u32[]{:S(2)}, u32[]{:S(2)}) collective-permute-start(bf16[128,640]{1,0:T(8,128)(2,1)S(1)} %get-tuple-element.42), channel_id=1, source_target_pairs={{0,2},{2,0},{4,6},{6,4},{1,3},{3,1},{5,7},{7,5},{8,10},{10,8},{12,... | collective-permute-start | bytes 491528 | tf_op jit(solution)/shard_map/ppermute | solution.py:51
  60.3 3.6 %collective-permute-done.25.refs_4_ = bf16[136,640]{1,0:T(8,128)(2,1)S(1)} collective-permute-done((bf16[136,640]{1,0:T(8,128)(2,1)}, bf16[136,640]{1,0:T(8,128)(2,1)S(1)}, u32[]{:S(2)}, u32[]{:S(2)}) %collective-permute-start.25) | collective-permute-done | bytes 174112 | tf_op jit(solution)/shard_map/ppermute | solution.py:47
  65.1 6.3 %shard_map.61 = bf16[128,1280]{1,0:T(8,128)(2,1)} custom-call(s32[6]{0:T(128)S(1)} %stack.45.scalars, bf16[128,640]{1,0:T(8,128)(2,1)S(1)} %get-tuple-element.44.mine, bf16[128,640]{1,0:T(8,128)(2,1)S(1)} %collective-permute-done.24.pair, bf16[512,640]{1,0:T(8,128)(2,1)S(1)} %constant_dynamic-update-slice_fusion.5.prefix, f32[128,1]{1,0:T(8,128)S(1)} %copy.6.seg_col, ...), custom_call_target="tpu_custom_call" | custom-call | flops 754974720 | bytes 1474560 | tf_op jit(solution)/shard_map/pallas_call | solution.py:187
  (71 shorter events, 15.2 us)
Async XLA Ops:
  1.1 8.8 %collective-permute-start.1 = (bf16[64,640]{1,0:T(8,128)(2,1)S(1)}, bf16[64,640]{1,0:T(8,128)(2,1)S(1)}, u32[]{:S(2)}, u32[]{:S(2)}) collective-permute-start(bf16[64,640]{1,0:T(8,128)(2,1)S(1)} %get-tuple-element.24.refs_0_), channel_id=1, source_target_pairs={{0,2},{2,0},{4,6},{6,4},{1,3},{3,1},{5,7},{7,5},{8,10},{10,8},{12,... | collective-permute-start | bytes 245768 | tf_op jit(solution)/shard_map/ppermute | solution.py:51
  4.2 9.1 %collective-permute-start.7 = (bf16[64,640]{1,0:T(8,128)(2,1)S(1)}, bf16[64,640]{1,0:T(8,128)(2,1)S(1)}, u32[]{:S(2)}, u32[]{:S(2)}) collective-permute-start(bf16[64,640]{1,0:T(8,128)(2,1)S(1)} %get-tuple-element.24.refs_0_), channel_id=1, source_target_pairs={{0,4},{2,6},{4,0},{6,2},{1,5},{3,7},{5,1},{7,3},{8,12},{10,14},{12... | collective-permute-start | bytes 245768 | tf_op jit(solution)/shard_map/ppermute | solution.py:51
  6.7 7.2 %collective-permute-start.8 = (bf16[64,640]{1,0:T(8,128)(2,1)S(1)}, bf16[64,640]{1,0:T(8,128)(2,1)S(1)}, u32[]{:S(2)}, u32[]{:S(2)}) collective-permute-start(bf16[64,640]{1,0:T(8,128)(2,1)S(1)} %get-tuple-element.24.refs_0_), channel_id=1, source_target_pairs={{0,6},{2,4},{4,2},{6,0},{1,7},{3,5},{5,3},{7,1},{8,14},{10,12},{12... | collective-permute-start | bytes 245768 | tf_op jit(solution)/shard_map/ppermute | solution.py:51
  7.7 8.2 %collective-permute-start.6 = (bf16[128,640]{1,0:T(8,128)(2,1)S(1)}, bf16[128,640]{1,0:T(8,128)(2,1)S(1)}, u32[]{:S(2)}, u32[]{:S(2)}) collective-permute-start(bf16[128,640]{1,0:T(8,128)(2,1)S(1)} %pad_maximum_fusion.1), channel_id=1, source_target_pairs={{0,2},{2,0},{4,6},{6,4},{1,3},{3,1},{5,7},{7,5},{8,10},{10,8},{12,... | collective-permute-start | bytes 491528 | tf_op jit(solution)/shard_map/ppermute | solution.py:51
  9.9 4.5 %collective-permute-start.2 = (bf16[64,640]{1,0:T(8,128)(2,1)S(1)}, bf16[64,640]{1,0:T(8,128)(2,1)S(1)}, u32[]{:S(2)}, u32[]{:S(2)}) collective-permute-start(bf16[64,640]{1,0:T(8,128)(2,1)S(1)} %get-tuple-element.24.refs_0_), channel_id=1, source_target_pairs={{0,16},{16,0},{1,17},{17,1},{2,18},{18,2},{3,19},{19,3},{4,20},{20... | collective-permute-start | bytes 245768 | tf_op jit(solution)/shard_map/ppermute | solution.py:47
  13.3 8.9 %collective-permute-start = (bf16[128,2048]{1,0:T(8,128)(2,1)S(1)}, bf16[128,2048]{1,0:T(8,128)(2,1)S(1)}, u32[]{:S(2)}, u32[]{:S(2)}) collective-permute-start(bf16[128,2048]{1,0:T(8,128)(2,1)S(1)} %fusion.2.refs_0_), channel_id=1, source_target_pairs={{0,8},{8,0},{1,9},{9,1},{2,10},{10,2},{3,11},{11,3},{4,12},{12,4},... | collective-permute-start | bytes 1572872 | tf_op jit(solution)/shard_map/ppermute | solution.py:47
  15.9 7.4 %collective-permute-start.10 = (bf16[192,640]{1,0:T(8,128)(2,1)S(1)}, bf16[192,640]{1,0:T(8,128)(2,1)S(1)}, u32[]{:S(2)}, u32[]{:S(2)}) collective-permute-start(bf16[192,640]{1,0:T(8,128)(2,1)S(1)} %constant_dynamic-update-slice_fusion.refs_3_), channel_id=1, source_target_pairs={{0,1},{1,0},{2,3},{3,2},{4,5},{5,4},{6,7},{7,6},{8,9},{9,8},{10,11... | collective-permute-start | bytes 737288 | tf_op jit(solution)/shard_map/ppermute | solution.py:47
  17.5 6.2 %collective-permute-start.9 = (bf16[192,640]{1,0:T(8,128)(2,1)S(1)}, bf16[192,640]{1,0:T(8,128)(2,1)S(1)}, u32[]{:S(2)}, u32[]{:S(2)}) collective-permute-start(bf16[192,640]{1,0:T(8,128)(2,1)S(1)} %constant_dynamic-update-slice_fusion.refs_3_), channel_id=1, source_target_pairs={{0,16},{16,0},{1,17},{17,1},{2,18},{18,2},{3,19},{19,3},{4,20},{20... | collective-permute-start | bytes 737288 | tf_op jit(solution)/shard_map/ppermute | solution.py:47
  18.7 11.5 %collective-permute-start.11 = (bf16[128,640]{1,0:T(8,128)(2,1)S(1)}, bf16[128,640]{1,0:T(8,128)(2,1)S(1)}, u32[]{:S(2)}, u32[]{:S(2)}) collective-permute-start(bf16[128,640]{1,0:T(8,128)(2,1)S(1)} %pad_maximum_fusion.2), channel_id=1, source_target_pairs={{0,4},{2,6},{4,0},{6,2},{1,5},{3,7},{5,1},{7,3},{8,12},{10,14},{12... | collective-permute-start | bytes 491528 | tf_op jit(solution)/shard_map/ppermute | solution.py:51
  21.7 14.7 %collective-permute-start.4 = (bf16[128,2048]{1,0:T(8,128)(2,1)S(1)}, bf16[128,2048]{1,0:T(8,128)(2,1)S(1)}, u32[]{:S(2)}, u32[]{:S(2)}) collective-permute-start(bf16[128,2048]{1,0:T(8,128)(2,1)S(1)} %fusion.2.refs_0_), channel_id=1, source_target_pairs={{0,2},{2,0},{4,6},{6,4},{1,3},{3,1},{5,7},{7,5},{8,10},{10,8},{12,... | collective-permute-start | bytes 1572872 | tf_op jit(solution)/shard_map/ppermute | solution.py:51
  23.8 5.4 %collective-permute-start.15 = (bf16[128,640]{1,0:T(8,128)(2,1)S(1)}, bf16[128,640]{1,0:T(8,128)(2,1)S(1)}, u32[]{:S(2)}, u32[]{:S(2)}) collective-permute-start(bf16[128,640]{1,0:T(8,128)(2,1)S(1)} %pad_maximum_fusion.4), channel_id=1, source_target_pairs={{0,1},{1,0},{2,3},{3,2},{4,5},{5,4},{6,7},{7,6},{8,9},{9,8},{10,11... | collective-permute-start | bytes 491528 | tf_op jit(solution)/shard_map/ppermute | solution.py:47
  24.3 5.4 %collective-permute-start.16 = (bf16[128,640]{1,0:T(8,128)(2,1)S(1)}, bf16[128,640]{1,0:T(8,128)(2,1)S(1)}, u32[]{:S(2)}, u32[]{:S(2)}) collective-permute-start(bf16[128,640]{1,0:T(8,128)(2,1)S(1)} %slice.25), channel_id=1, source_target_pairs={{0,16},{16,0},{1,17},{17,1},{2,18},{18,2},{3,19},{19,3},{4,20},{20... | collective-permute-start | bytes 491528 | tf_op jit(solution)/shard_map/ppermute | solution.py:47
  30.1 6.3 %collective-permute-start.17 = (f32[128,640]{1,0:T(8,128)S(1)}, f32[128,640]{1,0:T(8,128)S(1)}, u32[]{:S(2)}, u32[]{:S(2)}) collective-permute-start(f32[128,640]{1,0:T(8,128)S(1)} %get-tuple-element.36), channel_id=1, source_target_pairs={{0,8},{8,0},{1,9},{9,1},{2,10},{10,2},{3,11},{11,3},{4,12},{12,4},... | collective-permute-start | bytes 983048 | tf_op jit(solution)/shard_map/ppermute | solution.py:47
  30.2 11.9 %collective-permute-start.14 = (bf16[128,640]{1,0:T(8,128)(2,1)S(1)}, bf16[128,640]{1,0:T(8,128)(2,1)S(1)}, u32[]{:S(2)}, u32[]{:S(2)}) collective-permute-start(bf16[128,640]{1,0:T(8,128)(2,1)S(1)} %pad_maximum_fusion.3), channel_id=1, source_target_pairs={{0,4},{2,6},{4,0},{6,2},{1,5},{3,7},{5,1},{7,3},{8,12},{10,14},{12... | collective-permute-start | bytes 491528 | tf_op jit(solution)/shard_map/ppermute | solution.py:51
  33.8 10.2 %collective-permute-start.12 = (bf16[256,640]{1,0:T(8,128)(2,1)S(1)}, bf16[256,640]{1,0:T(8,128)(2,1)S(1)}, u32[]{:S(2)}, u32[]{:S(2)}) collective-permute-start(bf16[256,640]{1,0:T(8,128)(2,1)S(1)} %pad_maximum_fusion.refs_0_), channel_id=1, source_target_pairs={{0,16},{16,0},{1,17},{17,1},{2,18},{18,2},{3,19},{19,3},{4,20},{20... | collective-permute-start | bytes 983048 | tf_op jit(solution)/shard_map/ppermute | solution.py:47
  34.4 9.8 %collective-permute-start.13 = (bf16[256,640]{1,0:T(8,128)(2,1)S(1)}, bf16[256,640]{1,0:T(8,128)(2,1)S(1)}, u32[]{:S(2)}, u32[]{:S(2)}) collective-permute-start(bf16[256,640]{1,0:T(8,128)(2,1)S(1)} %pad_maximum_fusion.refs_0_), channel_id=1, source_target_pairs={{0,1},{1,0},{2,3},{3,2},{4,5},{5,4},{6,7},{7,6},{8,9},{9,8},{10,11... | collective-permute-start | bytes 983048 | tf_op jit(solution)/shard_map/ppermute | solution.py:47
  36.4 11.2 %collective-permute-start.5 = (bf16[128,2048]{1,0:T(8,128)(2,1)S(1)}, bf16[128,2048]{1,0:T(8,128)(2,1)S(1)}, u32[]{:S(2)}, u32[]{:S(2)}) collective-permute-start(bf16[128,2048]{1,0:T(8,128)(2,1)S(1)} %collective-permute-done.4.refs_2_), channel_id=1, source_target_pairs={{0,8},{8,0},{1,9},{9,1},{2,10},{10,2},{3,11},{11,3},{4,12},{12,4},... | collective-permute-start | bytes 1572872 | tf_op jit(solution)/shard_map/ppermute | solution.py:47
  36.4 7.7 %collective-permute-start.18 = (bf16[136,640]{1,0:T(8,128)(2,1)S(1)}, bf16[136,640]{1,0:T(8,128)(2,1)S(1)}, u32[]{:S(2)}, u32[]{:S(2)}) collective-permute-start(bf16[136,640]{1,0:T(8,128)(2,1)S(1)} %fusion.5.refs_0_), channel_id=1, source_target_pairs={{0,2},{2,4},{4,6},{1,3},{3,5},{5,7},{8,10},{10,12},{12,14},{9,11},... | collective-permute-start | bytes 522248 | tf_op jit(solution)/shard_map/ppermute | solution.py:302
  42.1 10.6 %collective-permute-start.20 = (bf16[256,640]{1,0:T(8,128)(2,1)S(1)}, bf16[256,640]{1,0:T(8,128)(2,1)S(1)}, u32[]{:S(2)}, u32[]{:S(2)}) collective-permute-start(bf16[256,640]{1,0:T(8,128)(2,1)S(1)} %get-tuple-element.49), channel_id=1, source_target_pairs={{0,1},{1,0},{2,3},{3,2},{4,5},{5,4},{6,7},{7,6},{8,9},{9,8},{10,11... | collective-permute-start | bytes 983048 | tf_op jit(solution)/shard_map/ppermute | solution.py:47
  44.2 11.5 %collective-permute-start.22 = (bf16[256,640]{1,0:T(8,128)(2,1)S(1)}, bf16[256,640]{1,0:T(8,128)(2,1)S(1)}, u32[]{:S(2)}, u32[]{:S(2)}) collective-permute-start(bf16[256,640]{1,0:T(8,128)(2,1)S(1)} %collective-permute-done.13.refs_2_), channel_id=1, source_target_pairs={{0,16},{16,0},{1,17},{17,1},{2,18},{18,2},{3,19},{19,3},{4,20},{20... | collective-permute-start | bytes 983048 | tf_op jit(solution)/shard_map/ppermute | solution.py:47
  45.8 9.9 %collective-permute-start.21 = (bf16[136,640]{1,0:T(8,128)(2,1)S(1)}, bf16[136,640]{1,0:T(8,128)(2,1)S(1)}, u32[]{:S(2)}, u32[]{:S(2)}) collective-permute-start(bf16[136,640]{1,0:T(8,128)(2,1)S(1)} %collective-permute-done.18.refs_1_), channel_id=1, source_target_pairs={{0,1},{1,0},{2,3},{3,2},{4,5},{5,4},{6,7},{7,6},{8,9},{9,8},{10,11... | collective-permute-start | bytes 522248 | tf_op jit(solution)/shard_map/ppermute | solution.py:47
  49.3 6.4 %collective-permute-start.19 = (bf16[136,640]{1,0:T(8,128)(2,1)S(1)}, bf16[136,640]{1,0:T(8,128)(2,1)S(1)}, u32[]{:S(2)}, u32[]{:S(2)}) collective-permute-start(bf16[136,640]{1,0:T(8,128)(2,1)S(1)} %collective-permute-done.18.refs_1_), channel_id=1, source_target_pairs={{0,2},{2,4},{4,6},{1,3},{3,5},{5,7},{8,10},{10,12},{12,14},{9,11},... | collective-permute-start | bytes 522248 | tf_op jit(solution)/shard_map/ppermute | solution.py:306
  56.9 7.0 %collective-permute-start.25 = (bf16[136,640]{1,0:T(8,128)(2,1)}, bf16[136,640]{1,0:T(8,128)(2,1)S(1)}, u32[]{:S(2)}, u32[]{:S(2)}) collective-permute-start(bf16[136,640]{1,0:T(8,128)(2,1)} %broadcast_select_fusion), channel_id=1, source_target_pairs={{0,1},{1,0},{2,3},{3,2},{4,5},{5,4},{6,7},{7,6},{8,9},{9,8},{10,11... | collective-permute-start | bytes 522248 | tf_op jit(solution)/shard_map/ppermute | solution.py:47
  58.7 6.4 %collective-permute-start.24 = (bf16[128,640]{1,0:T(8,128)(2,1)S(1)}, bf16[128,640]{1,0:T(8,128)(2,1)S(1)}, u32[]{:S(2)}, u32[]{:S(2)}) collective-permute-start(bf16[128,640]{1,0:T(8,128)(2,1)S(1)} %get-tuple-element.42), channel_id=1, source_target_pairs={{0,2},{2,0},{4,6},{6,4},{1,3},{3,1},{5,7},{7,5},{8,10},{10,8},{12,... | collective-permute-start | bytes 491528 | tf_op jit(solution)/shard_map/ppermute | solution.py:51
  (6 other events, 41.3 us)

commit v6 on v5

--- a/solution.py
+++ b/solution.py
@@ -164,16 +164,17 @@
         base = head * REPEATS * HD
         heads = [divmod(head * REPEATS + r, QH // HD) for r in range(REPEATS)]
         queries = jnp.concatenate([q_all[part, :, h * HD:(h + 1) * HD] for part, h in heads], axis=0)
-        keys = jnp.concatenate([block[:rows, cols] for block in blocks], axis=0)
-        values = jnp.concatenate([block[:rows, vcols] for block in blocks], axis=0)
+        keys = jnp.concatenate([prefix[:, cols]] + [block[:rows, cols] for block in blocks], axis=0)
+        values = jnp.concatenate([prefix[:, vcols]] + [block[:rows, vcols] for block in blocks], axis=0)
         contract = (((1,), (1,)), ((), ()))
-        s_pre = lax.dot_general(queries, prefix[:, cols], contract, preferred_element_type=F32)
-        s_suf = lax.dot_general(queries, keys, contract, preferred_element_type=F32) + bias
+        scores = lax.dot_general(queries, keys, contract, preferred_element_type=F32)
+        count = prefix.shape[0]
+        s_pre, s_suf = scores[:, :count], scores[:, count:] + bias
         top = jnp.maximum(jnp.max(s_pre, axis=-1, keepdims=True), jnp.max(s_suf, axis=-1, keepdims=True))
         p_pre, p_suf = jnp.exp(s_pre - top), jnp.exp(s_suf - top)
         total = jnp.sum(p_pre, axis=-1, keepdims=True) + jnp.sum(p_suf, axis=-1, keepdims=True)
-        numerator = jnp.dot(p_pre.astype(BF16), prefix[:, vcols], preferred_element_type=F32)
-        numerator += jnp.dot(p_suf.astype(BF16), values, preferred_element_type=F32)
+        rounded = jnp.concatenate([p_pre.astype(BF16), p_suf.astype(BF16)], axis=1)
+        numerator = jnp.dot(rounded, values, preferred_element_type=F32)
         context = (numerator / total).astype(BF16)
         for r in range(REPEATS):
             out[:, base + r * HD:base + (r + 1) * HD] = context[r * rows:(r + 1) * rows]

time: 71.6 us -> 71.7 us (level)
  no operation moved by 1% of the time
where the time goes in v6:
time: 71.7 us; the launch traced here: 71.4 us
  starting transfers between devices  37.8 us (53%)
  waiting for transfers between devices  17.1 us (24%)
  Pallas kernels  11.4 us (16%)
  other arithmetic  3.27 us (5%)
  local copies, waits for them, and re-layouts  1.57 us (2%)
    ppermute x16, starting transfers between devices, swap(): return lax.ppermute(x, axis, [(0, 1), (1, 0)])  17.5 us
    ppermute x8, starting transfers between devices, z_swap(): return lax.ppermute(x, 'z', [(i, i ^ distance) for i in range(4)])  15.1 us
    ppermute x16, waiting for transfers between devices, swap(): return lax.ppermute(x, axis, [(0, 1), (1, 0)])  12.1 us
    pallas_call x1, Pallas kernels, attend(): pl.pallas_call(functools.partial(attend_kernel, earlier), out_shape=jax.S...  6.31 us
    ppermute x8, waiting for transfers between devices, z_swap(): return lax.ppermute(x, 'z', [(i, i ^ distance) for i in range(4)])  4.97 us
    pallas_call x2, Pallas kernels, order_features(): pl.pallas_call(functools.partial(order_kernel, order), out_shape=jax.Shap...  2.87 us
    ppermute x1, starting transfers between devices, swap_body(): four_back = lax.ppermute(*gate('four_back', two_back), 'z', upward)  2.65 us
    ppermute x1, starting transfers between devices, swap_body(): two_back = lax.ppermute(*gate('two_back', block), 'z', upward)  2.55 us
  transfers between devices with their start and end apart: 26, of which 12 were waited for; matrix products, arithmetic and copies ran while one was open for 5% of the time, Pallas kernels for 7%

profile of v6, /device:TPU:0, one launch (start us, length us, event | category | flops | bytes accessed | tf_op | source)
XLA Modules:
  0.0 71.4 jit_solution(12782611114929022055)
XLA Ops:
  1.1 3.1 %collective-permute-start.1 = (bf16[64,640]{1,0:T(8,128)(2,1)S(1)}, bf16[64,640]{1,0:T(8,128)(2,1)S(1)}, u32[]{:S(2)}, u32[]{:S(2)}) collective-permute-start(bf16[64,640]{1,0:T(8,128)(2,1)S(1)} %get-tuple-element.24.refs_0_), channel_id=1, source_target_pairs={{0,2},{2,0},{4,6},{6,4},{1,3},{3,1},{5,7},{7,5},{8,10},{10,8},{12,... | collective-permute-start | bytes 245768 | tf_op jit(solution)/shard_map/ppermute | solution.py:51
  4.2 2.6 %collective-permute-start.7 = (bf16[64,640]{1,0:T(8,128)(2,1)S(1)}, bf16[64,640]{1,0:T(8,128)(2,1)S(1)}, u32[]{:S(2)}, u32[]{:S(2)}) collective-permute-start(bf16[64,640]{1,0:T(8,128)(2,1)S(1)} %get-tuple-element.24.refs_0_), channel_id=1, source_target_pairs={{0,4},{2,6},{4,0},{6,2},{1,5},{3,7},{5,1},{7,3},{8,12},{10,14},{12... | collective-permute-start | bytes 245768 | tf_op jit(solution)/shard_map/ppermute | solution.py:51
  8.6 1.2 %fusion = f32[128]{0:T(128)S(1)} fusion(bf16[1,128,2048]{2,1,0:T(8,128)(2,1)} %param.5), kind=kLoop, calls=%fused_computation.2 | loop fusion | flops 786304 | bytes 524800 | tf_op jit(solution)/shard_map/reduce_sum | solution.py:42
  9.9 1.6 %collective-permute-start.2 = (bf16[64,640]{1,0:T(8,128)(2,1)S(1)}, bf16[64,640]{1,0:T(8,128)(2,1)S(1)}, u32[]{:S(2)}, u32[]{:S(2)}) collective-permute-start(bf16[64,640]{1,0:T(8,128)(2,1)S(1)} %get-tuple-element.24.refs_0_), channel_id=1, source_target_pairs={{0,16},{16,0},{1,17},{17,1},{2,18},{18,2},{3,19},{19,3},{4,20},{20... | collective-permute-start | bytes 245768 | tf_op jit(solution)/shard_map/ppermute | solution.py:47
  11.4 1.5 %collective-permute-start.3 = (bf16[64,640]{1,0:T(8,128)(2,1)S(1)}, bf16[64,640]{1,0:T(8,128)(2,1)S(1)}, u32[]{:S(2)}, u32[]{:S(2)}) collective-permute-start(bf16[64,640]{1,0:T(8,128)(2,1)S(1)} %get-tuple-element.24.refs_0_), channel_id=1, source_target_pairs={{0,1},{1,0},{2,3},{3,2},{4,5},{5,4},{6,7},{7,6},{8,9},{9,8},{10,11... | collective-permute-start | bytes 245768 | tf_op jit(solution)/shard_map/ppermute | solution.py:47
  14.4 1.5 %collective-permute-done.3.refs_2_ = bf16[64,640]{1,0:T(8,128)(2,1)S(1)} collective-permute-done((bf16[64,640]{1,0:T(8,128)(2,1)S(1)}, bf16[64,640]{1,0:T(8,128)(2,1)S(1)}, u32[]{:S(2)}, u32[]{:S(2)}) %collective-permute-start.3) | collective-permute-done | bytes 81952 | tf_op jit(solution)/shard_map/ppermute | solution.py:47
  15.9 1.6 %collective-permute-start.10 = (bf16[192,640]{1,0:T(8,128)(2,1)S(1)}, bf16[192,640]{1,0:T(8,128)(2,1)S(1)}, u32[]{:S(2)}, u32[]{:S(2)}) collective-permute-start(bf16[192,640]{1,0:T(8,128)(2,1)S(1)} %constant_dynamic-update-slice_fusion.refs_3_), channel_id=1, source_target_pairs={{0,1},{1,0},{2,3},{3,2},{4,5},{5,4},{6,7},{7,6},{8,9},{9,8},{10,11... | collective-permute-start | bytes 737288 | tf_op jit(solution)/shard_map/ppermute | solution.py:47
  18.7 3.0 %collective-permute-start.11 = (bf16[128,640]{1,0:T(8,128)(2,1)S(1)}, bf16[128,640]{1,0:T(8,128)(2,1)S(1)}, u32[]{:S(2)}, u32[]{:S(2)}) collective-permute-start(bf16[128,640]{1,0:T(8,128)(2,1)S(1)} %pad_maximum_fusion.2), channel_id=1, source_target_pairs={{0,4},{2,6},{4,0},{6,2},{1,5},{3,7},{5,1},{7,3},{8,12},{10,14},{12... | collective-permute-start | bytes 491528 | tf_op jit(solution)/shard_map/ppermute | solution.py:51
  24.3 1.6 %collective-permute-start.16 = (bf16[128,640]{1,0:T(8,128)(2,1)S(1)}, bf16[128,640]{1,0:T(8,128)(2,1)S(1)}, u32[]{:S(2)}, u32[]{:S(2)}) collective-permute-start(bf16[128,640]{1,0:T(8,128)(2,1)S(1)} %slice.25), channel_id=1, source_target_pairs={{0,16},{16,0},{1,17},{17,1},{2,18},{18,2},{3,19},{19,3},{4,20},{20... | collective-permute-start | bytes 491528 | tf_op jit(solution)/shard_map/ppermute | solution.py:47
  26.7 2.4 %collective-permute-done.15.refs_0_ = bf16[128,640]{1,0:T(8,128)(2,1)S(1)} collective-permute-done((bf16[128,640]{1,0:T(8,128)(2,1)S(1)}, bf16[128,640]{1,0:T(8,128)(2,1)S(1)}, u32[]{:S(2)}, u32[]{:S(2)}) %collective-permute-start.15) | collective-permute-done | bytes 163872 | tf_op jit(solution)/shard_map/ppermute | solution.py:47
  30.2 3.6 %collective-permute-start.14 = (bf16[128,640]{1,0:T(8,128)(2,1)S(1)}, bf16[128,640]{1,0:T(8,128)(2,1)S(1)}, u32[]{:S(2)}, u32[]{:S(2)}) collective-permute-start(bf16[128,640]{1,0:T(8,128)(2,1)S(1)} %pad_maximum_fusion.3), channel_id=1, source_target_pairs={{0,4},{2,6},{4,0},{6,2},{1,5},{3,7},{5,1},{7,3},{8,12},{10,14},{12... | collective-permute-start | bytes 491528 | tf_op jit(solution)/shard_map/ppermute | solution.py:51
  34.4 2.0 %collective-permute-start.13 = (bf16[256,640]{1,0:T(8,128)(2,1)S(1)}, bf16[256,640]{1,0:T(8,128)(2,1)S(1)}, u32[]{:S(2)}, u32[]{:S(2)}) collective-permute-start(bf16[256,640]{1,0:T(8,128)(2,1)S(1)} %pad_maximum_fusion.refs_0_), channel_id=1, source_target_pairs={{0,1},{1,0},{2,3},{3,2},{4,5},{5,4},{6,7},{7,6},{8,9},{9,8},{10,11... | collective-permute-start | bytes 983048 | tf_op jit(solution)/shard_map/ppermute | solution.py:47
  36.4 2.5 %collective-permute-start.18 = (bf16[136,640]{1,0:T(8,128)(2,1)S(1)}, bf16[136,640]{1,0:T(8,128)(2,1)S(1)}, u32[]{:S(2)}, u32[]{:S(2)}) collective-permute-start(bf16[136,640]{1,0:T(8,128)(2,1)S(1)} %fusion.5.refs_0_), channel_id=1, source_target_pairs={{0,2},{2,4},{4,6},{1,3},{3,5},{5,7},{8,10},{10,12},{12,14},{9,11},... | collective-permute-start | bytes 522248 | tf_op jit(solution)/shard_map/ppermute | solution.py:303
  39.0 3.1 %collective-permute-done.14 = bf16[128,640]{1,0:T(8,128)(2,1)S(1)} collective-permute-done((bf16[128,640]{1,0:T(8,128)(2,1)S(1)}, bf16[128,640]{1,0:T(8,128)(2,1)S(1)}, u32[]{:S(2)}, u32[]{:S(2)}) %collective-permute-start.14) | collective-permute-done | bytes 163872 | tf_op jit(solution)/shard_map/ppermute | solution.py:51
  42.1 1.8 %collective-permute-start.20 = (bf16[256,640]{1,0:T(8,128)(2,1)S(1)}, bf16[256,640]{1,0:T(8,128)(2,1)S(1)}, u32[]{:S(2)}, u32[]{:S(2)}) collective-permute-start(bf16[256,640]{1,0:T(8,128)(2,1)S(1)} %get-tuple-element.49), channel_id=1, source_target_pairs={{0,1},{1,0},{2,3},{3,2},{4,5},{5,4},{6,7},{7,6},{8,9},{9,8},{10,11... | collective-permute-start | bytes 983048 | tf_op jit(solution)/shard_map/ppermute | solution.py:47
  44.2 1.6 %collective-permute-start.22 = (bf16[256,640]{1,0:T(8,128)(2,1)S(1)}, bf16[256,640]{1,0:T(8,128)(2,1)S(1)}, u32[]{:S(2)}, u32[]{:S(2)}) collective-permute-start(bf16[256,640]{1,0:T(8,128)(2,1)S(1)} %collective-permute-done.13.refs_2_), channel_id=1, source_target_pairs={{0,16},{16,0},{1,17},{17,1},{2,18},{18,2},{3,19},{19,3},{4,20},{20... | collective-permute-start | bytes 983048 | tf_op jit(solution)/shard_map/ppermute | solution.py:47
  45.8 1.7 %collective-permute-start.21 = (bf16[136,640]{1,0:T(8,128)(2,1)S(1)}, bf16[136,640]{1,0:T(8,128)(2,1)S(1)}, u32[]{:S(2)}, u32[]{:S(2)}) collective-permute-start(bf16[136,640]{1,0:T(8,128)(2,1)S(1)} %collective-permute-done.18.refs_1_), channel_id=1, source_target_pairs={{0,1},{1,0},{2,3},{3,2},{4,5},{5,4},{6,7},{7,6},{8,9},{9,8},{10,11... | collective-permute-start | bytes 522248 | tf_op jit(solution)/shard_map/ppermute | solution.py:47
  47.5 1.7 %shard_map.55.features = bf16[512,1024]{1,0:T(8,128)(2,1)S(1)} custom-call(s32[5]{0:T(128)S(1)} %stack.51.bits, bf16[128,2048]{1,0:T(8,128)(2,1)S(1)} %fusion.2.refs_0_, bf16[128,2048]{1,0:T(8,128)(2,1)S(1)} %collective-permute-done.refs_1_, bf16[128,2048]{1,0:T(8,128)(2,1)S(1)} %collective-permute-done.4.refs_2_, ...), custom_call_target="tpu_custom_call" | custom-call | bytes 4194304 | tf_op jit(solution)/shard_map/pallas_call | solution.py:76
  49.3 2.7 %collective-permute-start.19 = (bf16[136,640]{1,0:T(8,128)(2,1)S(1)}, bf16[136,640]{1,0:T(8,128)(2,1)S(1)}, u32[]{:S(2)}, u32[]{:S(2)}) collective-permute-start(bf16[136,640]{1,0:T(8,128)(2,1)S(1)} %collective-permute-done.18.refs_1_), channel_id=1, source_target_pairs={{0,2},{2,4},{4,6},{1,3},{3,5},{5,7},{8,10},{10,12},{12,14},{9,11},... | collective-permute-start | bytes 522248 | tf_op jit(solution)/shard_map/ppermute | solution.py:307
  53.6 2.1 %collective-permute-done.21.refs_3_ = bf16[136,640]{1,0:T(8,128)(2,1)S(1)} collective-permute-done((bf16[136,640]{1,0:T(8,128)(2,1)S(1)}, bf16[136,640]{1,0:T(8,128)(2,1)S(1)}, u32[]{:S(2)}, u32[]{:S(2)}) %collective-permute-start.21) | collective-permute-done | bytes 174112 | tf_op jit(solution)/shard_map/ppermute | solution.py:47
  56.9 1.7 %collective-permute-start.25 = (bf16[136,640]{1,0:T(8,128)(2,1)}, bf16[136,640]{1,0:T(8,128)(2,1)S(1)}, u32[]{:S(2)}, u32[]{:S(2)}) collective-permute-start(bf16[136,640]{1,0:T(8,128)(2,1)} %broadcast_select_fusion), channel_id=1, source_target_pairs={{0,1},{1,0},{2,3},{3,2},{4,5},{5,4},{6,7},{7,6},{8,9},{9,8},{10,11... | collective-permute-start | bytes 522248 | tf_op jit(solution)/shard_map/ppermute | solution.py:47
  58.7 1.4 %collective-permute-start.24 = (bf16[128,640]{1,0:T(8,128)(2,1)S(1)}, bf16[128,640]{1,0:T(8,128)(2,1)S(1)}, u32[]{:S(2)}, u32[]{:S(2)}) collective-permute-start(bf16[128,640]{1,0:T(8,128)(2,1)S(1)} %get-tuple-element.42), channel_id=1, source_target_pairs={{0,2},{2,0},{4,6},{6,4},{1,3},{3,1},{5,7},{7,5},{8,10},{10,8},{12,... | collective-permute-start | bytes 491528 | tf_op jit(solution)/shard_map/ppermute | solution.py:51
  60.3 3.6 %collective-permute-done.25.refs_4_ = bf16[136,640]{1,0:T(8,128)(2,1)S(1)} collective-permute-done((bf16[136,640]{1,0:T(8,128)(2,1)}, bf16[136,640]{1,0:T(8,128)(2,1)S(1)}, u32[]{:S(2)}, u32[]{:S(2)}) %collective-permute-start.25) | collective-permute-done | bytes 174112 | tf_op jit(solution)/shard_map/ppermute | solution.py:47
  65.1 6.3 %shard_map.61 = bf16[128,1280]{1,0:T(8,128)(2,1)} custom-call(s32[6]{0:T(128)S(1)} %stack.45.scalars, bf16[128,640]{1,0:T(8,128)(2,1)S(1)} %get-tuple-element.44.mine, bf16[128,640]{1,0:T(8,128)(2,1)S(1)} %collective-permute-done.24.pair, bf16[512,640]{1,0:T(8,128)(2,1)S(1)} %constant_dynamic-update-slice_fusion.5.prefix, f32[128,1]{1,0:T(8,128)S(1)} %copy.6.seg_col, ...), custom_call_target="tpu_custom_call" | custom-call | flops 754974720 | bytes 1474560 | tf_op jit(solution)/shard_map/pallas_call | solution.py:188
  (71 shorter events, 15.2 us)
Async XLA Ops:
  1.1 8.8 %collective-permute-start.1 = (bf16[64,640]{1,0:T(8,128)(2,1)S(1)}, bf16[64,640]{1,0:T(8,128)(2,1)S(1)}, u32[]{:S(2)}, u32[]{:S(2)}) collective-permute-start(bf16[64,640]{1,0:T(8,128)(2,1)S(1)} %get-tuple-element.24.refs_0_), channel_id=1, source_target_pairs={{0,2},{2,0},{4,6},{6,4},{1,3},{3,1},{5,7},{7,5},{8,10},{10,8},{12,... | collective-permute-start | bytes 245768 | tf_op jit(solution)/shard_map/ppermute | solution.py:51
  4.2 9.1 %collective-permute-start.7 = (bf16[64,640]{1,0:T(8,128)(2,1)S(1)}, bf16[64,640]{1,0:T(8,128)(2,1)S(1)}, u32[]{:S(2)}, u32[]{:S(2)}) collective-permute-start(bf16[64,640]{1,0:T(8,128)(2,1)S(1)} %get-tuple-element.24.refs_0_), channel_id=1, source_target_pairs={{0,4},{2,6},{4,0},{6,2},{1,5},{3,7},{5,1},{7,3},{8,12},{10,14},{12... | collective-permute-start | bytes 245768 | tf_op jit(solution)/shard_map/ppermute | solution.py:51
  6.7 7.2 %collective-permute-start.8 = (bf16[64,640]{1,0:T(8,128)(2,1)S(1)}, bf16[64,640]{1,0:T(8,128)(2,1)S(1)}, u32[]{:S(2)}, u32[]{:S(2)}) collective-permute-start(bf16[64,640]{1,0:T(8,128)(2,1)S(1)} %get-tuple-element.24.refs_0_), channel_id=1, source_target_pairs={{0,6},{2,4},{4,2},{6,0},{1,7},{3,5},{5,3},{7,1},{8,14},{10,12},{12... | collective-permute-start | bytes 245768 | tf_op jit(solution)/shard_map/ppermute | solution.py:51
  7.7 8.2 %collective-permute-start.6 = (bf16[128,640]{1,0:T(8,128)(2,1)S(1)}, bf16[128,640]{1,0:T(8,128)(2,1)S(1)}, u32[]{:S(2)}, u32[]{:S(2)}) collective-permute-start(bf16[128,640]{1,0:T(8,128)(2,1)S(1)} %pad_maximum_fusion.1), channel_id=1, source_target_pairs={{0,2},{2,0},{4,6},{6,4},{1,3},{3,1},{5,7},{7,5},{8,10},{10,8},{12,... | collective-permute-start | bytes 491528 | tf_op jit(solution)/shard_map/ppermute | solution.py:51
  9.9 4.5 %collective-permute-start.2 = (bf16[64,640]{1,0:T(8,128)(2,1)S(1)}, bf16[64,640]{1,0:T(8,128)(2,1)S(1)}, u32[]{:S(2)}, u32[]{:S(2)}) collective-permute-start(bf16[64,640]{1,0:T(8,128)(2,1)S(1)} %get-tuple-element.24.refs_0_), channel_id=1, source_target_pairs={{0,16},{16,0},{1,17},{17,1},{2,18},{18,2},{3,19},{19,3},{4,20},{20... | collective-permute-start | bytes 245768 | tf_op jit(solution)/shard_map/ppermute | solution.py:47
  13.3 8.9 %collective-permute-start = (bf16[128,2048]{1,0:T(8,128)(2,1)S(1)}, bf16[128,2048]{1,0:T(8,128)(2,1)S(1)}, u32[]{:S(2)}, u32[]{:S(2)}) collective-permute-start(bf16[128,2048]{1,0:T(8,128)(2,1)S(1)} %fusion.2.refs_0_), channel_id=1, source_target_pairs={{0,8},{8,0},{1,9},{9,1},{2,10},{10,2},{3,11},{11,3},{4,12},{12,4},... | collective-permute-start | bytes 1572872 | tf_op jit(solution)/shard_map/ppermute | solution.py:47
  15.9 7.4 %collective-permute-start.10 = (bf16[192,640]{1,0:T(8,128)(2,1)S(1)}, bf16[192,640]{1,0:T(8,128)(2,1)S(1)}, u32[]{:S(2)}, u32[]{:S(2)}) collective-permute-start(bf16[192,640]{1,0:T(8,128)(2,1)S(1)} %constant_dynamic-update-slice_fusion.refs_3_), channel_id=1, source_target_pairs={{0,1},{1,0},{2,3},{3,2},{4,5},{5,4},{6,7},{7,6},{8,9},{9,8},{10,11... | collective-permute-start | bytes 737288 | tf_op jit(solution)/shard_map/ppermute | solution.py:47
  17.5 6.2 %collective-permute-start.9 = (bf16[192,640]{1,0:T(8,128)(2,1)S(1)}, bf16[192,640]{1,0:T(8,128)(2,1)S(1)}, u32[]{:S(2)}, u32[]{:S(2)}) collective-permute-start(bf16[192,640]{1,0:T(8,128)(2,1)S(1)} %constant_dynamic-update-slice_fusion.refs_3_), channel_id=1, source_target_pairs={{0,16},{16,0},{1,17},{17,1},{2,18},{18,2},{3,19},{19,3},{4,20},{20... | collective-permute-start | bytes 737288 | tf_op jit(solution)/shard_map/ppermute | solution.py:47
  18.7 11.5 %collective-permute-start.11 = (bf16[128,640]{1,0:T(8,128)(2,1)S(1)}, bf16[128,640]{1,0:T(8,128)(2,1)S(1)}, u32[]{:S(2)}, u32[]{:S(2)}) collective-permute-start(bf16[128,640]{1,0:T(8,128)(2,1)S(1)} %pad_maximum_fusion.2), channel_id=1, source_target_pairs={{0,4},{2,6},{4,0},{6,2},{1,5},{3,7},{5,1},{7,3},{8,12},{10,14},{12... | collective-permute-start | bytes 491528 | tf_op jit(solution)/shard_map/ppermute | solution.py:51
  21.7 14.7 %collective-permute-start.4 = (bf16[128,2048]{1,0:T(8,128)(2,1)S(1)}, bf16[128,2048]{1,0:T(8,128)(2,1)S(1)}, u32[]{:S(2)}, u32[]{:S(2)}) collective-permute-start(bf16[128,2048]{1,0:T(8,128)(2,1)S(1)} %fusion.2.refs_0_), channel_id=1, source_target_pairs={{0,2},{2,0},{4,6},{6,4},{1,3},{3,1},{5,7},{7,5},{8,10},{10,8},{12,... | collective-permute-start | bytes 1572872 | tf_op jit(solution)/shard_map/ppermute | solution.py:51
  23.8 5.4 %collective-permute-start.15 = (bf16[128,640]{1,0:T(8,128)(2,1)S(1)}, bf16[128,640]{1,0:T(8,128)(2,1)S(1)}, u32[]{:S(2)}, u32[]{:S(2)}) collective-permute-start(bf16[128,640]{1,0:T(8,128)(2,1)S(1)} %pad_maximum_fusion.4), channel_id=1, source_target_pairs={{0,1},{1,0},{2,3},{3,2},{4,5},{5,4},{6,7},{7,6},{8,9},{9,8},{10,11... | collective-permute-start | bytes 491528 | tf_op jit(solution)/shard_map/ppermute | solution.py:47
  24.3 5.4 %collective-permute-start.16 = (bf16[128,640]{1,0:T(8,128)(2,1)S(1)}, bf16[128,640]{1,0:T(8,128)(2,1)S(1)}, u32[]{:S(2)}, u32[]{:S(2)}) collective-permute-start(bf16[128,640]{1,0:T(8,128)(2,1)S(1)} %slice.25), channel_id=1, source_target_pairs={{0,16},{16,0},{1,17},{17,1},{2,18},{18,2},{3,19},{19,3},{4,20},{20... | collective-permute-start | bytes 491528 | tf_op jit(solution)/shard_map/ppermute | solution.py:47
  30.1 6.3 %collective-permute-start.17 = (f32[128,640]{1,0:T(8,128)S(1)}, f32[128,640]{1,0:T(8,128)S(1)}, u32[]{:S(2)}, u32[]{:S(2)}) collective-permute-start(f32[128,640]{1,0:T(8,128)S(1)} %get-tuple-element.36), channel_id=1, source_target_pairs={{0,8},{8,0},{1,9},{9,1},{2,10},{10,2},{3,11},{11,3},{4,12},{12,4},... | collective-permute-start | bytes 983048 | tf_op jit(solution)/shard_map/ppermute | solution.py:47
  30.2 11.9 %collective-permute-start.14 = (bf16[128,640]{1,0:T(8,128)(2,1)S(1)}, bf16[128,640]{1,0:T(8,128)(2,1)S(1)}, u32[]{:S(2)}, u32[]{:S(2)}) collective-permute-start(bf16[128,640]{1,0:T(8,128)(2,1)S(1)} %pad_maximum_fusion.3), channel_id=1, source_target_pairs={{0,4},{2,6},{4,0},{6,2},{1,5},{3,7},{5,1},{7,3},{8,12},{10,14},{12... | collective-permute-start | bytes 491528 | tf_op jit(solution)/shard_map/ppermute | solution.py:51
  33.8 10.2 %collective-permute-start.12 = (bf16[256,640]{1,0:T(8,128)(2,1)S(1)}, bf16[256,640]{1,0:T(8,128)(2,1)S(1)}, u32[]{:S(2)}, u32[]{:S(2)}) collective-permute-start(bf16[256,640]{1,0:T(8,128)(2,1)S(1)} %pad_maximum_fusion.refs_0_), channel_id=1, source_target_pairs={{0,16},{16,0},{1,17},{17,1},{2,18},{18,2},{3,19},{19,3},{4,20},{20... | collective-permute-start | bytes 983048 | tf_op jit(solution)/shard_map/ppermute | solution.py:47
  34.4 9.8 %collective-permute-start.13 = (bf16[256,640]{1,0:T(8,128)(2,1)S(1)}, bf16[256,640]{1,0:T(8,128)(2,1)S(1)}, u32[]{:S(2)}, u32[]{:S(2)}) collective-permute-start(bf16[256,640]{1,0:T(8,128)(2,1)S(1)} %pad_maximum_fusion.refs_0_), channel_id=1, source_target_pairs={{0,1},{1,0},{2,3},{3,2},{4,5},{5,4},{6,7},{7,6},{8,9},{9,8},{10,11... | collective-permute-start | bytes 983048 | tf_op jit(solution)/shard_map/ppermute | solution.py:47
  36.4 11.2 %collective-permute-start.5 = (bf16[128,2048]{1,0:T(8,128)(2,1)S(1)}, bf16[128,2048]{1,0:T(8,128)(2,1)S(1)}, u32[]{:S(2)}, u32[]{:S(2)}) collective-permute-start(bf16[128,2048]{1,0:T(8,128)(2,1)S(1)} %collective-permute-done.4.refs_2_), channel_id=1, source_target_pairs={{0,8},{8,0},{1,9},{9,1},{2,10},{10,2},{3,11},{11,3},{4,12},{12,4},... | collective-permute-start | bytes 1572872 | tf_op jit(solution)/shard_map/ppermute | solution.py:47
  36.4 7.7 %collective-permute-start.18 = (bf16[136,640]{1,0:T(8,128)(2,1)S(1)}, bf16[136,640]{1,0:T(8,128)(2,1)S(1)}, u32[]{:S(2)}, u32[]{:S(2)}) collective-permute-start(bf16[136,640]{1,0:T(8,128)(2,1)S(1)} %fusion.5.refs_0_), channel_id=1, source_target_pairs={{0,2},{2,4},{4,6},{1,3},{3,5},{5,7},{8,10},{10,12},{12,14},{9,11},... | collective-permute-start | bytes 522248 | tf_op jit(solution)/shard_map/ppermute | solution.py:303
  42.1 10.6 %collective-permute-start.20 = (bf16[256,640]{1,0:T(8,128)(2,1)S(1)}, bf16[256,640]{1,0:T(8,128)(2,1)S(1)}, u32[]{:S(2)}, u32[]{:S(2)}) collective-permute-start(bf16[256,640]{1,0:T(8,128)(2,1)S(1)} %get-tuple-element.49), channel_id=1, source_target_pairs={{0,1},{1,0},{2,3},{3,2},{4,5},{5,4},{6,7},{7,6},{8,9},{9,8},{10,11... | collective-permute-start | bytes 983048 | tf_op jit(solution)/shard_map/ppermute | solution.py:47
  44.2 11.5 %collective-permute-start.22 = (bf16[256,640]{1,0:T(8,128)(2,1)S(1)}, bf16[256,640]{1,0:T(8,128)(2,1)S(1)}, u32[]{:S(2)}, u32[]{:S(2)}) collective-permute-start(bf16[256,640]{1,0:T(8,128)(2,1)S(1)} %collective-permute-done.13.refs_2_), channel_id=1, source_target_pairs={{0,16},{16,0},{1,17},{17,1},{2,18},{18,2},{3,19},{19,3},{4,20},{20... | collective-permute-start | bytes 983048 | tf_op jit(solution)/shard_map/ppermute | solution.py:47
  45.8 9.9 %collective-permute-start.21 = (bf16[136,640]{1,0:T(8,128)(2,1)S(1)}, bf16[136,640]{1,0:T(8,128)(2,1)S(1)}, u32[]{:S(2)}, u32[]{:S(2)}) collective-permute-start(bf16[136,640]{1,0:T(8,128)(2,1)S(1)} %collective-permute-done.18.refs_1_), channel_id=1, source_target_pairs={{0,1},{1,0},{2,3},{3,2},{4,5},{5,4},{6,7},{7,6},{8,9},{9,8},{10,11... | collective-permute-start | bytes 522248 | tf_op jit(solution)/shard_map/ppermute | solution.py:47
  49.3 6.4 %collective-permute-start.19 = (bf16[136,640]{1,0:T(8,128)(2,1)S(1)}, bf16[136,640]{1,0:T(8,128)(2,1)S(1)}, u32[]{:S(2)}, u32[]{:S(2)}) collective-permute-start(bf16[136,640]{1,0:T(8,128)(2,1)S(1)} %collective-permute-done.18.refs_1_), channel_id=1, source_target_pairs={{0,2},{2,4},{4,6},{1,3},{3,5},{5,7},{8,10},{10,12},{12,14},{9,11},... | collective-permute-start | bytes 522248 | tf_op jit(solution)/shard_map/ppermute | solution.py:307
  56.9 7.0 %collective-permute-start.25 = (bf16[136,640]{1,0:T(8,128)(2,1)}, bf16[136,640]{1,0:T(8,128)(2,1)S(1)}, u32[]{:S(2)}, u32[]{:S(2)}) collective-permute-start(bf16[136,640]{1,0:T(8,128)(2,1)} %broadcast_select_fusion), channel_id=1, source_target_pairs={{0,1},{1,0},{2,3},{3,2},{4,5},{5,4},{6,7},{7,6},{8,9},{9,8},{10,11... | collective-permute-start | bytes 522248 | tf_op jit(solution)/shard_map/ppermute | solution.py:47
  58.7 6.4 %collective-permute-start.24 = (bf16[128,640]{1,0:T(8,128)(2,1)S(1)}, bf16[128,640]{1,0:T(8,128)(2,1)S(1)}, u32[]{:S(2)}, u32[]{:S(2)}) collective-permute-start(bf16[128,640]{1,0:T(8,128)(2,1)S(1)} %get-tuple-element.42), channel_id=1, source_target_pairs={{0,2},{2,0},{4,6},{6,4},{1,3},{3,1},{5,7},{7,5},{8,10},{10,8},{12,... | collective-permute-start | bytes 491528 | tf_op jit(solution)/shard_map/ppermute | solution.py:51
  (6 other events, 41.3 us)
